TPU v7x, 256 devices: a whole 4x4x8 slice. The times are simulated.
256 devices in a mesh: grp: 8 (over z), nb: 32 (over x, y, core).
Axes of the slice: x: 4, y: 4, z: 8, core: 2. Of those that a mesh axis runs over, the one named last changes fastest.
Arguments:
- hidden: bfloat16 [512, 64, 4096], P('nb')
- query_weight: bfloat16 [4096, 2048], P(None, 'grp')
- keys: bfloat16 [96, 128, 2048], P('nb', None, 'grp')
- values: bfloat16 [96, 128, 2048], P('nb', None, 'grp'), may hold values from -6 to 6
- neighbour_ids: int32 [512, 2], P('nb'), may hold values from 0 to 95, as said below
- neighbour_counts: int32 [512], P('nb'), may hold values from 1 to 2
- d_context: bfloat16 [512, 64, 2048], P('nb', None, 'grp'), may hold values from -6 to 6
Outputs:
- context: bfloat16 [512, 64, 2048], P('nb', None, 'grp')
- d_hidden: bfloat16 [512, 64, 4096], P('nb', None, 'grp')
- d_keys: bfloat16 [96, 128, 2048], P('nb', None, 'grp')
- d_values: bfloat16 [96, 128, 2048], P('nb', None, 'grp')
- d_weight: bfloat16 [4096, 2048], P('nb', 'grp')
Inputs may be any that keep to these rules, and one draw needn't show every extreme that they name: `neighbour_ids`: block b belongs to index b // 3 of nb. The 32 references of the spans of one index of nb name the blocks of one index of nb at most 2 times; in every draw the blocks of some one index of nb are named exactly 2 times by the spans of every index of nb.
All inputs are finite; a program needn't handle non-finite values.
Results may differ from a plain program's by a relative error of at most 0.02.
The roundings to bfloat16 on the way count: a program that leaves them out, or rounds other values in their place, can miss the bound.
Values may be sent and summed in bfloat16 or wider, within the bound.
No kernel may reach another device: no remote copies, remote signals or barrier semaphores. Data moves between devices by JAX's collectives and lax.ppermute only.
A program may use at most 128 MiB of HBM per device.

v0:
```python
import math

import jax
import jax.numpy as jnp
from jax import lax
from jax.experimental import pallas as pl
from jax.experimental.pallas import tpu as pltpu
from jax.sharding import Mesh, PartitionSpec as P

DH = 128
SIDE = 4
CHIPS = SIDE * SIDE
NB = ("chip", "core")
F32 = jnp.float32
BF16 = jnp.bfloat16
VMEM_LIMIT = 40 * 2**20


def chip_pairs(move):
    pairs = []
    for x in range(SIDE):
        for y in range(SIDE):
            to_x, to_y = move(x, y)
            pairs.append((x * SIDE + y, to_x * SIDE + to_y))
    return pairs


LINKS = (
    chip_pairs(lambda x, y: (x ^ 1, y)),
    chip_pairs(lambda x, y: (x, y ^ 1)),
    chip_pairs(lambda x, y: (x ^ 3, y)),
    chip_pairs(lambda x, y: (x, y ^ 3)),
)


def cube_bits(chip):
    x, y = chip // SIDE, chip % SIDE
    return ((x ^ (x >> 1)) & 1, (y ^ (y >> 1)) & 1, x >> 1, y >> 1)


def cube_place(mine, chip, stream):
    here, there = cube_bits(mine), cube_bits(chip)
    across = [a ^ b for a, b in zip(here, there)]
    return sum(across[(stream + k) % 4] << k for k in range(4))


def swap(value):
    return lax.ppermute(value, "core", [(0, 1), (1, 0)])


def summed(parts, start, stop):
    total = 0.0
    for array, first in parts:
        total = total + array[first + start : first + stop].astype(F32)
    return total.astype(BF16)


def send(streams, k):
    came = [lax.ppermute(h, "chip", LINKS[(s + k) % 4]) for s, h in enumerate(streams)]
    return list(came)


def attention_body(
    slots, counts, q_own, q_sib, g_own, g_sib, k_in, v_in,
    ctx_own, gq_own, pair_sib, dk00, dk01, dk10, dk11, dv00, dv01, dv10, dv11,
    k_all, v_all, dk_all, dv_all, in_sem, out_sem,
):
    scale = 1.0 / math.sqrt(DH)
    block_len = k_all.shape[1]
    loads = [
        pltpu.make_async_copy(k_in, k_all, in_sem.at[0]),
        pltpu.make_async_copy(v_in, v_all, in_sem.at[1]),
    ]
    for copy in loads:
        copy.start()
    blank = jnp.zeros(dk_all.shape[1:], BF16)

    def clear(n, carry):
        dk_all[n] = blank
        dv_all[n] = blank
        return carry

    lax.fori_loop(0, dk_all.shape[0], clear, 0, unroll=4)
    for copy in loads:
        copy.wait()
    spans = q_own.shape[0]
    rows = (((1,), (1,)), ((), ()))
    cols = (((0,), (0,)), ((), ()))

    def step(i, carry):
        batch = [(q_own, g_own, i, i), (q_sib, g_sib, i, i + spans)]
        q = [qr[n] for qr, _, n, _ in batch]
        g = [gr[n] for _, gr, n, _ in batch]
        refs = [(2 * span, 2 * span + 1) for _, _, _, span in batch]
        k = [jnp.concatenate([k_all[slots[0, r]] for r in pair], axis=0) for pair in refs]
        v = [jnp.concatenate([v_all[slots[0, r]] for r in pair], axis=0) for pair in refs]
        s = [lax.dot_general(a, b, rows, preferred_element_type=F32) for a, b in zip(q, k)]
        ga = [lax.dot_general(a, b, rows, preferred_element_type=F32) for a, b in zip(g, v)]
        place = lax.broadcasted_iota(jnp.int32, s[0].shape, 1)
        s = [
            jnp.where(place < counts[span] * block_len, a, -jnp.inf)
            for a, (_, _, _, span) in zip(s, batch)
        ]
        w = [jnp.exp(a - jnp.max(a, axis=1, keepdims=True)) for a in s]
        att = [a / jnp.sum(a, axis=1, keepdims=True) for a in w]
        low = [a.astype(BF16) for a in att]
        gs = [
            (a * (b - jnp.sum(a * b, axis=1, keepdims=True))).astype(BF16)
            for a, b in zip(att, ga)
        ]
        ctx = [jnp.dot(a, b, preferred_element_type=F32).astype(BF16) for a, b in zip(low, v)]
        gq = [(jnp.dot(a, b, preferred_element_type=F32) * scale).astype(BF16) for a, b in zip(gs, k)]
        dk = [lax.dot_general(a, b, cols, preferred_element_type=F32).astype(BF16) for a, b in zip(gs, q)]
        dv = [lax.dot_general(a, b, cols, preferred_element_type=F32).astype(BF16) for a, b in zip(low, g)]
        ctx_own[i] = ctx[0]
        gq_own[i] = gq[0]
        pair_sib[0, i] = ctx[1]
        pair_sib[1, i] = gq[1]
        for n, pair in enumerate(refs):
            for j, r in enumerate(pair):
                at = slots[1, r]
                part = dk[n][j * block_len : (j + 1) * block_len].astype(F32)
                dk_all[at] = (dk_all[at].astype(F32) + part).astype(BF16)
                at = slots[2, r]
                part = dv[n][j * block_len : (j + 1) * block_len].astype(F32)
                dv_all[at] = (dv_all[at].astype(F32) + part).astype(BF16)
        return carry

    lax.fori_loop(0, spans, step, 0, unroll=2)
    half = dk00.shape[0]
    stores = []
    for n, ref in enumerate((dk00, dk01, dk10, dk11)):
        stores.append(pltpu.make_async_copy(dk_all.at[pl.ds(n * half, half)], ref, out_sem.at[n]))
    for n, ref in enumerate((dv00, dv01, dv10, dv11)):
        stores.append(pltpu.make_async_copy(dv_all.at[pl.ds(n * half, half)], ref, out_sem.at[4 + n]))
    for copy in stores:
        copy.start()
    for copy in stores:
        copy.wait()


def attention(slots, counts, q_own, q_sib, g_own, g_sib, k_in, v_in):
    spans, span_len, width = q_own.shape
    total, block_len, _ = k_in.shape
    small = jax.ShapeDtypeStruct((spans, span_len, width), BF16)
    pair = jax.ShapeDtypeStruct((2, spans, span_len, width), BF16)
    large = pltpu.HBM((total // 4, block_len, width), BF16)
    whole = pltpu.VMEM((total, block_len, width), BF16)
    in_smem = pl.BlockSpec(memory_space=pltpu.SMEM)
    in_vmem = pl.BlockSpec(memory_space=pltpu.VMEM)
    in_hbm = pl.BlockSpec(memory_space=pltpu.HBM)
    left = pl.BlockSpec(memory_space=pl.ANY)
    return pl.pallas_call(
        attention_body,
        out_shape=[small, small, pair] + [large] * 8,
        in_specs=[in_smem] * 2 + [in_vmem] * 4 + [left] * 2,
        out_specs=[in_vmem] * 3 + [in_hbm] * 8,
        scratch_shapes=[whole] * 4 + [pltpu.SemaphoreType.DMA((2,)), pltpu.SemaphoreType.DMA((8,))],
        compiler_params=pltpu.CompilerParams(vmem_limit_bytes=VMEM_LIMIT),
        name="attention",
    )(slots, counts, q_own, q_sib, g_own, g_sib, k_in, v_in)


def weight_body(places, gq_ref, hid_ref, own, sib, gq_t):
    step = pl.program_id(0)

    @pl.when(step == 0)
    def _():
        gq_t[...] = gq_ref[...].T

    term = jnp.dot(gq_t[...], hid_ref[...], preferred_element_type=F32).astype(BF16)
    streams, _, cut, part = own.shape
    core = places[streams, 0]
    per_step = hid_ref.shape[1] // part
    for t in range(per_step):
        chip = step * (per_step // 2) + t // 2
        pieces = [term[s * cut : (s + 1) * cut, t * part : (t + 1) * part] for s in range(streams)]

        @pl.when(core == t % 2)
        def _():
            for s in range(streams):
                own[s, places[s, chip]] = pieces[s]

        @pl.when(core != t % 2)
        def _():
            for s in range(streams):
                sib[s, places[s, chip]] = pieces[s]


def weight_terms(places, grad_rows, hidden_rows):
    rows, model_width = hidden_rows.shape
    head_cols = grad_rows.shape[1]
    part = model_width // (2 * CHIPS)
    wide = 4 * part
    shape = (4, CHIPS, head_cols // 4, part)
    return pl.pallas_call(
        weight_body,
        out_shape=[jax.ShapeDtypeStruct(shape, BF16)] * 2,
        grid_spec=pltpu.PrefetchScalarGridSpec(
            num_scalar_prefetch=1,
            grid=(model_width // wide,),
            in_specs=[
                pl.BlockSpec(grad_rows.shape, lambda i, p: (0, 0)),
                pl.BlockSpec((rows, wide), lambda i, p: (0, i)),
            ],
            out_specs=[pl.BlockSpec(shape, lambda i, p: (0, 0, 0, 0))] * 2,
            scratch_shapes=[pltpu.VMEM(grad_rows.shape[::-1], BF16)],
        ),
        compiler_params=pltpu.CompilerParams(vmem_limit_bytes=VMEM_LIMIT),
        name="weight_terms",
    )(places, grad_rows, hidden_rows)


def hidden_body(gq_ref, w_ref, out):
    total = None
    for g in range(gq_ref.shape[0]):
        term = lax.dot_general(
            gq_ref[g], w_ref[g], (((1,), (1,)), ((), ())), preferred_element_type=F32
        )
        term = term.astype(BF16).astype(F32)
        total = term if total is None else total + term
    out[...] = total.astype(BF16)


def hidden_grads(every_grad, weight_rows):
    groups, rows, head_cols = every_grad.shape
    wide = weight_rows.shape[1]
    chunk = rows // 4
    return pl.pallas_call(
        hidden_body,
        out_shape=jax.ShapeDtypeStruct((rows, wide), BF16),
        grid=(rows // chunk,),
        in_specs=[
            pl.BlockSpec((groups, chunk, head_cols), lambda i: (0, i, 0)),
            pl.BlockSpec(weight_rows.shape, lambda i: (0, 0, 0)),
        ],
        out_specs=pl.BlockSpec((chunk, wide), lambda i: (i, 0)),
        compiler_params=pltpu.CompilerParams(vmem_limit_bytes=VMEM_LIMIT),
        name="hidden_grads",
    )(every_grad, weight_rows)


def per_device(hidden, query_weight, keys, values, neighbour_ids, neighbour_counts, d_context):
    spans, span_len, model_width = hidden.shape
    blocks, block_len, head_cols = keys.shape
    groups = lax.axis_size("grp")
    scale = 1.0 / math.sqrt(DH)
    chip = lax.axis_index("chip")
    core = lax.axis_index("core")
    rows = spans * span_len
    refs = neighbour_ids.size

    def both(array):
        first, second = array[..., :DH], array[..., DH:]
        return jnp.where(core == 0, first, second), jnp.where(core == 0, second, first)

    def joined(own, other):
        return jnp.where(
            core == 0,
            jnp.concatenate([own, other], axis=-1),
            jnp.concatenate([other, own], axis=-1),
        )

    with jax.named_scope("gather"):
        own, other = both(jnp.stack([keys, values]))
        came = swap(other)
        every_key = lax.all_gather(jnp.concatenate([own[0], came[0]]), "chip", axis=0, tiled=True)
        every_value = lax.all_gather(jnp.concatenate([own[1], came[1]]), "chip", axis=0, tiled=True)
    with jax.named_scope("weight_rows"):
        wide = model_width // groups
        weight_rows = lax.all_to_all(query_weight, "grp", split_axis=0, concat_axis=0, tiled=True)
        weight_rows = weight_rows.reshape(groups, wide, head_cols)
    with jax.named_scope("queries"):
        hidden_rows = hidden.reshape(rows, model_width)
        projected = jnp.dot(hidden_rows, query_weight, preferred_element_type=F32) * scale
        queries = projected.astype(BF16).reshape(spans, span_len, head_cols)
        query_own, query_other = both(queries)
        grad_own, grad_other = both(d_context)
        came = swap(jnp.stack([query_other, grad_other]))
        query_sib, grad_sib = came[0], came[1]
    with jax.named_scope("slots"):
        table = jnp.concatenate([neighbour_ids.reshape(-1), neighbour_counts])
        table_sib = swap(table)
        ids = jnp.concatenate([table[:refs], table_sib[:refs]])
        counts = jnp.concatenate([table[refs:], table_sib[refs:]])
        owner, local = ids // blocks, ids % blocks
        far = jnp.where(owner % 2 == core, 0, 1)
        host = owner // 2

        def slot(near_stream, far_stream):
            near_place = cube_place(chip, host, near_stream)
            far_place = CHIPS + cube_place(chip, host, far_stream)
            return jnp.where(far == 0, near_place, far_place) * blocks + local

        slots = jnp.stack([(host * 2 + far) * blocks + local, slot(0, 1), slot(2, 3)])
        every = jnp.arange(CHIPS, dtype=jnp.int32)
        places = jnp.stack(
            [cube_place(chip, every, s) for s in range(4)] + [jnp.broadcast_to(core, (CHIPS,))]
        )
    with jax.named_scope("attend"):
        out = attention(
            slots, counts, query_own, query_sib, grad_own, grad_sib, every_key, every_value
        )
        ctx_own, gq_own, pair_sib = out[:3]
        low = [g.reshape(-1, DH) for g in out[3::2]]
        high = [g.reshape(-1, DH) for g in out[4::2]]
    with jax.named_scope("grad_queries"):
        pair = swap(pair_sib)
        context = joined(ctx_own, pair[0])
        grad_rows = joined(gq_own, pair[1]).reshape(rows, head_cols)
        every_grad = lax.all_gather(grad_rows, "grp", axis=0, tiled=False)
    with jax.named_scope("return"):
        came = send(high, 3)
        terms, terms_sib = weight_terms(places, grad_rows, hidden_rows)
        cut = terms.shape[2]
        terms = terms.reshape(4, -1, DH)
        others = swap(terms_sib).reshape(4, -1, DH)
        span = terms.shape[1] // 2
        kv = [[(a, 0), (b, 0)] for a, b in zip(low, came)]
        dw = [[(terms[s], 0), (others[s], 0)] for s in range(4)]
        came_w = send([summed(p, span, 2 * span) for p in dw], 3)
        for s in range(4):
            dw[s].append((came_w[s], 0))
        size = low[0].shape[0]
        for k in (2, 1, 0):
            size //= 2
            span //= 2
            packed = [
                jnp.concatenate([summed(a, size, 2 * size), summed(b, span, 2 * span)])
                for a, b in zip(kv, dw)
            ]
            packed = lax.optimization_barrier(packed)
            came = send(packed, k)
            came = lax.optimization_barrier(came)
            for s in range(4):
                kv[s].append((came[s], 0))
                dw[s].append((came[s], size))
        kv = [summed(p, 0, size) for p in kv]
        dw = [summed(p, 0, span) for p in dw]
        other = swap(jnp.concatenate([kv[1], kv[3]]))
        d_keys = joined(kv[0], other[:size]).reshape(blocks, block_len, head_cols)
        d_values = joined(kv[2], other[size:]).reshape(blocks, block_len, head_cols)
        d_weight = jnp.concatenate(dw).T
    with jax.named_scope("d_hidden"):
        d_hidden = hidden_grads(every_grad, weight_rows).reshape(spans, span_len, wide)
    return context, d_hidden, d_keys, d_values, d_weight


def solution(mesh):
    fine = Mesh(mesh.devices.reshape(mesh.devices.shape[0], CHIPS, 2), ("grp", "chip", "core"))
    placed = (
        P(NB, None, None),
        P(None, "grp"),
        P(NB, None, "grp"),
        P(NB, None, "grp"),
        P(NB, None),
        P(NB),
        P(NB, None, "grp"),
    )
    return jax.shard_map(
        per_device,
        mesh=fine,
        in_specs=placed,
        out_specs=(
            P(NB, None, "grp"),
            P(NB, None, "grp"),
            P(NB, None, "grp"),
            P(NB, None, "grp"),
            P(NB, "grp"),
        ),
        check_vma=False,
    )
```

profile of v0, /device:TPU:8, one launch (start us, length us, event | category | flops | bytes accessed | tf_op | source)
XLA Modules:
  0.0 252.6 jit_solution(11543603223698530000)
XLA Ops:
  13.2 6.4 %fusion = bf16[1024,256]{1,0:T(8,128)(2,1)S(1)} fusion(bf16[1024,4096]{1,0:T(8,128)(2,1)} %bitcast.206, bf16[4096,256]{1,0:T(8,128)(2,1)} %param.8), kind=kOutput, calls=%fused_computation.1 | convolution fusion | flops 2148007936 | bytes 11010048 | tf_op jit(solution)/shard_map/queries/dot_general | solution.py:275
  20.2 8.5 %all-to-all-start = ((bf16[8,512,256]{2,1,0:T(8,128)(2,1)}), bf16[8,512,256]{2,1,0:T(8,128)(2,1)S(1)}, u32[]{:S(2)}, u32[]{:S(2)}) async-start(bf16[8,512,256]{2,1,0:T(8,128)(2,1)} %bitcast.212), calls=%async_computation | async-start | bytes 4194304 | tf_op jit(solution)/shard_map/weight_rows/all_to_all | solution.py:271
  30.3 35.9 %all-gather.4.cloned.1.call-done.k_in = bf16[96,128,128]{2,1,0:T(8,128)(2,1)} async-done(((bf16[6,128,128]{2,1,0:T(8,128)(2,1)}), bf16[96,128,128]{2,1,0:T(8,128)(2,1)}) %all-gather.4.cloned.1.call-update) | async-done | bytes 3145744 | tf_op jit(solution)/shard_map/gather/all_gather | solution.py:267
  66.2 55.0 %all-gather.6.cloned.1.call-done.v_in = bf16[96,128,128]{2,1,0:T(8,128)(2,1)} async-done(((bf16[6,128,128]{2,1,0:T(8,128)(2,1)}), bf16[96,128,128]{2,1,0:T(8,128)(2,1)}) %all-gather.6.cloned.1.call-update) | async-done | bytes 3145744 | tf_op jit(solution)/shard_map/gather/all_gather | solution.py:268
  121.2 1.9 copy-done.2
  123.1 1.9 copy-done.3
  125.0 15.2 %attention.1 = (bf16[16,64,128]{2,1,0:T(8,128)(2,1)S(1)}, bf16[16,64,128]{2,1,0:T(8,128)(2,1)S(1)}, bf16[2,16,64,128]{3,2,1,0:T(8,128)(2,1)}, bf16[24,128,128]{2...) custom-call(s32[3,64]{1,0:T(4,128)S(1)} %pad_add_fusion.slots, ...), custom_call_target="tpu_custom_call" | custom-call | tf_op jit(solution)/shard_map/attend/attention/pallas_call | solution.py:153
  144.1 1.8 slice.613
  147.4 1.8 slice.606
  150.8 1.8 slice.599
  155.7 1.8 collective-permute-start.9
  158.4 1.6 fusion.94
  160.0 1.8 fusion.98
  162.0 3.4 %copy-done = bf16[16,64,4096]{2,1,0:T(8,128)(2,1)S(1)} copy-done((bf16[16,64,4096]{2,1,0:T(8,128)(2,1)S(1)}, bf16[16,64,4096]{2,1,0:T(8,128)(2,1)}, u32[]{:S(2)}) %copy-start) | copy-done | bytes 8388632
  165.4 6.4 %weight_terms.1 = (bf16[4,16,64,128]{3,2,1,0:T(8,128)(2,1)S(1)}, bf16[4,16,64,128]{3,2,1,0:T(8,128)(2,1)}) custom-call(s32[5,16]{1,0:T(8,128)S(1)} %stack.38.places, bf16[1024,256]{1,0:T(8,128)(2,1)S(1)} %maximum_select_fusion.2.gq_ref, bf16[1024,4096]{1,0:T(8,128)(2,1)S(1)} %bitcast.207), custom_call_target="tpu_custom_call" | custom-call | tf_op jit(solution)/shard_map/return/weight_terms/pallas_call | solution.py:196
  174.0 1.7 collective-permute-done.9
  189.2 1.8 collective-permute-start.13
  193.0 2.6 %collective-permute-start.16 = (bf16[1792,128]{1,0:T(8,128)(2,1)S(1)}, bf16[1792,128]{1,0:T(8,128)(2,1)S(1)}, u32[]{:S(2)}, u32[]{:S(2)}) collective-permute-start(bf16[1792,128]{1,0:T(8,128)(2,1)S(1)} %pad_maximum_fusion.4), channel_id=1, source_target_pairs={{0,2},{2,0},{4,6},{6,4},{8,10},{10,8},{12,14},{14,12},{16,18},{18,... | collective-permute-start | bytes 1376264 | tf_op jit(solution)/shard_map/return/ppermute | solution.py:59
  197.5 3.4 %collective-permute-done.13 = bf16[1792,128]{1,0:T(8,128)(2,1)S(1)} collective-permute-done((bf16[1792,128]{1,0:T(8,128)(2,1)S(1)}, bf16[1792,128]{1,0:T(8,128)(2,1)S(1)}, u32[]{:S(2)}, u32[]{:S(2)}) %collective-permute-start.13) | collective-permute-done | bytes 458784 | tf_op jit(solution)/shard_map/return/ppermute | solution.py:59
  207.4 1.8 collective-permute-start.17
  214.2 2.3 collective-permute-done.18
  229.1 2.1 collective-permute-done.23
  239.8 2.2 copy-done.1
  242.0 4.0 %hidden_grads.1 = bf16[1024,512]{1,0:T(8,128)(2,1)} custom-call(bf16[8,1024,256]{2,1,0:T(8,128)(2,1)S(1)} %copy-done.1, bf16[8,512,256]{2,1,0:T(8,128)(2,1)S(1)} %all-to-all-done.w_ref), custom_call_target="tpu_custom_call" | custom-call | tf_op jit(solution)/shard_map/d_hidden/hidden_grads/pallas_call | solution.py:229
  (188 shorter events, 71.2 us)
Async XLA Ops:
  7.2 59.0 %all-gather.4.cloned.1.call-start = ((), (), s32[]{:S(2)}) async-start(), calls=%async_computation.1 | async-start | bytes 3342336 | tf_op jit(solution)/shard_map/gather/all_gather | solution.py:267
  10.7 110.5 %all-gather.6.cloned.1.call-start = ((), (), s32[]{:S(2)}) async-start(), calls=%async_computation.2 | async-start | bytes 3342336 | tf_op jit(solution)/shard_map/gather/all_gather | solution.py:268
  13.1 15.8 %collective-permute-start = (s32[48]{0:T(128)S(1)}, s32[48]{0:T(128)S(1)}, u32[]{:S(2)}, u32[]{:S(2)}) collective-permute-start(s32[48]{0:T(128)S(1)} %pad_add_fusion.1), channel_id=1, source_target_pairs={{0,1},{1,0},{2,3},{3,2},{4,5},{5,4},{6,7},{7,6},{8,9},{9,8},{10,11... | collective-permute-start | bytes 584 | tf_op jit(solution)/shard_map/slots/ppermute | solution.py:48
  19.8 9.5 %collective-permute-start.1 = (bf16[2,16,64,128]{3,2,1,0:T(8,128)(2,1)S(1)}, bf16[2,16,64,128]{3,2,1,0:T(8,128)(2,1)}, u32[]{:S(2)}, u32[]{:S(2)}) collective-permute-start(bf16[2,16,64,128]{3,2,1,0:T(8,128)(2,1)S(1)} %pad_maximum_fusion), channel_id=1, source_target_pairs={{0,1},{1,0},{2,3},{3,2},{4,5},{5,4},{6,7},{7,6},{8,9},{9,8},{10,11... | collective-permute-start | bytes 1572872 | tf_op jit(solution)/shard_map/queries/ppermute | solution.py:48
  20.2 219.6 %all-to-all-start = ((bf16[8,512,256]{2,1,0:T(8,128)(2,1)}), bf16[8,512,256]{2,1,0:T(8,128)(2,1)S(1)}, u32[]{:S(2)}, u32[]{:S(2)}) async-start(bf16[8,512,256]{2,1,0:T(8,128)(2,1)} %bitcast.212), calls=%async_computation | async-start | bytes 4194304 | tf_op jit(solution)/shard_map/weight_rows/all_to_all | solution.py:271
  28.7 211.2 %all-gather.8.cloned.1.call-start = ((), (), s32[]{:S(2)}) async-start(), calls=%async_computation.3 | async-start | bytes 4718592 | tf_op jit(solution)/shard_map/grad_queries/all_gather | solution.py:311
  140.9 19.1 %collective-permute-start.3 = (bf16[2,16,64,128]{3,2,1,0:T(8,128)(2,1)}, bf16[2,16,64,128]{3,2,1,0:T(8,128)(2,1)}, u32[]{:S(2)}, u32[]{:S(2)}) collective-permute-start(bf16[2,16,64,128]{3,2,1,0:T(8,128)(2,1)} %get-tuple-element.43), channel_id=1, source_target_pairs={{0,1},{1,0},{2,3},{3,2},{4,5},{5,4},{6,7},{7,6},{8,9},{9,8},{10,11... | collective-permute-start | bytes 1572872 | tf_op jit(solution)/shard_map/grad_queries/ppermute | solution.py:48
  140.9 31.9 %collective-permute-start.11 = (bf16[3072,128]{1,0:T(8,128)(2,1)}, bf16[3072,128]{1,0:T(8,128)(2,1)}, u32[]{:S(2)}, u32[]{:S(2)}) collective-permute-start(bf16[3072,128]{1,0:T(8,128)(2,1)} %bitcast.225), channel_id=1, source_target_pairs={{0,24},{2,26},{4,28},{6,30},{8,16},{10,18},{12,20},{14,22},{16,8},... | collective-permute-start | bytes 2359304 | tf_op jit(solution)/shard_map/return/ppermute | solution.py:59
  155.7 20.1 %collective-permute-start.9 = (bf16[3072,128]{1,0:T(8,128)(2,1)}, bf16[3072,128]{1,0:T(8,128)(2,1)}, u32[]{:S(2)}, u32[]{:S(2)}) collective-permute-start(bf16[3072,128]{1,0:T(8,128)(2,1)} %bitcast.30), channel_id=1, source_target_pairs={{0,2},{2,0},{4,6},{6,4},{8,10},{10,8},{12,14},{14,12},{16,18},{18,... | collective-permute-start | bytes 2359304 | tf_op jit(solution)/shard_map/return/ppermute | solution.py:59
  157.5 19.7 %collective-permute-start.7 = (bf16[3072,128]{1,0:T(8,128)(2,1)}, bf16[3072,128]{1,0:T(8,128)(2,1)}, u32[]{:S(2)}, u32[]{:S(2)}) collective-permute-start(bf16[3072,128]{1,0:T(8,128)(2,1)} %bitcast.26), channel_id=1, source_target_pairs={{0,8},{2,10},{4,12},{6,14},{8,0},{10,2},{12,4},{14,6},{16,24},{18,... | collective-permute-start | bytes 2359304 | tf_op jit(solution)/shard_map/return/ppermute | solution.py:59
  157.5 20.9 %collective-permute-start.4 = (bf16[3072,128]{1,0:T(8,128)(2,1)}, bf16[3072,128]{1,0:T(8,128)(2,1)}, u32[]{:S(2)}, u32[]{:S(2)}) collective-permute-start(bf16[3072,128]{1,0:T(8,128)(2,1)} %bitcast.19), channel_id=1, source_target_pairs={{0,6},{2,4},{4,2},{6,0},{8,14},{10,12},{12,10},{14,8},{16,22},{18,... | collective-permute-start | bytes 2359304 | tf_op jit(solution)/shard_map/return/ppermute | solution.py:59
  171.8 7.9 %collective-permute-start.5 = (bf16[4,16,64,128]{3,2,1,0:T(8,128)(2,1)}, bf16[4,16,64,128]{3,2,1,0:T(8,128)(2,1)}, u32[]{:S(2)}, u32[]{:S(2)}) collective-permute-start(bf16[4,16,64,128]{3,2,1,0:T(8,128)(2,1)} %get-tuple-element.48), channel_id=1, source_target_pairs={{0,1},{1,0},{2,3},{3,2},{4,5},{5,4},{6,7},{7,6},{8,9},{9,8},{10,11... | collective-permute-start | bytes 3145736 | tf_op jit(solution)/shard_map/return/ppermute | solution.py:48
  180.9 6.3 %collective-permute-start.12 = (bf16[512,128]{1,0:T(8,128)(2,1)S(1)}, bf16[512,128]{1,0:T(8,128)(2,1)S(1)}, u32[]{:S(2)}, u32[]{:S(2)}) collective-permute-start(bf16[512,128]{1,0:T(8,128)(2,1)S(1)} %bitcast.224), channel_id=1, source_target_pairs={{0,24},{2,26},{4,28},{6,30},{8,16},{10,18},{12,20},{14,22},{16,8},... | collective-permute-start | bytes 393224 | tf_op jit(solution)/shard_map/return/ppermute | solution.py:59
  183.8 5.0 %collective-permute-start.8 = (bf16[512,128]{1,0:T(8,128)(2,1)S(1)}, bf16[512,128]{1,0:T(8,128)(2,1)S(1)}, u32[]{:S(2)}, u32[]{:S(2)}) collective-permute-start(bf16[512,128]{1,0:T(8,128)(2,1)S(1)} %bitcast.222), channel_id=1, source_target_pairs={{0,8},{2,10},{4,12},{6,14},{8,0},{10,2},{12,4},{14,6},{16,24},{18,... | collective-permute-start | bytes 393224 | tf_op jit(solution)/shard_map/return/ppermute | solution.py:59
  189.2 11.7 %collective-permute-start.13 = (bf16[1792,128]{1,0:T(8,128)(2,1)S(1)}, bf16[1792,128]{1,0:T(8,128)(2,1)S(1)}, u32[]{:S(2)}, u32[]{:S(2)}) collective-permute-start(bf16[1792,128]{1,0:T(8,128)(2,1)S(1)} %pad_maximum_fusion.1), channel_id=1, source_target_pairs={{0,24},{2,26},{4,28},{6,30},{8,16},{10,18},{12,20},{14,22},{16,8},... | collective-permute-start | bytes 1376264 | tf_op jit(solution)/shard_map/return/ppermute | solution.py:59
  191.0 10.1 %collective-permute-start.14 = (bf16[1792,128]{1,0:T(8,128)(2,1)S(1)}, bf16[1792,128]{1,0:T(8,128)(2,1)S(1)}, u32[]{:S(2)}, u32[]{:S(2)}) collective-permute-start(bf16[1792,128]{1,0:T(8,128)(2,1)S(1)} %pad_maximum_fusion.2), channel_id=1, source_target_pairs={{0,6},{2,4},{4,2},{6,0},{8,14},{10,12},{12,10},{14,8},{16,22},{18,... | collective-permute-start | bytes 1376264 | tf_op jit(solution)/shard_map/return/ppermute | solution.py:59
  192.0 9.5 %collective-permute-start.15 = (bf16[1792,128]{1,0:T(8,128)(2,1)S(1)}, bf16[1792,128]{1,0:T(8,128)(2,1)S(1)}, u32[]{:S(2)}, u32[]{:S(2)}) collective-permute-start(bf16[1792,128]{1,0:T(8,128)(2,1)S(1)} %pad_maximum_fusion.3), channel_id=1, source_target_pairs={{0,8},{2,10},{4,12},{6,14},{8,0},{10,2},{12,4},{14,6},{16,24},{18,... | collective-permute-start | bytes 1376264 | tf_op jit(solution)/shard_map/return/ppermute | solution.py:59
  193.0 9.9 %collective-permute-start.16 = (bf16[1792,128]{1,0:T(8,128)(2,1)S(1)}, bf16[1792,128]{1,0:T(8,128)(2,1)S(1)}, u32[]{:S(2)}, u32[]{:S(2)}) collective-permute-start(bf16[1792,128]{1,0:T(8,128)(2,1)S(1)} %pad_maximum_fusion.4), channel_id=1, source_target_pairs={{0,2},{2,0},{4,6},{6,4},{8,10},{10,8},{12,14},{14,12},{16,18},{18,... | collective-permute-start | bytes 1376264 | tf_op jit(solution)/shard_map/return/ppermute | solution.py:59
  207.4 6.8 %collective-permute-start.17 = (bf16[896,128]{1,0:T(8,128)(2,1)S(1)}, bf16[896,128]{1,0:T(8,128)(2,1)S(1)}, u32[]{:S(2)}, u32[]{:S(2)}) collective-permute-start(bf16[896,128]{1,0:T(8,128)(2,1)S(1)} %pad_maximum_fusion.5), channel_id=1, source_target_pairs={{0,2},{2,0},{4,6},{6,4},{8,10},{10,8},{12,14},{14,12},{16,18},{18,... | collective-permute-start | bytes 688136 | tf_op jit(solution)/shard_map/return/ppermute | solution.py:59
  209.3 7.2 %collective-permute-start.18 = (bf16[896,128]{1,0:T(8,128)(2,1)S(1)}, bf16[896,128]{1,0:T(8,128)(2,1)S(1)}, u32[]{:S(2)}, u32[]{:S(2)}) collective-permute-start(bf16[896,128]{1,0:T(8,128)(2,1)S(1)} %pad_maximum_fusion.6), channel_id=1, source_target_pairs={{0,24},{2,26},{4,28},{6,30},{8,16},{10,18},{12,20},{14,22},{16,8},... | collective-permute-start | bytes 688136 | tf_op jit(solution)/shard_map/return/ppermute | solution.py:59
  210.9 6.0 %collective-permute-start.19 = (bf16[896,128]{1,0:T(8,128)(2,1)S(1)}, bf16[896,128]{1,0:T(8,128)(2,1)S(1)}, u32[]{:S(2)}, u32[]{:S(2)}) collective-permute-start(bf16[896,128]{1,0:T(8,128)(2,1)S(1)} %pad_maximum_fusion.7), channel_id=1, source_target_pairs={{0,6},{2,4},{4,2},{6,0},{8,14},{10,12},{12,10},{14,8},{16,22},{18,... | collective-permute-start | bytes 688136 | tf_op jit(solution)/shard_map/return/ppermute | solution.py:59
  211.8 6.0 %collective-permute-start.20 = (bf16[896,128]{1,0:T(8,128)(2,1)S(1)}, bf16[896,128]{1,0:T(8,128)(2,1)S(1)}, u32[]{:S(2)}, u32[]{:S(2)}) collective-permute-start(bf16[896,128]{1,0:T(8,128)(2,1)S(1)} %pad_maximum_fusion.8), channel_id=1, source_target_pairs={{0,8},{2,10},{4,12},{6,14},{8,0},{10,2},{12,4},{14,6},{16,24},{18,... | collective-permute-start | bytes 688136 | tf_op jit(solution)/shard_map/return/ppermute | solution.py:59
  223.4 5.4 %collective-permute-start.21 = (bf16[448,128]{1,0:T(8,128)(2,1)S(1)}, bf16[448,128]{1,0:T(8,128)(2,1)S(1)}, u32[]{:S(2)}, u32[]{:S(2)}) collective-permute-start(bf16[448,128]{1,0:T(8,128)(2,1)S(1)} %pad_maximum_fusion.13), channel_id=1, source_target_pairs={{0,8},{2,10},{4,12},{6,14},{8,0},{10,2},{12,4},{14,6},{16,24},{18,... | collective-permute-start | bytes 344072 | tf_op jit(solution)/shard_map/return/ppermute | solution.py:59
  225.2 6.0 %collective-permute-start.23 = (bf16[448,128]{1,0:T(8,128)(2,1)S(1)}, bf16[448,128]{1,0:T(8,128)(2,1)S(1)}, u32[]{:S(2)}, u32[]{:S(2)}) collective-permute-start(bf16[448,128]{1,0:T(8,128)(2,1)S(1)} %pad_maximum_fusion.15), channel_id=1, source_target_pairs={{0,24},{2,26},{4,28},{6,30},{8,16},{10,18},{12,20},{14,22},{16,8},... | collective-permute-start | bytes 344072 | tf_op jit(solution)/shard_map/return/ppermute | solution.py:59
  (35 other events, 427.6 us)
Sparse Core Ops, SparseCore 0:
  11.1 55.0 all-gather.3
  69.2 51.9 all-gather.5
  172.9 55.6 all-gather.7
where the time goes:
time: 258 us; the launch traced here: 253 us
  waiting for transfers between devices  108 us (42%)
  starting transfers between devices  34 us (13%)
  local copies, waits for them, and re-layouts  32.2 us (12%)
  other arithmetic  31.6 us (12%)
  Pallas kernels  25.6 us (10%)
  between operations  14.4 us (6%)
  matrix products  6.37 us (2%)
    all_gather x1, waiting for transfers between devices, per_device(): lax.all_gather(jnp.concatenate([own[1], came[1]]), 'chip', axis=0, tiled=...  55 us
    all_gather x1, waiting for transfers between devices, per_device(): lax.all_gather(jnp.concatenate([own[0], came[0]]), 'chip', axis=0, tiled=...  35.9 us
    ppermute x20, starting transfers between devices, send(): lax.ppermute(h, 'chip', LINKS[(s + k) % 4])  24.6 us
    convert_element_type x29, other arithmetic, summed(): return total.astype(BF16)  22 us
    slice x12, local copies, waits for them, and re-layouts, summed(): total = total + array[first + start:first + stop].astype(F32)  17.4 us
    ppermute x20, waiting for transfers between devices, send(): lax.ppermute(h, 'chip', LINKS[(s + k) % 4])  16.1 us
    pallas_call x1, Pallas kernels, attention(): pl.pallas_call(attention_body, out_shape=[small, small, pair] + [large] *...  15.2 us
    unnamed x60, local copies, waits for them, and re-layouts  11.6 us
  transfers between devices with their start and end apart: 30, of which 19 were waited for; matrix products, arithmetic and copies ran while one was open for 23% of the time, Pallas kernels for 9%

commit v1 on v0

v1 whole, which is shorter than its diff:
```python
import math

import jax
import jax.numpy as jnp
from jax import lax
from jax.experimental import pallas as pl
from jax.experimental.pallas import tpu as pltpu
from jax.sharding import Mesh, PartitionSpec as P

DH = 128
SIDE = 4
CHIPS = SIDE * SIDE
NB = ("chip", "core")
F32 = jnp.float32
BF16 = jnp.bfloat16
MIB = 2**20


def chip_pairs(move):
    pairs = []
    for x in range(SIDE):
        for y in range(SIDE):
            to_x, to_y = move(x, y)
            pairs.append((x * SIDE + y, to_x * SIDE + to_y))
    return pairs


LINKS = (
    chip_pairs(lambda x, y: (x ^ 1, y)),
    chip_pairs(lambda x, y: (x, y ^ 1)),
    chip_pairs(lambda x, y: (x ^ 3, y)),
    chip_pairs(lambda x, y: (x, y ^ 3)),
)


def cube_bits(chip):
    x, y = chip // SIDE, chip % SIDE
    return ((x ^ (x >> 1)) & 1, (y ^ (y >> 1)) & 1, x >> 1, y >> 1)


ORDERS = ((0, 1, 3, 2), (0, 1, 2, 3), (2, 3, 1, 0), (2, 3, 0, 1))


GATHER_ORDERS = ((0, 1, 2, 3), (1, 2, 3, 0), (2, 3, 0, 1), (3, 0, 1, 2))


def cube_place(mine, chip, order):
    here, there = cube_bits(mine), cube_bits(chip)
    across = [a ^ b for a, b in zip(here, there)]
    return sum(across[d] << k for k, d in enumerate(order))


def square_pairs(pair, bits):
    moves = [dict(LINKS[d]) for k, d in enumerate(ORDERS[2 * pair][:2]) if bits >> k & 1]
    pairs = []
    for start in range(CHIPS):
        to = start
        for move in moves:
            to = move[to]
        pairs.append((start, to))
    return pairs


def swap(value):
    return lax.ppermute(value, "core", [(0, 1), (1, 0)])


def send(streams, k):
    return [lax.ppermute(h, "chip", LINKS[ORDERS[s][k]]) for s, h in enumerate(streams)]


def in_hbm(array):
    return pltpu.with_memory_space_constraint(array, pltpu.HBM)


def add_up(block, *refs):
    total = refs[0][block].astype(F32)
    for ref in refs[1:]:
        total = total + ref[block].astype(F32)
    return total


def half_body(kept, came, out, held, sem, offset):
    size = held.shape[1]
    loads = [pltpu.make_async_copy(kept[s], held.at[s], sem.at[s]) for s in range(4)]
    for copy in loads:
        copy.start()
    for s in range(4):
        loads[s].wait()

        def step(i, carry):
            total = held[s, i].astype(F32) + came[s][offset + i].astype(F32)
            out[s][i] = total.astype(BF16)
            return carry

        lax.fori_loop(0, size, step, 0, unroll=4)


def in_vmem(body, name, out_shape, *operands):
    vmem = pl.BlockSpec(memory_space=pltpu.VMEM)
    return pl.pallas_call(
        body,
        out_shape=out_shape,
        in_specs=[vmem] * len(operands),
        out_specs=[vmem] * len(out_shape),
        compiler_params=pltpu.CompilerParams(vmem_limit_bytes=6 * MIB),
        name=name,
    )(*operands)


def combine_half(name, kept, came, offset):
    def body(*refs):
        half_body(refs[:4], refs[4:8], refs[8:12], *refs[12:], offset)

    vmem = pl.BlockSpec(memory_space=pltpu.VMEM)
    return pl.pallas_call(
        body,
        out_shape=[jax.ShapeDtypeStruct(kept[0].shape, BF16)] * 4,
        in_specs=[pl.BlockSpec(memory_space=pl.ANY)] * 4 + [vmem] * 4,
        out_specs=[vmem] * 4,
        scratch_shapes=[pltpu.VMEM((4, *kept[0].shape), BF16), pltpu.SemaphoreType.DMA((4,))],
        compiler_params=pltpu.CompilerParams(vmem_limit_bytes=6 * MIB),
        name=name,
    )(*[in_hbm(k) for k in kept], *came)


def square_body(*refs):
    cut = refs[0].shape[0] // 4
    mine = refs[14]

    def step(i, carry):
        for s in range(4):
            for m in range(3):
                total = add_up((m + 1) * cut + i, refs[s], refs[4 + s])
                refs[8 + s // 2 * 3 + m][s % 2, i] = total.astype(BF16)
            mine[s, i] = add_up(i, refs[s], refs[4 + s])
        return carry

    lax.fori_loop(0, cut, step, 0)


def combine_square(kept, came):
    size, block_len, width = kept[0].shape
    shape = jax.ShapeDtypeStruct((2, size // 4, block_len, width), BF16)
    mine = jax.ShapeDtypeStruct((4, size // 4, block_len, width), F32)
    return in_vmem(square_body, "combine_square", [shape] * 6 + [mine], *kept, *came)


def last_body(mine_in, *refs):
    came, (out_own, out_sib), (mine, held, sem) = refs[:6], refs[6:8], refs[8:]
    loads = [pltpu.make_async_copy(mine_in, mine, sem.at[6])]
    for n in range(6):
        loads.append(pltpu.make_async_copy(came[n], held.at[n], sem.at[n]))
    for copy in loads:
        copy.start()
    for copy in loads:
        copy.wait()

    def step(i, carry):
        for s in range(4):
            pair = s // 2
            total = mine[s, i]
            for n in range(3 * pair, 3 * pair + 3):
                total = total + held[n, s % 2, i].astype(F32)
            (out_sib if s % 2 else out_own)[pair, i] = total.astype(BF16)
        return carry

    lax.fori_loop(0, mine.shape[1], step, 0)


def combine_last(mine, square):
    part = (2, *mine.shape[1:])
    left = pl.BlockSpec(memory_space=pl.ANY)
    vmem = pl.BlockSpec(memory_space=pltpu.VMEM)
    return pl.pallas_call(
        last_body,
        out_shape=[jax.ShapeDtypeStruct(part, BF16)] * 2,
        in_specs=[left] * 7,
        out_specs=[vmem] * 2,
        scratch_shapes=[
            pltpu.VMEM(mine.shape, F32),
            pltpu.VMEM((6, *part), BF16),
            pltpu.SemaphoreType.DMA((7,)),
        ],
        compiler_params=pltpu.CompilerParams(vmem_limit_bytes=6 * MIB),
        name="combine_last",
    )(mine, *[in_hbm(a) for a in square])


def join_body(*refs):
    size = refs[0].shape[0]

    def step(i, carry):
        for s in range(4):
            refs[8 + s][i] = refs[s][i]
            refs[8 + s][size + i] = refs[4 + s][i]
        return carry

    lax.fori_loop(0, size, step, 0, unroll=2)


def join_halves(held, came):
    shape = jax.ShapeDtypeStruct((2 * held[0].shape[0], *held[0].shape[1:]), BF16)
    return in_vmem(join_body, "join_halves", [shape] * 4, *held, *came)


def project_body(core, hid_ref, w_ref, own, other):
    scale = 1.0 / math.sqrt(DH)
    both = jnp.dot(hid_ref[...], w_ref[...], preferred_element_type=F32) * scale
    first, second = both[:, :DH].astype(BF16), both[:, DH:].astype(BF16)

    @pl.when(core[0] == 0)
    def _():
        own[...] = first
        other[...] = second

    @pl.when(core[0] != 0)
    def _():
        own[...] = second
        other[...] = first


def project(core, hidden_rows, query_weight):
    rows, model_width = hidden_rows.shape
    chunk = rows // 8
    out_spec = pl.BlockSpec((chunk, DH), lambda i, p: (i, 0))
    return pl.pallas_call(
        project_body,
        out_shape=[jax.ShapeDtypeStruct((rows, DH), BF16)] * 2,
        grid_spec=pltpu.PrefetchScalarGridSpec(
            num_scalar_prefetch=1,
            grid=(rows // chunk,),
            in_specs=[
                pl.BlockSpec((chunk, model_width), lambda i, p: (i, 0)),
                pl.BlockSpec(query_weight.shape, lambda i, p: (0, 0)),
            ],
            out_specs=[out_spec] * 2,
        ),
        compiler_params=pltpu.CompilerParams(vmem_limit_bytes=12 * MIB),
        name="project",
    )(core, in_hbm(hidden_rows), query_weight)


def weight_sum_body(terms, out):
    total = terms[0].astype(F32)
    for n in range(1, terms.shape[0]):
        total = total + terms[n].astype(F32)
    out[...] = total.T.astype(BF16)


def weight_sum(terms):
    _, head_cols, part = terms.shape
    shape = jax.ShapeDtypeStruct((part, head_cols), BF16)
    return in_vmem(weight_sum_body, "weight_sum", [shape], terms)[0]


def attention_body(
    slots, counts, q_own, q_sib, g_own, g_sib, *refs
):
    kv_in, (ctx_own, gq_own, pair_sib), outs = refs[:8], refs[8:11], refs[11:23]
    kv_all, dk_all, dv_all, in_sem, out_sem = refs[23:]
    scale = 1.0 / math.sqrt(DH)
    block_len = kv_all.shape[1]
    half = dk_all.shape[0] // 4
    loads = []
    for n, ref in enumerate(kv_in):
        part = kv_all.at[pl.ds(n * half, half)]
        loads.append(pltpu.make_async_copy(ref, part, in_sem.at[n]))
    for copy in loads:
        copy.start()
    blank = jnp.zeros(dk_all.shape[1:], BF16)

    def clear(n, carry):
        dk_all[n] = blank
        dv_all[n] = blank
        return carry

    lax.fori_loop(0, dk_all.shape[0], clear, 0, unroll=4)
    for copy in loads:
        copy.wait()
    spans = q_own.shape[0]
    rows = (((1,), (1,)), ((), ()))
    cols = (((0,), (0,)), ((), ()))

    def step(i, carry):
        batch = [(q_own, g_own, i, i), (q_sib, g_sib, i, i + spans)]
        q = [qr[n] for qr, _, n, _ in batch]
        g = [gr[n] for _, gr, n, _ in batch]
        refs = [(2 * span, 2 * span + 1) for _, _, _, span in batch]
        k = [jnp.concatenate([kv_all[slots[0, r]] for r in pair], axis=0) for pair in refs]
        v = [jnp.concatenate([kv_all[slots[1, r]] for r in pair], axis=0) for pair in refs]
        s = [lax.dot_general(a, b, rows, preferred_element_type=F32) for a, b in zip(q, k)]
        ga = [lax.dot_general(a, b, rows, preferred_element_type=F32) for a, b in zip(g, v)]
        place = lax.broadcasted_iota(jnp.int32, s[0].shape, 1)
        s = [
            jnp.where(place < counts[span] * block_len, a, -jnp.inf)
            for a, (_, _, _, span) in zip(s, batch)
        ]
        w = [jnp.exp(a - jnp.max(a, axis=1, keepdims=True)) for a in s]
        att = [a / jnp.sum(a, axis=1, keepdims=True) for a in w]
        low = [a.astype(BF16) for a in att]
        gs = [
            (a * (b - jnp.sum(a * b, axis=1, keepdims=True))).astype(BF16)
            for a, b in zip(att, ga)
        ]
        ctx = [jnp.dot(a, b, preferred_element_type=F32).astype(BF16) for a, b in zip(low, v)]
        gq = [(jnp.dot(a, b, preferred_element_type=F32) * scale).astype(BF16) for a, b in zip(gs, k)]
        dk = [lax.dot_general(a, b, cols, preferred_element_type=F32).astype(BF16) for a, b in zip(gs, q)]
        dv = [lax.dot_general(a, b, cols, preferred_element_type=F32).astype(BF16) for a, b in zip(low, g)]
        ctx_own[i] = ctx[0]
        gq_own[i] = gq[0]
        pair_sib[0, i] = ctx[1]
        pair_sib[1, i] = gq[1]
        for n, pair in enumerate(refs):
            for j, r in enumerate(pair):
                at = slots[2, r]
                part = dk[n][j * block_len : (j + 1) * block_len].astype(F32)
                dk_all[at] = (dk_all[at].astype(F32) + part).astype(BF16)
                at = slots[3, r]
                part = dv[n][j * block_len : (j + 1) * block_len].astype(F32)
                dv_all[at] = (dv_all[at].astype(F32) + part).astype(BF16)
        return carry

    lax.fori_loop(0, spans, step, 0, unroll=2)
    stores = []
    for s in range(4):
        whole = dk_all if s < 2 else dv_all
        at = s % 2 * 2 * half
        for ref in outs[3 * s : 3 * s + 3]:
            size = ref.shape[0]
            stores.append(
                pltpu.make_async_copy(whole.at[pl.ds(at, size)], ref, out_sem.at[len(stores)])
            )
            at += size
    for copy in stores:
        copy.start()
    for copy in stores:
        copy.wait()


def attention(slots, counts, q_own, q_sib, g_own, g_sib, gathered):
    spans, span_len, width = q_own.shape
    half, block_len, _ = gathered[0].shape
    small = jax.ShapeDtypeStruct((spans, span_len, width), BF16)
    pair = jax.ShapeDtypeStruct((2, spans, span_len, width), BF16)
    pieces = [half // 2, half // 2, half] * 4
    large = [pltpu.HBM((n, block_len, width), BF16) for n in pieces]
    grads = pltpu.VMEM((4 * half, block_len, width), BF16)
    smem = pl.BlockSpec(memory_space=pltpu.SMEM)
    vmem = pl.BlockSpec(memory_space=pltpu.VMEM)
    hbm = pl.BlockSpec(memory_space=pltpu.HBM)
    left = pl.BlockSpec(memory_space=pl.ANY)
    return pl.pallas_call(
        attention_body,
        out_shape=[small, small, pair] + large,
        in_specs=[smem] * 2 + [vmem] * 4 + [left] * 8,
        out_specs=[vmem] * 3 + [hbm] * 12,
        scratch_shapes=[
            pltpu.VMEM((8 * half, block_len, width), BF16),
            grads,
            grads,
            pltpu.SemaphoreType.DMA((8,)),
            pltpu.SemaphoreType.DMA((12,)),
        ],
        compiler_params=pltpu.CompilerParams(vmem_limit_bytes=20 * MIB),
        name="attention",
    )(slots, counts, q_own, q_sib, g_own, g_sib, *gathered)


def weight_body(core, gq_ref, hid_ref, own, sib, gq_t):
    step = pl.program_id(0)

    @pl.when(step == 0)
    def _():
        gq_t[...] = gq_ref[...].T

    term = jnp.dot(gq_t[...], hid_ref[...], preferred_element_type=F32).astype(BF16)
    chips, _, part = own.shape
    for n in range(chips):
        even = term[:, 2 * n * part : (2 * n + 1) * part]
        odd = term[:, (2 * n + 1) * part : (2 * n + 2) * part]

        @pl.when(core[0] == 0)
        def _():
            own[n] = even
            sib[n] = odd

        @pl.when(core[0] != 0)
        def _():
            own[n] = odd
            sib[n] = even


def weight_terms(core, grad_rows, hidden_rows):
    rows, model_width = hidden_rows.shape
    head_cols = grad_rows.shape[1]
    part = model_width // (2 * CHIPS)
    chips = 2
    wide = 2 * chips * part
    out_spec = pl.BlockSpec((chips, head_cols, part), lambda i, p: (i, 0, 0))
    return pl.pallas_call(
        weight_body,
        out_shape=[jax.ShapeDtypeStruct((CHIPS, head_cols, part), BF16)] * 2,
        grid_spec=pltpu.PrefetchScalarGridSpec(
            num_scalar_prefetch=1,
            grid=(CHIPS // chips,),
            in_specs=[
                pl.BlockSpec(grad_rows.shape, lambda i, p: (0, 0)),
                pl.BlockSpec((rows, wide), lambda i, p: (0, i)),
            ],
            out_specs=[out_spec] * 2,
            scratch_shapes=[pltpu.VMEM(grad_rows.shape[::-1], BF16)],
        ),
        compiler_params=pltpu.CompilerParams(vmem_limit_bytes=12 * MIB),
        name="weight_terms",
    )(core, grad_rows, in_hbm(hidden_rows))


def hidden_body(core, gq_ref, mine, other, out):
    wide = mine.shape[1]
    for n, w_ref in enumerate((mine, other)):
        total = None
        for g in range(gq_ref.shape[0]):
            term = lax.dot_general(
                gq_ref[g], w_ref[g], (((1,), (1,)), ((), ())), preferred_element_type=F32
            )
            term = term.astype(BF16).astype(F32)
            total = term if total is None else total + term
        at = pl.multiple_of((core[0] if n == 0 else 1 - core[0]) * wide, wide)
        out[:, pl.ds(at, wide)] = total.astype(BF16)


def hidden_grads(core, every_grad, mine, other):
    groups, rows, head_cols = every_grad.shape
    wide = 2 * mine.shape[1]
    chunk = rows // 4
    return pl.pallas_call(
        hidden_body,
        out_shape=jax.ShapeDtypeStruct((rows, wide), BF16),
        grid_spec=pltpu.PrefetchScalarGridSpec(
            num_scalar_prefetch=1,
            grid=(rows // chunk,),
            in_specs=[
                pl.BlockSpec((groups, chunk, head_cols), lambda i, p: (0, i, 0)),
                pl.BlockSpec(mine.shape, lambda i, p: (0, 0, 0)),
                pl.BlockSpec(mine.shape, lambda i, p: (0, 0, 0)),
            ],
            out_specs=pl.BlockSpec((chunk, wide), lambda i, p: (i, 0)),
        ),
        compiler_params=pltpu.CompilerParams(vmem_limit_bytes=16 * MIB),
        name="hidden_grads",
    )(core, in_hbm(every_grad), mine, other)


def per_device(hidden, query_weight, keys, values, neighbour_ids, neighbour_counts, d_context):
    spans, span_len, model_width = hidden.shape
    blocks, block_len, head_cols = keys.shape
    groups = lax.axis_size("grp")
    chip = lax.axis_index("chip")
    core = lax.axis_index("core")
    core_at = core.reshape(1)
    rows = spans * span_len
    refs = neighbour_ids.size

    def both(array):
        first, second = array[..., :DH], array[..., DH:]
        return jnp.where(core == 0, first, second), jnp.where(core == 0, second, first)

    def joined(own, other):
        return jnp.where(
            core == 0,
            jnp.concatenate([own, other], axis=-1),
            jnp.concatenate([other, own], axis=-1),
        )

    with jax.named_scope("gather"):
        own, other = both(jnp.stack([keys, values]))
        came = swap(other)
        held = list(lax.optimization_barrier([own[0], came[0], own[1], came[1]]))
        def across(pieces, k):
            return [lax.ppermute(p, "chip", LINKS[GATHER_ORDERS[s][k]]) for s, p in enumerate(pieces)]

        for k in range(2):
            came = across(held, k)
            held = [jnp.concatenate([a, b]) for a, b in zip(held, came)]
        held = join_halves(held, across(held, 2))
        last = across(held, 3)
    with jax.named_scope("queries"):
        hidden_rows = hidden.reshape(rows, model_width)
        query_own, query_other = project(core_at, hidden_rows, query_weight)
        query_own, query_other, leaving = lax.optimization_barrier(
            (query_own, query_other, query_weight)
        )
        last, query_own, query_other = lax.optimization_barrier((last, query_own, query_other))
        gathered = [part for parts in zip(held, last) for part in parts]
        query_own = query_own.reshape(spans, span_len, DH)
        query_sib = swap(query_other.reshape(spans, span_len, DH))
    with jax.named_scope("weight_rows"):
        wide = model_width // groups
        asked = leaving.reshape(groups, 2, wide // 2, head_cols)
        asked = jnp.where(core == 0, asked[:, 0], asked[:, 1])
        weight_own = lax.all_to_all(asked, "grp", split_axis=0, concat_axis=0, tiled=True)
    with jax.named_scope("more"):
        grad_own, grad_other = both(d_context)
        grad_sib = swap(grad_other)
    with jax.named_scope("slots"):
        table = jnp.concatenate([neighbour_ids.reshape(-1), neighbour_counts])
        table_sib = swap(table)
        ids = jnp.concatenate([table[:refs], table_sib[:refs]])
        counts = jnp.concatenate([table[refs:], table_sib[refs:]])
        owner, local = ids // blocks, ids % blocks
        far = jnp.where(owner % 2 == core, 0, 1)
        host = owner // 2

        def slot(orders, first):
            near_place = cube_place(chip, host, orders[0])
            far_place = CHIPS + cube_place(chip, host, orders[1])
            return (first + jnp.where(far == 0, near_place, far_place)) * blocks + local

        slots = jnp.stack(
            [
                slot(GATHER_ORDERS[:2], 0),
                slot(GATHER_ORDERS[2:], 2 * CHIPS),
                slot(ORDERS[:2], 0),
                slot(ORDERS[2:], 0),
            ]
        )
    with jax.named_scope("attend"):
        out = attention(slots, counts, query_own, query_sib, grad_own, grad_sib, gathered)
        ctx_own, gq_own, pair_sib = out[:3]
        low, mid, high = out[3::3], out[4::3], out[5::3]
    with jax.named_scope("grad_queries"):
        pair = swap(pair_sib)
        grad_rows = joined(gq_own, pair[1]).reshape(rows, head_cols)
        grad_rows, high, weight_own = lax.optimization_barrier((grad_rows, high, weight_own))
        weight_other = swap(weight_own)
        every_grad = lax.all_gather(grad_rows, "grp", axis=0, tiled=False)
    with jax.named_scope("return"):
        first = send(high, 3)
        terms, terms_sib = weight_terms(core_at, grad_rows, hidden_rows)
        first, terms, terms_sib = lax.optimization_barrier((first, terms, terms_sib))
        halved = combine_half("combine_high", mid, first, mid[0].shape[0])
        halved, terms, terms_sib = lax.optimization_barrier((halved, terms, terms_sib))
        second = send(halved, 2)
        terms = (terms.astype(F32) + swap(terms_sib).astype(F32)).astype(BF16)
        stays = combine_half("combine_low", low, first, 0)
        second, stays, terms = lax.optimization_barrier((second, stays, terms))
        *square, mine = combine_square(stays, second)
        square = [
            lax.ppermute(square[3 * pair + m], "chip", square_pairs(pair, m + 1))
            for pair in range(2)
            for m in range(3)
        ]
        square, mine, terms = lax.optimization_barrier((square, mine, terms))
        terms = lax.all_to_all(terms, "chip", split_axis=0, concat_axis=0, tiled=True)
        d_hidden = hidden_grads(core_at, every_grad, weight_own, weight_other)
        sums, sums_sib = combine_last(mine, square)
        other = swap(sums_sib)
        other, d_hidden = lax.optimization_barrier((other, d_hidden))
        d_keys = joined(sums[0], other[0])
        d_values = joined(sums[1], other[1])
        d_weight = weight_sum(terms)
        d_hidden = d_hidden.reshape(spans, span_len, wide)
    with jax.named_scope("context"):
        context = joined(ctx_own, pair[0])
    return context, d_hidden, d_keys, d_values, d_weight


def solution(mesh):
    fine = Mesh(mesh.devices.reshape(mesh.devices.shape[0], CHIPS, 2), ("grp", "chip", "core"))
    placed = (
        P(NB, None, None),
        P(None, "grp"),
        P(NB, None, "grp"),
        P(NB, None, "grp"),
        P(NB, None),
        P(NB),
        P(NB, None, "grp"),
    )
    return jax.shard_map(
        per_device,
        mesh=fine,
        in_specs=placed,
        out_specs=(
            P(NB, None, "grp"),
            P(NB, None, "grp"),
            P(NB, None, "grp"),
            P(NB, None, "grp"),
            P(NB, "grp"),
        ),
        check_vma=False,
    )
```

time: 258 us -> 184 us (0.71); the launches traced: 253 us -> 182 us
  waiting for transfers between devices: 108 us -> 50.9 us
  other arithmetic: 31.6 us -> 8.4 us
  local copies, waits for them, and re-layouts: 32.2 us -> 10.8 us
  Pallas kernels: 25.6 us -> 45.8 us
  starting transfers between devices: 34 us -> 51.8 us
  matrix products: 6.37 us -> 0 us
    all_gather x2 -> x0, waiting for transfers between devices: 90.9 us -> none  [the longest x1 55 us: per_device(): lax.all_gather(jnp.concatenate([own[1], came[1]]), 'chip', axis=0, tiled=...]
    ppermute x20 -> x30, waiting for transfers between devices: 16.1 us -> 38.6 us  [the longest x8 16.9 us: send(): lax.ppermute(h, 'chip', LINKS[ORDERS[s][k]])]
    convert_element_type x29 -> x1, other arithmetic: 22 us -> 1.25 us  [per_device(): terms = (terms.astype(F32) + swap(terms_sib).astype(F32)).astype(BF16)]
    pallas_call x2 -> x9, Pallas kernels: 21.6 us -> 40.2 us  [the longest x1 16.1 us: attention(): pl.pallas_call(attention_body, out_shape=[small, small, pair] + large, in...]
    slice x13 -> x0, local copies, waits for them, and re-layouts: 17.4 us -> none  [the longest x12 17.4 us: summed(): total = total + array[first + start:first + stop].astype(F32)]
    ppermute x20 -> x30, starting transfers between devices: 24.6 us -> 36.9 us  [the longest x16 20.6 us: across(): lax.ppermute(p, 'chip', LINKS[GATHER_ORDERS[s][k]])]
    all_to_all x1 -> x2, waiting for transfers between devices: 0.01 us -> 7.77 us  [the longest x1 7.77 us: per_device(): lax.all_to_all(terms, 'chip', split_axis=0, concat_axis=0, tiled=True)]
    dot_general x1 -> x0, matrix products: 6.37 us -> none  [per_device(): jnp.dot(hidden_rows, query_weight, preferred_element_type=F32) * scale]
  transfers between devices with their start and end apart: 30 -> 41, of which waited for: 19 -> 20; matrix products, arithmetic and copies ran while one was open for 23% -> 5% of each run, Pallas kernels for 9% -> 25%
where the time goes in v1:
time: 184 us; the launch traced here: 182 us
  starting transfers between devices  51.8 us (28%)
  waiting for transfers between devices  50.9 us (28%)
  Pallas kernels  45.8 us (25%)
  between operations  14.5 us (8%)
  local copies, waits for them, and re-layouts  10.8 us (6%)
  other arithmetic  8.4 us (5%)
    ppermute x16, starting transfers between devices, across(): lax.ppermute(p, 'chip', LINKS[GATHER_ORDERS[s][k]])  20.6 us
    ppermute x8, waiting for transfers between devices, send(): lax.ppermute(h, 'chip', LINKS[ORDERS[s][k]])  16.9 us
    pallas_call x1, Pallas kernels, attention(): pl.pallas_call(attention_body, out_shape=[small, small, pair] + large, in...  16.1 us
    ppermute x16, waiting for transfers between devices, across(): lax.ppermute(p, 'chip', LINKS[GATHER_ORDERS[s][k]])  13.8 us
    ppermute x8, starting transfers between devices, send(): lax.ppermute(h, 'chip', LINKS[ORDERS[s][k]])  8.76 us
    all_to_all x1, starting transfers between devices, per_device(): lax.all_to_all(asked, 'grp', split_axis=0, concat_axis=0, tiled=True)  8.6 us
    unnamed x51, local copies, waits for them, and re-layouts  8.01 us
    ppermute x6, waiting for transfers between devices, per_device(): lax.ppermute(square[3 * pair + m], 'chip', square_pairs(pair, m + 1))  7.94 us
  transfers between devices with their start and end apart: 41, of which 20 were waited for; matrix products, arithmetic and copies ran while one was open for 5% of the time, Pallas kernels for 25%

profile of v1, /device:TPU:8, one launch (start us, length us, event | category | flops | bytes accessed | tf_op | source)
XLA Modules:
  0.0 182.2 jit_solution(9864860612005582102)
XLA Ops:
  12.4 1.9 %collective-permute-start.6 = (bf16[3,128,128]{2,1,0:T(8,128)(2,1)S(1)}, bf16[3,128,128]{2,1,0:T(8,128)(2,1)S(1)}, u32[]{:S(2)}, u32[]{:S(2)}) collective-permute-start(bf16[3,128,128]{2,1,0:T(8,128)(2,1)S(1)} %get-tuple-element.97), channel_id=1, source_target_pairs={{0,24},{2,26},{4,28},{6,30},{8,16},{10,18},{12,20},{14,22},{16,8},... | collective-permute-start | bytes 294920 | tf_op jit(solution)/shard_map/gather/ppermute | solution.py:481
  14.3 2.5 %collective-permute-start.8 = (bf16[3,128,128]{2,1,0:T(8,128)(2,1)S(1)}, bf16[3,128,128]{2,1,0:T(8,128)(2,1)S(1)}, u32[]{:S(2)}, u32[]{:S(2)}) collective-permute-start(bf16[3,128,128]{2,1,0:T(8,128)(2,1)S(1)} %get-tuple-element.98), channel_id=1, source_target_pairs={{0,6},{2,4},{4,2},{6,0},{8,14},{10,12},{12,10},{14,8},{16,22},{18,... | collective-permute-start | bytes 294920 | tf_op jit(solution)/shard_map/gather/ppermute | solution.py:481
  21.9 4.7 %collective-permute-done.9 = bf16[6,128,128]{2,1,0:T(8,128)(2,1)S(1)} collective-permute-done((bf16[6,128,128]{2,1,0:T(8,128)(2,1)S(1)}, bf16[6,128,128]{2,1,0:T(8,128)(2,1)S(1)}, u32[]{:S(2)}, u32[]{:S(2)}) %collective-permute-start.9) | collective-permute-done | bytes 196640 | tf_op jit(solution)/shard_map/gather/ppermute | solution.py:481
  30.8 1.8 %collective-permute-start.10 = (bf16[12,128,128]{2,1,0:T(8,128)(2,1)S(1)}, bf16[12,128,128]{2,1,0:T(8,128)(2,1)}, u32[]{:S(2)}, u32[]{:S(2)}) collective-permute-start(bf16[12,128,128]{2,1,0:T(8,128)(2,1)S(1)} %constant_dynamic-update-slice_fusion.refs_0_), channel_id=1, source_target_pairs={{0,24},{2,26},{4,28},{6,30},{8,16},{10,18},{12,20},{14,22},{16,8},... | collective-permute-start | bytes 1179656 | tf_op jit(solution)/shard_map/gather/ppermute | solution.py:481
  33.4 7.5 %project.1 = (bf16[1024,128]{1,0:T(8,128)(2,1)S(1)}, bf16[1024,128]{1,0:T(8,128)(2,1)S(1)}) custom-call(s32[1]{0:T(128)} %bitcast.7.core, bf16[1024,4096]{1,0:T(8,128)(2,1)} %bitcast.47, bf16[4096,256]{1,0:T(8,128)(2,1)S(1)} %copy-done), custom_call_target="tpu_custom_call" | custom-call | tf_op jit(solution)/shard_map/queries/project/pallas_call | solution.py:227
  43.0 3.1 %join_halves.1 = (bf16[24,128,128]{2,1,0:T(8,128)(2,1)S(1)}, bf16[24,128,128]{2,1,0:T(8,128)(2,1)}, bf16[24,128,128]{2,1,0:T(8,128)(2,1)}, bf16[24,128,128]{2,1,0:T(8,128)(2,1)}) custom-call(bf16[12,128,128]{2,1,0:T(8,128)(2,1)S(1)} %constant_dynamic-update-slice_fusion.refs_0_, bf16[12,128,128]{2,1,0:T(8,128)(2,1)S(1)} %copy-done.5, ...), custom_call_target="tpu_custom_call" | custom-call | tf_op jit(solution)/shard_map/gather/join_halves/pallas_call | solution.py:101
  47.7 2.1 %collective-permute-start.16 = (bf16[24,128,128]{2,1,0:T(8,128)(2,1)}, bf16[24,128,128]{2,1,0:T(8,128)(2,1)}, u32[]{:S(2)}, u32[]{:S(2)}) collective-permute-start(bf16[24,128,128]{2,1,0:T(8,128)(2,1)} %get-tuple-element.101.refs_4_), channel_id=1, source_target_pairs={{0,2},{2,0},{4,6},{6,4},{8,10},{10,8},{12,14},{14,12},{16,18},{18,... | collective-permute-start | bytes 2359304 | tf_op jit(solution)/shard_map/gather/ppermute | solution.py:481
  52.2 8.6 %all-to-all-start = ((bf16[8,256,256]{2,1,0:T(8,128)(2,1)}), bf16[8,256,256]{2,1,0:T(8,128)(2,1)S(1)}, u32[]{:S(2)}, u32[]{:S(2)}) async-start(bf16[8,256,256]{2,1,0:T(8,128)(2,1)} %fusion.1), calls=%async_computation | async-start | bytes 2097152 | tf_op jit(solution)/shard_map/weight_rows/all_to_all | solution.py:502
  61.4 4.7 %collective-permute-done.14.refs_1_ = bf16[24,128,128]{2,1,0:T(8,128)(2,1)} collective-permute-done((bf16[24,128,128]{2,1,0:T(8,128)(2,1)S(1)}, bf16[24,128,128]{2,1,0:T(8,128)(2,1)}, u32[]{:S(2)}, u32[]{:S(2)}) %collective-permute-start.14) | collective-permute-done | bytes 786464 | tf_op jit(solution)/shard_map/gather/ppermute | solution.py:481
  67.8 2.7 %collective-permute-done.17.refs_7_ = bf16[24,128,128]{2,1,0:T(8,128)(2,1)} collective-permute-done((bf16[24,128,128]{2,1,0:T(8,128)(2,1)}, bf16[24,128,128]{2,1,0:T(8,128)(2,1)}, u32[]{:S(2)}, u32[]{:S(2)}) %collective-permute-start.17) | collective-permute-done | bytes 786464 | tf_op jit(solution)/shard_map/gather/ppermute | solution.py:481
  72.0 16.1 %attention.1 = (bf16[16,64,128]{2,1,0:T(8,128)(2,1)S(1)}, bf16[16,64,128]{2,1,0:T(8,128)(2,1)S(1)}, bf16[2,16,64,128]{3,2,1,0:T(8,128)(2,1)S(1)}, bf16[12,128,12...) custom-call(s32[4,64]{1,0:T(4,128)S(1)} %pad_add_fusion.slots, ...), custom_call_target="tpu_custom_call" | custom-call | tf_op jit(solution)/shard_map/attend/attention/pallas_call | solution.py:353
  97.2 7.8 %weight_terms.1 = (bf16[16,256,128]{2,1,0:T(8,128)(2,1)S(1)}, bf16[16,256,128]{2,1,0:T(8,128)(2,1)S(1)}) custom-call(s32[1]{0:T(128)} %bitcast.7.core, bf16[1024,256]{1,0:T(8,128)(2,1)S(1)} %copy-done.1, bf16[1024,4096]{1,0:T(8,128)(2,1)} %bitcast.48), custom_call_target="tpu_custom_call" | custom-call | tf_op jit(solution)/shard_map/return/weight_terms/pallas_call | solution.py:401
  105.0 8.6 %collective-permute-done.21.refs_4_ = bf16[24,128,128]{2,1,0:T(8,128)(2,1)S(1)} collective-permute-done((bf16[24,128,128]{2,1,0:T(8,128)(2,1)}, bf16[24,128,128]{2,1,0:T(8,128)(2,1)S(1)}, u32[]{:S(2)}, u32[]{:S(2)}) %collective-permute-start.21) | collective-permute-done | bytes 786464 | tf_op jit(solution)/shard_map/return/ppermute | solution.py:69
  116.8 1.9 %collective-permute-start.26 = (bf16[12,128,128]{2,1,0:T(8,128)(2,1)S(1)}, bf16[12,128,128]{2,1,0:T(8,128)(2,1)S(1)}, u32[]{:S(2)}, u32[]{:S(2)}) collective-permute-start(bf16[12,128,128]{2,1,0:T(8,128)(2,1)S(1)} %get-tuple-element.143), channel_id=1, source_target_pairs={{0,24},{2,26},{4,28},{6,30},{8,16},{10,18},{12,20},{14,22},{16,8},... | collective-permute-start | bytes 1179656 | tf_op jit(solution)/shard_map/return/ppermute | solution.py:69
  118.7 1.9 %collective-permute-start.27 = (bf16[12,128,128]{2,1,0:T(8,128)(2,1)S(1)}, bf16[12,128,128]{2,1,0:T(8,128)(2,1)S(1)}, u32[]{:S(2)}, u32[]{:S(2)}) collective-permute-start(bf16[12,128,128]{2,1,0:T(8,128)(2,1)S(1)} %get-tuple-element.144), channel_id=1, source_target_pairs={{0,2},{2,0},{4,6},{6,4},{8,10},{10,8},{12,14},{14,12},{16,18},{18,... | collective-permute-start | bytes 1179656 | tf_op jit(solution)/shard_map/return/ppermute | solution.py:69
  123.9 3.7 %collective-permute-done.25.refs_4_ = bf16[12,128,128]{2,1,0:T(8,128)(2,1)S(1)} collective-permute-done((bf16[12,128,128]{2,1,0:T(8,128)(2,1)S(1)}, bf16[12,128,128]{2,1,0:T(8,128)(2,1)S(1)}, u32[]{:S(2)}, u32[]{:S(2)}) %collective-permute-start.25) | collective-permute-done | bytes 393248 | tf_op jit(solution)/shard_map/return/ppermute | solution.py:69
  133.6 2.4 %collective-permute-start.32 = (bf16[2,3,128,128]{3,2,1,0:T(8,128)(2,1)S(1)}, bf16[2,3,128,128]{3,2,1,0:T(8,128)(2,1)S(1)}, u32[]{:S(2)}, u32[]{:S(2)}) collective-permute-start(bf16[2,3,128,128]{3,2,1,0:T(8,128)(2,1)S(1)} %get-tuple-element.166), channel_id=1, source_target_pairs={{0,10},{2,8},{4,14},{6,12},{8,2},{10,0},{12,6},{14,4},{16,26},{18,... | collective-permute-start | bytes 589832 | tf_op jit(solution)/shard_map/return/ppermute | solution.py:550
  138.3 1.9 %collective-permute-done.30.refs_0_ = bf16[2,3,128,128]{3,2,1,0:T(8,128)(2,1)S(1)} collective-permute-done((bf16[2,3,128,128]{3,2,1,0:T(8,128)(2,1)S(1)}, bf16[2,3,128,128]{3,2,1,0:T(8,128)(2,1)S(1)}, u32[]{:S(2)}, u32[]{:S(2)}) %collective-permute-start.30) | collective-permute-done | bytes 196640 | tf_op jit(solution)/shard_map/return/ppermute | solution.py:550
  142.9 2.0 %collective-permute-done.33.refs_3_ = bf16[2,3,128,128]{3,2,1,0:T(8,128)(2,1)S(1)} collective-permute-done((bf16[2,3,128,128]{3,2,1,0:T(8,128)(2,1)S(1)}, bf16[2,3,128,128]{3,2,1,0:T(8,128)(2,1)S(1)}, u32[]{:S(2)}, u32[]{:S(2)}) %collective-permute-start.33) | collective-permute-done | bytes 196640 | tf_op jit(solution)/shard_map/return/ppermute | solution.py:550
  145.0 3.1 %collective-permute-done.35.refs_5_ = bf16[2,3,128,128]{3,2,1,0:T(8,128)(2,1)S(1)} collective-permute-done((bf16[2,3,128,128]{3,2,1,0:T(8,128)(2,1)S(1)}, bf16[2,3,128,128]{3,2,1,0:T(8,128)(2,1)S(1)}, u32[]{:S(2)}, u32[]{:S(2)}) %collective-permute-start.35) | collective-permute-done | bytes 196640 | tf_op jit(solution)/shard_map/return/ppermute | solution.py:550
  148.7 5.6 %all-to-all-start.1 = ((bf16[16,256,128]{2,1,0:T(8,128)(2,1)}), bf16[16,256,128]{2,1,0:T(8,128)(2,1)S(1)}, u32[]{:S(2)}, u32[]{:S(2)}) async-start(bf16[16,256,128]{2,1,0:T(8,128)(2,1)} %add_convert_fusion), calls=%async_computation.1 | async-start | bytes 2097152 | tf_op jit(solution)/shard_map/return/all_to_all | solution.py:555
  154.3 2.0 %maximum_select_fusion = bf16[16,64,256]{2,1,0:T(8,128)(2,1)} fusion(bf16[16,64,128]{2,1,0:T(8,128)(2,1)} %get-tuple-element.193, bf16[16,64,128]{2,1,0:T(8,128)(2,1)S(1)} %copy-done.9, pred[]{:T(512)S(6)} %eq.81), kind=kLoop, calls=%fused_computation.5 | loop fusion | flops 2359296 | bytes 1048577 | tf_op jit(solution)/shard_map/context/jit(_where)/select_n | solution.py:470
  159.3 7.8 %all-to-all-done.1.terms = bf16[16,256,128]{2,1,0:T(8,128)(2,1)S(1)} async-done(((bf16[16,256,128]{2,1,0:T(8,128)(2,1)}), bf16[16,256,128]{2,1,0:T(8,128)(2,1)S(1)}, u32[]{:S(2)}, u32[]{:S(2)}) %all-to-all-start.1) | async-done | bytes 1048608 | tf_op jit(solution)/shard_map/return/all_to_all | solution.py:555
  167.9 5.6 %hidden_grads.1 = bf16[1024,512]{1,0:T(8,128)(2,1)} custom-call(s32[1]{0:T(128)} %bitcast.7.core, bf16[8,1024,256]{2,1,0:T(8,128)(2,1)} %bitcast.49, bf16[8,256,256]{2,1,0:T(8,128)(2,1)S(1)} %all-to-all-done.mine, bf16[8,256,256]{2,1,0:T(8,128)(2,1)S(1)} %collective-permute-done.37.other), custom_call_target="tpu_custom_call" | custom-call | tf_op jit(solution)/shard_map/return/hidden_grads/pallas_call | solution.py:437
  (149 shorter events, 57.8 us)
Async XLA Ops:
  17.5 13.2 %collective-permute-start.3 = (bf16[6,128,128]{2,1,0:T(8,128)(2,1)S(1)}, bf16[6,128,128]{2,1,0:T(8,128)(2,1)S(1)}, u32[]{:S(2)}, u32[]{:S(2)}) collective-permute-start(bf16[6,128,128]{2,1,0:T(8,128)(2,1)S(1)} %pad_maximum_fusion.1), channel_id=1, source_target_pairs={{0,2},{2,0},{4,6},{6,4},{8,10},{10,8},{12,14},{14,12},{16,18},{18,... | collective-permute-start | bytes 589832 | tf_op jit(solution)/shard_map/gather/ppermute | solution.py:481
  18.9 10.3 %collective-permute-start.5 = (bf16[6,128,128]{2,1,0:T(8,128)(2,1)S(1)}, bf16[6,128,128]{2,1,0:T(8,128)(2,1)S(1)}, u32[]{:S(2)}, u32[]{:S(2)}) collective-permute-start(bf16[6,128,128]{2,1,0:T(8,128)(2,1)S(1)} %pad_maximum_fusion.2), channel_id=1, source_target_pairs={{0,24},{2,26},{4,28},{6,30},{8,16},{10,18},{12,20},{14,22},{16,8},... | collective-permute-start | bytes 589832 | tf_op jit(solution)/shard_map/gather/ppermute | solution.py:481
  27.3 13.5 %collective-permute-start.13 = (bf16[12,128,128]{2,1,0:T(8,128)(2,1)}, bf16[12,128,128]{2,1,0:T(8,128)(2,1)}, u32[]{:S(2)}, u32[]{:S(2)}) collective-permute-start(bf16[12,128,128]{2,1,0:T(8,128)(2,1)} %constant_dynamic-update-slice_fusion.9.refs_3_), channel_id=1, source_target_pairs={{0,2},{2,0},{4,6},{6,4},{8,10},{10,8},{12,14},{14,12},{16,18},{18,... | collective-permute-start | bytes 1179656 | tf_op jit(solution)/shard_map/gather/ppermute | solution.py:481
  28.7 12.1 %collective-permute-start.12 = (bf16[12,128,128]{2,1,0:T(8,128)(2,1)S(1)}, bf16[12,128,128]{2,1,0:T(8,128)(2,1)}, u32[]{:S(2)}, u32[]{:S(2)}) collective-permute-start(bf16[12,128,128]{2,1,0:T(8,128)(2,1)S(1)} %constant_dynamic-update-slice_fusion.6.refs_2_), channel_id=1, source_target_pairs={{0,8},{2,10},{4,12},{6,14},{8,0},{10,2},{12,4},{14,6},{16,24},{18,... | collective-permute-start | bytes 1179656 | tf_op jit(solution)/shard_map/gather/ppermute | solution.py:481
  29.3 11.6 %collective-permute-start.11 = (bf16[12,128,128]{2,1,0:T(8,128)(2,1)S(1)}, bf16[12,128,128]{2,1,0:T(8,128)(2,1)}, u32[]{:S(2)}, u32[]{:S(2)}) collective-permute-start(bf16[12,128,128]{2,1,0:T(8,128)(2,1)S(1)} %constant_dynamic-update-slice_fusion.3.refs_1_), channel_id=1, source_target_pairs={{0,6},{2,4},{4,2},{6,0},{8,14},{10,12},{12,10},{14,8},{16,22},{18,... | collective-permute-start | bytes 1179656 | tf_op jit(solution)/shard_map/gather/ppermute | solution.py:481
  30.8 10.1 %collective-permute-start.10 = (bf16[12,128,128]{2,1,0:T(8,128)(2,1)S(1)}, bf16[12,128,128]{2,1,0:T(8,128)(2,1)}, u32[]{:S(2)}, u32[]{:S(2)}) collective-permute-start(bf16[12,128,128]{2,1,0:T(8,128)(2,1)S(1)} %constant_dynamic-update-slice_fusion.refs_0_), channel_id=1, source_target_pairs={{0,24},{2,26},{4,28},{6,30},{8,16},{10,18},{12,20},{14,22},{16,8},... | collective-permute-start | bytes 1179656 | tf_op jit(solution)/shard_map/gather/ppermute | solution.py:481
  33.4 27.6 %collective-permute-start = (s32[48]{0:T(128)}, s32[48]{0:T(128)S(1)}, u32[]{:S(2)}, u32[]{:S(2)}) collective-permute-start(s32[48]{0:T(128)} %pad_add_fusion.1), channel_id=1, source_target_pairs={{0,1},{1,0},{2,3},{3,2},{4,5},{5,4},{6,7},{7,6},{8,9},{9,8},{10,11... | collective-permute-start | bytes 584 | tf_op jit(solution)/shard_map/slots/ppermute | solution.py:65
  46.0 20.1 %collective-permute-start.14 = (bf16[24,128,128]{2,1,0:T(8,128)(2,1)S(1)}, bf16[24,128,128]{2,1,0:T(8,128)(2,1)}, u32[]{:S(2)}, u32[]{:S(2)}) collective-permute-start(bf16[24,128,128]{2,1,0:T(8,128)(2,1)S(1)} %get-tuple-element.99.refs_0_), channel_id=1, source_target_pairs={{0,6},{2,4},{4,2},{6,0},{8,14},{10,12},{12,10},{14,8},{16,22},{18,... | collective-permute-start | bytes 2359304 | tf_op jit(solution)/shard_map/gather/ppermute | solution.py:481
  46.3 20.0 %collective-permute-start.15 = (bf16[24,128,128]{2,1,0:T(8,128)(2,1)}, bf16[24,128,128]{2,1,0:T(8,128)(2,1)}, u32[]{:S(2)}, u32[]{:S(2)}) collective-permute-start(bf16[24,128,128]{2,1,0:T(8,128)(2,1)} %get-tuple-element.100.refs_2_), channel_id=1, source_target_pairs={{0,8},{2,10},{4,12},{6,14},{8,0},{10,2},{12,4},{14,6},{16,24},{18,... | collective-permute-start | bytes 2359304 | tf_op jit(solution)/shard_map/gather/ppermute | solution.py:481
  47.7 20.1 %collective-permute-start.16 = (bf16[24,128,128]{2,1,0:T(8,128)(2,1)}, bf16[24,128,128]{2,1,0:T(8,128)(2,1)}, u32[]{:S(2)}, u32[]{:S(2)}) collective-permute-start(bf16[24,128,128]{2,1,0:T(8,128)(2,1)} %get-tuple-element.101.refs_4_), channel_id=1, source_target_pairs={{0,2},{2,0},{4,6},{6,4},{8,10},{10,8},{12,14},{14,12},{16,18},{18,... | collective-permute-start | bytes 2359304 | tf_op jit(solution)/shard_map/gather/ppermute | solution.py:481
  49.8 20.6 %collective-permute-start.17 = (bf16[24,128,128]{2,1,0:T(8,128)(2,1)}, bf16[24,128,128]{2,1,0:T(8,128)(2,1)}, u32[]{:S(2)}, u32[]{:S(2)}) collective-permute-start(bf16[24,128,128]{2,1,0:T(8,128)(2,1)} %get-tuple-element.102.refs_6_), channel_id=1, source_target_pairs={{0,24},{2,26},{4,28},{6,30},{8,16},{10,18},{12,20},{14,22},{16,8},... | collective-permute-start | bytes 2359304 | tf_op jit(solution)/shard_map/gather/ppermute | solution.py:481
  52.2 40.2 %all-to-all-start = ((bf16[8,256,256]{2,1,0:T(8,128)(2,1)}), bf16[8,256,256]{2,1,0:T(8,128)(2,1)S(1)}, u32[]{:S(2)}, u32[]{:S(2)}) async-start(bf16[8,256,256]{2,1,0:T(8,128)(2,1)} %fusion.1), calls=%async_computation | async-start | bytes 2097152 | tf_op jit(solution)/shard_map/weight_rows/all_to_all | solution.py:502
  60.8 107.1 %all-gather.3.cloned.1.call-start = ((), (), s32[]{:S(2)}) async-start(), calls=%async_computation.2 | async-start | bytes 4718592 | tf_op jit(solution)/shard_map/grad_queries/all_gather | solution.py:537
  92.4 21.1 %collective-permute-start.21 = (bf16[24,128,128]{2,1,0:T(8,128)(2,1)}, bf16[24,128,128]{2,1,0:T(8,128)(2,1)S(1)}, u32[]{:S(2)}, u32[]{:S(2)}) collective-permute-start(bf16[24,128,128]{2,1,0:T(8,128)(2,1)} %get-tuple-element.125), channel_id=1, source_target_pairs={{0,24},{2,26},{4,28},{6,30},{8,16},{10,18},{12,20},{14,22},{16,8},... | collective-permute-start | bytes 2359304 | tf_op jit(solution)/shard_map/return/ppermute | solution.py:69
  93.8 19.7 %collective-permute-start.22 = (bf16[24,128,128]{2,1,0:T(8,128)(2,1)}, bf16[24,128,128]{2,1,0:T(8,128)(2,1)S(1)}, u32[]{:S(2)}, u32[]{:S(2)}) collective-permute-start(bf16[24,128,128]{2,1,0:T(8,128)(2,1)} %get-tuple-element.126), channel_id=1, source_target_pairs={{0,6},{2,4},{4,2},{6,0},{8,14},{10,12},{12,10},{14,8},{16,22},{18,... | collective-permute-start | bytes 2359304 | tf_op jit(solution)/shard_map/return/ppermute | solution.py:69
  95.2 19.2 %collective-permute-start.23 = (bf16[24,128,128]{2,1,0:T(8,128)(2,1)}, bf16[24,128,128]{2,1,0:T(8,128)(2,1)S(1)}, u32[]{:S(2)}, u32[]{:S(2)}) collective-permute-start(bf16[24,128,128]{2,1,0:T(8,128)(2,1)} %get-tuple-element.127), channel_id=1, source_target_pairs={{0,8},{2,10},{4,12},{6,14},{8,0},{10,2},{12,4},{14,6},{16,24},{18,... | collective-permute-start | bytes 2359304 | tf_op jit(solution)/shard_map/return/ppermute | solution.py:69
  95.3 19.2 %collective-permute-start.24 = (bf16[24,128,128]{2,1,0:T(8,128)(2,1)S(1)}, bf16[24,128,128]{2,1,0:T(8,128)(2,1)S(1)}, u32[]{:S(2)}, u32[]{:S(2)}) collective-permute-start(bf16[24,128,128]{2,1,0:T(8,128)(2,1)S(1)} %copy-done.19), channel_id=1, source_target_pairs={{0,2},{2,0},{4,6},{6,4},{8,10},{10,8},{12,14},{14,12},{16,18},{18,... | collective-permute-start | bytes 2359304 | tf_op jit(solution)/shard_map/return/ppermute | solution.py:69
  116.1 11.5 %collective-permute-start.25 = (bf16[12,128,128]{2,1,0:T(8,128)(2,1)S(1)}, bf16[12,128,128]{2,1,0:T(8,128)(2,1)S(1)}, u32[]{:S(2)}, u32[]{:S(2)}) collective-permute-start(bf16[12,128,128]{2,1,0:T(8,128)(2,1)S(1)} %get-tuple-element.142), channel_id=1, source_target_pairs={{0,6},{2,4},{4,2},{6,0},{8,14},{10,12},{12,10},{14,8},{16,22},{18,... | collective-permute-start | bytes 1179656 | tf_op jit(solution)/shard_map/return/ppermute | solution.py:69
  116.8 12.4 %collective-permute-start.26 = (bf16[12,128,128]{2,1,0:T(8,128)(2,1)S(1)}, bf16[12,128,128]{2,1,0:T(8,128)(2,1)S(1)}, u32[]{:S(2)}, u32[]{:S(2)}) collective-permute-start(bf16[12,128,128]{2,1,0:T(8,128)(2,1)S(1)} %get-tuple-element.143), channel_id=1, source_target_pairs={{0,24},{2,26},{4,28},{6,30},{8,16},{10,18},{12,20},{14,22},{16,8},... | collective-permute-start | bytes 1179656 | tf_op jit(solution)/shard_map/return/ppermute | solution.py:69
  118.7 11.1 %collective-permute-start.27 = (bf16[12,128,128]{2,1,0:T(8,128)(2,1)S(1)}, bf16[12,128,128]{2,1,0:T(8,128)(2,1)S(1)}, u32[]{:S(2)}, u32[]{:S(2)}) collective-permute-start(bf16[12,128,128]{2,1,0:T(8,128)(2,1)S(1)} %get-tuple-element.144), channel_id=1, source_target_pairs={{0,2},{2,0},{4,6},{6,4},{8,10},{10,8},{12,14},{14,12},{16,18},{18,... | collective-permute-start | bytes 1179656 | tf_op jit(solution)/shard_map/return/ppermute | solution.py:69
  120.7 10.6 %collective-permute-start.28 = (bf16[12,128,128]{2,1,0:T(8,128)(2,1)S(1)}, bf16[12,128,128]{2,1,0:T(8,128)(2,1)S(1)}, u32[]{:S(2)}, u32[]{:S(2)}) collective-permute-start(bf16[12,128,128]{2,1,0:T(8,128)(2,1)S(1)} %get-tuple-element.145), channel_id=1, source_target_pairs={{0,8},{2,10},{4,12},{6,14},{8,0},{10,2},{12,4},{14,6},{16,24},{18,... | collective-permute-start | bytes 1179656 | tf_op jit(solution)/shard_map/return/ppermute | solution.py:69
  142.8 25.0 %collective-permute-start.37 = (bf16[8,256,256]{2,1,0:T(8,128)(2,1)S(1)}, bf16[8,256,256]{2,1,0:T(8,128)(2,1)S(1)}, u32[]{:S(2)}, u32[]{:S(2)}) collective-permute-start(bf16[8,256,256]{2,1,0:T(8,128)(2,1)S(1)} %all-to-all-done.mine), channel_id=1, source_target_pairs={{0,1},{1,0},{2,3},{3,2},{4,5},{5,4},{6,7},{7,6},{8,9},{9,8},{10,11... | collective-permute-start | bytes 3145736 | tf_op jit(solution)/shard_map/grad_queries/ppermute | solution.py:65
  148.7 18.3 %all-to-all-start.1 = ((bf16[16,256,128]{2,1,0:T(8,128)(2,1)}), bf16[16,256,128]{2,1,0:T(8,128)(2,1)S(1)}, u32[]{:S(2)}, u32[]{:S(2)}) async-start(bf16[16,256,128]{2,1,0:T(8,128)(2,1)} %add_convert_fusion), calls=%async_computation.1 | async-start | bytes 2097152 | tf_op jit(solution)/shard_map/return/all_to_all | solution.py:555
  159.1 14.4 %collective-permute-start.36 = (bf16[2,3,128,128]{3,2,1,0:T(8,128)(2,1)S(1)}, bf16[2,3,128,128]{3,2,1,0:T(8,128)(2,1)}, u32[]{:S(2)}, u32[]{:S(2)}) collective-permute-start(bf16[2,3,128,128]{3,2,1,0:T(8,128)(2,1)S(1)} %get-tuple-element.179), channel_id=1, source_target_pairs={{0,1},{1,0},{2,3},{3,2},{4,5},{5,4},{6,7},{7,6},{8,9},{9,8},{10,11... | collective-permute-start | bytes 589832 | tf_op jit(solution)/shard_map/return/ppermute | solution.py:65
  (38 other events, 275.0 us)
Sparse Core Ops, SparseCore 0:
  92.6 55.8 all-gather.2

commit v2 on v1

--- a/solution.py
+++ b/solution.py
@@ -39,9 +39,6 @@
 
 
 ORDERS = ((0, 1, 3, 2), (0, 1, 2, 3), (2, 3, 1, 0), (2, 3, 0, 1))
-
-
-GATHER_ORDERS = ((0, 1, 2, 3), (1, 2, 3, 0), (2, 3, 0, 1), (3, 0, 1, 2))
 
 
 def cube_place(mine, chip, order):
@@ -187,21 +184,46 @@
     )(mine, *[in_hbm(a) for a in square])
 
 
+def square_join_body(*refs):
+    cut = refs[0].shape[1]
+    for s in range(4):
+        for m in range(4):
+            for i in range(cut):
+                refs[8 + s][m * cut + i] = refs[2 * m + s // 2][s % 2, i]
+
+
+def join_square(pairs, came):
+    _, cut, block_len, width = pairs[0].shape
+    shape = jax.ShapeDtypeStruct((4 * cut, block_len, width), BF16)
+    return in_vmem(square_join_body, "join_square", [shape] * 4, *pairs, *came)
+
+
 def join_body(*refs):
-    size = refs[0].shape[0]
-
-    def step(i, carry):
-        for s in range(4):
-            refs[8 + s][i] = refs[s][i]
-            refs[8 + s][size + i] = refs[4 + s][i]
-        return carry
-
-    lax.fori_loop(0, size, step, 0, unroll=2)
+    held, came, out, sem = refs[:4], refs[4:8], refs[8:12], refs[12]
+    size = held[0].shape[0]
+    copies = []
+    for s in range(4):
+        for part, ref in enumerate((held[s], came[s])):
+            to = out[s].at[pl.ds(part * size, size)]
+            copies.append(pltpu.make_async_copy(ref, to, sem.at[2 * s + part]))
+    for copy in copies:
+        copy.start()
+    for copy in copies:
+        copy.wait()
 
 
 def join_halves(held, came):
     shape = jax.ShapeDtypeStruct((2 * held[0].shape[0], *held[0].shape[1:]), BF16)
-    return in_vmem(join_body, "join_halves", [shape] * 4, *held, *came)
+    left = pl.BlockSpec(memory_space=pl.ANY)
+    return pl.pallas_call(
+        join_body,
+        out_shape=[shape] * 4,
+        in_specs=[left] * 8,
+        out_specs=[left] * 4,
+        scratch_shapes=[pltpu.SemaphoreType.DMA((8,))],
+        compiler_params=pltpu.CompilerParams(vmem_limit_bytes=MIB),
+        name="join_halves",
+    )(*held, *came)
 
 
 def project_body(core, hid_ref, w_ref, own, other):
@@ -476,13 +498,19 @@
     with jax.named_scope("gather"):
         own, other = both(jnp.stack([keys, values]))
         came = swap(other)
-        held = list(lax.optimization_barrier([own[0], came[0], own[1], came[1]]))
+        pairs = lax.optimization_barrier(
+            [jnp.stack([own[0], came[0]]), jnp.stack([own[1], came[1]])]
+        )
+
         def across(pieces, k):
-            return [lax.ppermute(p, "chip", LINKS[GATHER_ORDERS[s][k]]) for s, p in enumerate(pieces)]
-
-        for k in range(2):
-            came = across(held, k)
-            held = [jnp.concatenate([a, b]) for a, b in zip(held, came)]
+            return [lax.ppermute(p, "chip", LINKS[ORDERS[s][k]]) for s, p in enumerate(pieces)]
+
+        came = [
+            lax.ppermute(pairs[pair], "chip", square_pairs(pair, m))
+            for m in (1, 2, 3)
+            for pair in range(2)
+        ]
+        held = join_square(pairs, came)
         held = join_halves(held, across(held, 2))
         last = across(held, 3)
     with jax.named_scope("queries"):
@@ -519,8 +547,8 @@
 
         slots = jnp.stack(
             [
-                slot(GATHER_ORDERS[:2], 0),
-                slot(GATHER_ORDERS[2:], 2 * CHIPS),
+                slot(ORDERS[:2], 0),
+                slot(ORDERS[2:], 2 * CHIPS),
                 slot(ORDERS[:2], 0),
                 slot(ORDERS[2:], 0),
             ]
@@ -538,7 +566,8 @@
     with jax.named_scope("return"):
         first = send(high, 3)
         terms, terms_sib = weight_terms(core_at, grad_rows, hidden_rows)
-        first, terms, terms_sib = lax.optimization_barrier((first, terms, terms_sib))
+        context = joined(ctx_own, pair[0])
+        first, terms, terms_sib, context = lax.optimization_barrier((first, terms, terms_sib, context))
         halved = combine_half("combine_high", mid, first, mid[0].shape[0])
         halved, terms, terms_sib = lax.optimization_barrier((halved, terms, terms_sib))
         second = send(halved, 2)
@@ -557,12 +586,11 @@
         sums, sums_sib = combine_last(mine, square)
         other = swap(sums_sib)
         other, d_hidden = lax.optimization_barrier((other, d_hidden))
+        d_hidden, terms = lax.optimization_barrier((d_hidden, terms))
         d_keys = joined(sums[0], other[0])
         d_values = joined(sums[1], other[1])
         d_weight = weight_sum(terms)
         d_hidden = d_hidden.reshape(spans, span_len, wide)
-    with jax.named_scope("context"):
-        context = joined(ctx_own, pair[0])
     return context, d_hidden, d_keys, d_values, d_weight
 
 

time: 184 us -> 223 us (1.21)
  Pallas kernels: 45.8 us -> 92.6 us
  waiting for transfers between devices: 50.9 us -> 46.4 us
  local copies, waits for them, and re-layouts: 10.8 us -> 7.11 us
    pallas_call x0 -> x1, Pallas kernels: none -> 49 us  [join_halves(): pl.pallas_call(join_body, out_shape=[shape] * 4, in_specs=[left] * 8, out...]
    all_to_all x1, waiting for transfers between devices: 7.77 us -> 4.08 us  [per_device(): lax.all_to_all(terms, 'chip', split_axis=0, concat_axis=0, tiled=True)]
    ppermute x16 -> x14, waiting for transfers between devices: 13.8 us -> 16.1 us  [the longest x8 10.2 us: across(): lax.ppermute(p, 'chip', LINKS[ORDERS[s][k]])]
    unnamed x51 -> x39, local copies, waits for them, and re-layouts: 8.01 us -> 5.83 us
    ppermute x16 -> x14, starting transfers between devices: 20.6 us -> 20.9 us  [the longest x6 10.6 us: per_device(): lax.ppermute(pairs[pair], 'chip', square_pairs(pair, m))]
  transfers between devices with their start and end apart: 41 -> 39, of which waited for: 20 -> 23; matrix products, arithmetic and copies ran while one was open for 5% -> 3% of each run, Pallas kernels for 25% -> 41%
where the time goes in v2:
time: 223 us; the launch traced here: 221 us
  Pallas kernels  92.6 us (42%)
  starting transfers between devices  53.4 us (24%)
  waiting for transfers between devices  46.4 us (21%)
  between operations  14.5 us (7%)
  other arithmetic  7.49 us (3%)
  local copies, waits for them, and re-layouts  7.11 us (3%)
    pallas_call x1, Pallas kernels, join_halves(): pl.pallas_call(join_body, out_shape=[shape] * 4, in_specs=[left] * 8, out...  49 us
    pallas_call x1, Pallas kernels, attention(): pl.pallas_call(attention_body, out_shape=[small, small, pair] + large, in...  16 us
    ppermute x8, waiting for transfers between devices, send(): lax.ppermute(h, 'chip', LINKS[ORDERS[s][k]])  15 us
    ppermute x6, starting transfers between devices, per_device(): lax.ppermute(pairs[pair], 'chip', square_pairs(pair, m))  10.6 us
    ppermute x8, starting transfers between devices, across(): lax.ppermute(p, 'chip', LINKS[ORDERS[s][k]])  10.4 us
    ppermute x8, waiting for transfers between devices, across(): lax.ppermute(p, 'chip', LINKS[ORDERS[s][k]])  10.2 us
    ppermute x8, starting transfers between devices, send(): lax.ppermute(h, 'chip', LINKS[ORDERS[s][k]])  9.42 us
    ppermute x6, starting transfers between devices, per_device(): lax.ppermute(square[3 * pair + m], 'chip', square_pairs(pair, m + 1))  8.8 us
  transfers between devices with their start and end apart: 39, of which 23 were waited for; matrix products, arithmetic and copies ran while one was open for 3% of the time, Pallas kernels for 41%

profile of v2, /device:TPU:8, one launch (start us, length us, event | category | flops | bytes accessed | tf_op | source)
XLA Modules:
  0.0 221.5 jit_solution(16276066803805566285)
XLA Ops:
  13.9 3.6 %collective-permute-start.7 = (bf16[2,3,128,128]{3,2,1,0:T(8,128)(2,1)S(1)}, bf16[2,3,128,128]{3,2,1,0:T(8,128)(2,1)S(1)}, u32[]{:S(2)}, u32[]{:S(2)}) collective-permute-start(bf16[2,3,128,128]{3,2,1,0:T(8,128)(2,1)S(1)} %pad_maximum_fusion.2.refs_1_), channel_id=1, source_target_pairs={{0,30},{2,28},{4,26},{6,24},{8,22},{10,20},{12,18},{14,16},{16,14}... | collective-permute-start | bytes 589832 | tf_op jit(solution)/shard_map/gather/ppermute | solution.py:509
  19.0 2.8 %collective-permute-start.3 = (bf16[2,3,128,128]{3,2,1,0:T(8,128)(2,1)S(1)}, bf16[2,3,128,128]{3,2,1,0:T(8,128)(2,1)S(1)}, u32[]{:S(2)}, u32[]{:S(2)}) collective-permute-start(bf16[2,3,128,128]{3,2,1,0:T(8,128)(2,1)S(1)} %pad_maximum_fusion.2.refs_1_), channel_id=1, source_target_pairs={{0,24},{2,26},{4,28},{6,30},{8,16},{10,18},{12,20},{14,22},{16,8},... | collective-permute-start | bytes 589832 | tf_op jit(solution)/shard_map/gather/ppermute | solution.py:509
  23.1 3.5 %collective-permute-done.5.refs_5_ = bf16[2,3,128,128]{3,2,1,0:T(8,128)(2,1)S(1)} collective-permute-done((bf16[2,3,128,128]{3,2,1,0:T(8,128)(2,1)S(1)}, bf16[2,3,128,128]{3,2,1,0:T(8,128)(2,1)S(1)}, u32[]{:S(2)}, u32[]{:S(2)}) %collective-permute-start.5) | collective-permute-done | bytes 196640 | tf_op jit(solution)/shard_map/gather/ppermute | solution.py:509
  28.6 2.4 %collective-permute-start.9 = (bf16[12,128,128]{2,1,0:T(8,128)(2,1)S(1)}, bf16[12,128,128]{2,1,0:T(8,128)(2,1)}, u32[]{:S(2)}, u32[]{:S(2)}) collective-permute-start(bf16[12,128,128]{2,1,0:T(8,128)(2,1)S(1)} %get-tuple-element.103.refs_1_), channel_id=1, source_target_pairs={{0,24},{2,26},{4,28},{6,30},{8,16},{10,18},{12,20},{14,22},{16,8},... | collective-permute-start | bytes 1179656 | tf_op jit(solution)/shard_map/gather/ppermute | solution.py:506
  31.1 2.9 %collective-permute-start.10 = (bf16[12,128,128]{2,1,0:T(8,128)(2,1)S(1)}, bf16[12,128,128]{2,1,0:T(8,128)(2,1)}, u32[]{:S(2)}, u32[]{:S(2)}) collective-permute-start(bf16[12,128,128]{2,1,0:T(8,128)(2,1)S(1)} %get-tuple-element.104.refs_2_), channel_id=1, source_target_pairs={{0,2},{2,0},{4,6},{6,4},{8,10},{10,8},{12,14},{14,12},{16,18},{18,... | collective-permute-start | bytes 1179656 | tf_op jit(solution)/shard_map/gather/ppermute | solution.py:506
  34.8 7.5 %project.1 = (bf16[1024,128]{1,0:T(8,128)(2,1)S(1)}, bf16[1024,128]{1,0:T(8,128)(2,1)S(1)}) custom-call(s32[1]{0:T(128)} %bitcast.3.core, bf16[1024,4096]{1,0:T(8,128)(2,1)} %bitcast.39, bf16[4096,256]{1,0:T(8,128)(2,1)S(1)} %copy-done), custom_call_target="tpu_custom_call" | custom-call | tf_op jit(solution)/shard_map/queries/project/pallas_call | solution.py:249
  45.9 49.0 %join_halves.1 = (bf16[24,128,128]{2,1,0:T(8,128)(2,1)S(1)}, bf16[24,128,128]{2,1,0:T(8,128)(2,1)}, bf16[24,128,128]{2,1,0:T(8,128)(2,1)}, bf16[24,128,128]{2,1,0:T(8,128)(2,1)}) custom-call(bf16[12,128,128]{2,1,0:T(8,128)(2,1)S(1)} %get-tuple-element.102.refs_0_, bf16[12,128,128]{2,1,0:T(8,128)(2,1)S(1)} %copy-done.5, bf16[12,128,128]{2,1,0:T(8,128)(2,1)S(1)} %copy-done.7, ...), custom_call_target="tpu_custom_call" | custom-call | tf_op jit(solution)/shard_map/gather/join_halves/pallas_call | solution.py:218
  94.9 1.7 collective-permute-start.12
  99.9 7.7 %all-to-all-start = ((bf16[8,256,256]{2,1,0:T(8,128)(2,1)}), bf16[8,256,256]{2,1,0:T(8,128)(2,1)S(1)}, u32[]{:S(2)}, u32[]{:S(2)}) async-start(bf16[8,256,256]{2,1,0:T(8,128)(2,1)} %fusion.1), calls=%async_computation | async-start | bytes 2097152 | tf_op jit(solution)/shard_map/weight_rows/all_to_all | solution.py:530
  108.1 6.7 %collective-permute-done.12.refs_1_ = bf16[24,128,128]{2,1,0:T(8,128)(2,1)} collective-permute-done((bf16[24,128,128]{2,1,0:T(8,128)(2,1)S(1)}, bf16[24,128,128]{2,1,0:T(8,128)(2,1)}, u32[]{:S(2)}, u32[]{:S(2)}) %collective-permute-start.12) | collective-permute-done | bytes 786464 | tf_op jit(solution)/shard_map/gather/ppermute | solution.py:506
  118.2 16.0 %attention.1 = (bf16[16,64,128]{2,1,0:T(8,128)(2,1)S(1)}, bf16[16,64,128]{2,1,0:T(8,128)(2,1)S(1)}, bf16[2,16,64,128]{3,2,1,0:T(8,128)(2,1)S(1)}, bf16[12,128,12...) custom-call(s32[4,64]{1,0:T(4,128)S(1)} %pad_add_fusion.slots, ...), custom_call_target="tpu_custom_call" | custom-call | tf_op jit(solution)/shard_map/attend/attention/pallas_call | solution.py:375
  134.4 1.8 collective-permute-done.18
  142.6 7.9 %weight_terms.1 = (bf16[16,256,128]{2,1,0:T(8,128)(2,1)S(1)}, bf16[16,256,128]{2,1,0:T(8,128)(2,1)S(1)}) custom-call(s32[1]{0:T(128)} %bitcast.3.core, bf16[1024,256]{1,0:T(8,128)(2,1)S(1)} %copy-done.1, bf16[1024,4096]{1,0:T(8,128)(2,1)} %bitcast.40), custom_call_target="tpu_custom_call" | custom-call | tf_op jit(solution)/shard_map/return/weight_terms/pallas_call | solution.py:423
  151.4 6.9 %collective-permute-done.19.refs_4_ = bf16[24,128,128]{2,1,0:T(8,128)(2,1)S(1)} collective-permute-done((bf16[24,128,128]{2,1,0:T(8,128)(2,1)}, bf16[24,128,128]{2,1,0:T(8,128)(2,1)S(1)}, u32[]{:S(2)}, u32[]{:S(2)}) %collective-permute-start.19) | collective-permute-done | bytes 786464 | tf_op jit(solution)/shard_map/return/ppermute | solution.py:66
  161.8 1.8 collective-permute-start.24
  163.6 1.8 collective-permute-start.25
  169.1 3.6 %collective-permute-done.23.refs_4_ = bf16[12,128,128]{2,1,0:T(8,128)(2,1)S(1)} collective-permute-done((bf16[12,128,128]{2,1,0:T(8,128)(2,1)S(1)}, bf16[12,128,128]{2,1,0:T(8,128)(2,1)S(1)}, u32[]{:S(2)}, u32[]{:S(2)}) %collective-permute-start.23) | collective-permute-done | bytes 393248 | tf_op jit(solution)/shard_map/return/ppermute | solution.py:66
  178.5 2.3 %collective-permute-start.30 = (bf16[2,3,128,128]{3,2,1,0:T(8,128)(2,1)S(1)}, bf16[2,3,128,128]{3,2,1,0:T(8,128)(2,1)S(1)}, u32[]{:S(2)}, u32[]{:S(2)}) collective-permute-start(bf16[2,3,128,128]{3,2,1,0:T(8,128)(2,1)S(1)} %get-tuple-element.174), channel_id=1, source_target_pairs={{0,10},{2,8},{4,14},{6,12},{8,2},{10,0},{12,6},{14,4},{16,26},{18,... | collective-permute-start | bytes 589832 | tf_op jit(solution)/shard_map/return/ppermute | solution.py:579
  180.7 1.8 collective-permute-start.31
  185.0 2.4 %collective-permute-start.33 = (bf16[2,3,128,128]{3,2,1,0:T(8,128)(2,1)S(1)}, bf16[2,3,128,128]{3,2,1,0:T(8,128)(2,1)S(1)}, u32[]{:S(2)}, u32[]{:S(2)}) collective-permute-start(bf16[2,3,128,128]{3,2,1,0:T(8,128)(2,1)S(1)} %get-tuple-element.177), channel_id=1, source_target_pairs={{0,30},{2,28},{4,26},{6,24},{8,22},{10,20},{12,18},{14,16},{16,14}... | collective-permute-start | bytes 589832 | tf_op jit(solution)/shard_map/return/ppermute | solution.py:579
  190.1 2.6 %collective-permute-done.33.refs_5_ = bf16[2,3,128,128]{3,2,1,0:T(8,128)(2,1)S(1)} collective-permute-done((bf16[2,3,128,128]{3,2,1,0:T(8,128)(2,1)S(1)}, bf16[2,3,128,128]{3,2,1,0:T(8,128)(2,1)S(1)}, u32[]{:S(2)}, u32[]{:S(2)}) %collective-permute-start.33) | collective-permute-done | bytes 196640 | tf_op jit(solution)/shard_map/return/ppermute | solution.py:579
  193.4 5.9 %all-to-all-start.1 = ((bf16[16,256,128]{2,1,0:T(8,128)(2,1)}), bf16[16,256,128]{2,1,0:T(8,128)(2,1)S(1)}, u32[]{:S(2)}, u32[]{:S(2)}) async-start(bf16[16,256,128]{2,1,0:T(8,128)(2,1)} %add_convert_fusion), calls=%async_computation.1 | async-start | bytes 2097152 | tf_op jit(solution)/shard_map/return/all_to_all | solution.py:584
  202.3 5.6 %hidden_grads.1 = bf16[1024,512]{1,0:T(8,128)(2,1)} custom-call(s32[1]{0:T(128)} %bitcast.3.core, bf16[8,1024,256]{2,1,0:T(8,128)(2,1)} %bitcast.41, bf16[8,256,256]{2,1,0:T(8,128)(2,1)S(1)} %all-to-all-done.mine, bf16[8,256,256]{2,1,0:T(8,128)(2,1)S(1)} %collective-permute-done.35.other), custom_call_target="tpu_custom_call" | custom-call | tf_op jit(solution)/shard_map/return/hidden_grads/pallas_call | solution.py:459
  207.9 4.1 %all-to-all-done.1.terms = bf16[16,256,128]{2,1,0:T(8,128)(2,1)S(1)} async-done(((bf16[16,256,128]{2,1,0:T(8,128)(2,1)}), bf16[16,256,128]{2,1,0:T(8,128)(2,1)S(1)}, u32[]{:S(2)}, u32[]{:S(2)}) %all-to-all-start.1) | async-done | bytes 1048608 | tf_op jit(solution)/shard_map/return/all_to_all | solution.py:584
  (128 shorter events, 54.8 us)
Async XLA Ops:
  11.7 10.7 %collective-permute-start.4 = (bf16[2,3,128,128]{3,2,1,0:T(8,128)(2,1)S(1)}, bf16[2,3,128,128]{3,2,1,0:T(8,128)(2,1)S(1)}, u32[]{:S(2)}, u32[]{:S(2)}) collective-permute-start(bf16[2,3,128,128]{3,2,1,0:T(8,128)(2,1)S(1)} %pad_maximum_fusion.1.refs_0_), channel_id=1, source_target_pairs={{0,2},{2,0},{4,6},{6,4},{8,10},{10,8},{12,14},{14,12},{16,18},{18,... | collective-permute-start | bytes 589832 | tf_op jit(solution)/shard_map/gather/ppermute | solution.py:509
  13.2 9.9 %collective-permute-start.2 = (bf16[2,3,128,128]{3,2,1,0:T(8,128)(2,1)S(1)}, bf16[2,3,128,128]{3,2,1,0:T(8,128)(2,1)S(1)}, u32[]{:S(2)}, u32[]{:S(2)}) collective-permute-start(bf16[2,3,128,128]{3,2,1,0:T(8,128)(2,1)S(1)} %pad_maximum_fusion.1.refs_0_), channel_id=1, source_target_pairs={{0,8},{2,10},{4,12},{6,14},{8,0},{10,2},{12,4},{14,6},{16,24},{18,... | collective-permute-start | bytes 589832 | tf_op jit(solution)/shard_map/gather/ppermute | solution.py:509
  27.5 14.8 %collective-permute-start.8 = (bf16[12,128,128]{2,1,0:T(8,128)(2,1)S(1)}, bf16[12,128,128]{2,1,0:T(8,128)(2,1)}, u32[]{:S(2)}, u32[]{:S(2)}) collective-permute-start(bf16[12,128,128]{2,1,0:T(8,128)(2,1)S(1)} %get-tuple-element.102.refs_0_), channel_id=1, source_target_pairs={{0,6},{2,4},{4,2},{6,0},{8,14},{10,12},{12,10},{14,8},{16,22},{18,... | collective-permute-start | bytes 1179656 | tf_op jit(solution)/shard_map/gather/ppermute | solution.py:506
  28.6 13.6 %collective-permute-start.9 = (bf16[12,128,128]{2,1,0:T(8,128)(2,1)S(1)}, bf16[12,128,128]{2,1,0:T(8,128)(2,1)}, u32[]{:S(2)}, u32[]{:S(2)}) collective-permute-start(bf16[12,128,128]{2,1,0:T(8,128)(2,1)S(1)} %get-tuple-element.103.refs_1_), channel_id=1, source_target_pairs={{0,24},{2,26},{4,28},{6,30},{8,16},{10,18},{12,20},{14,22},{16,8},... | collective-permute-start | bytes 1179656 | tf_op jit(solution)/shard_map/gather/ppermute | solution.py:506
  31.1 11.2 %collective-permute-start.10 = (bf16[12,128,128]{2,1,0:T(8,128)(2,1)S(1)}, bf16[12,128,128]{2,1,0:T(8,128)(2,1)}, u32[]{:S(2)}, u32[]{:S(2)}) collective-permute-start(bf16[12,128,128]{2,1,0:T(8,128)(2,1)S(1)} %get-tuple-element.104.refs_2_), channel_id=1, source_target_pairs={{0,2},{2,0},{4,6},{6,4},{8,10},{10,8},{12,14},{14,12},{16,18},{18,... | collective-permute-start | bytes 1179656 | tf_op jit(solution)/shard_map/gather/ppermute | solution.py:506
  34.0 9.9 %collective-permute-start.11 = (bf16[12,128,128]{2,1,0:T(8,128)(2,1)}, bf16[12,128,128]{2,1,0:T(8,128)(2,1)}, u32[]{:S(2)}, u32[]{:S(2)}) collective-permute-start(bf16[12,128,128]{2,1,0:T(8,128)(2,1)} %get-tuple-element.105.refs_3_), channel_id=1, source_target_pairs={{0,8},{2,10},{4,12},{6,14},{8,0},{10,2},{12,4},{14,6},{16,24},{18,... | collective-permute-start | bytes 1179656 | tf_op jit(solution)/shard_map/gather/ppermute | solution.py:506
  34.8 73.1 %collective-permute-start = (s32[48]{0:T(128)}, s32[48]{0:T(128)S(1)}, u32[]{:S(2)}, u32[]{:S(2)}) collective-permute-start(s32[48]{0:T(128)} %pad_add_fusion.1), channel_id=1, source_target_pairs={{0,1},{1,0},{2,3},{3,2},{4,5},{5,4},{6,7},{7,6},{8,9},{9,8},{10,11... | collective-permute-start | bytes 584 | tf_op jit(solution)/shard_map/slots/ppermute | solution.py:62
  94.9 19.8 %collective-permute-start.12 = (bf16[24,128,128]{2,1,0:T(8,128)(2,1)S(1)}, bf16[24,128,128]{2,1,0:T(8,128)(2,1)}, u32[]{:S(2)}, u32[]{:S(2)}) collective-permute-start(bf16[24,128,128]{2,1,0:T(8,128)(2,1)S(1)} %get-tuple-element.106.refs_0_), channel_id=1, source_target_pairs={{0,24},{2,26},{4,28},{6,30},{8,16},{10,18},{12,20},{14,22},{16,8},... | collective-permute-start | bytes 2359304 | tf_op jit(solution)/shard_map/gather/ppermute | solution.py:506
  96.6 18.1 %collective-permute-start.13 = (bf16[24,128,128]{2,1,0:T(8,128)(2,1)}, bf16[24,128,128]{2,1,0:T(8,128)(2,1)}, u32[]{:S(2)}, u32[]{:S(2)}) collective-permute-start(bf16[24,128,128]{2,1,0:T(8,128)(2,1)} %get-tuple-element.107.refs_2_), channel_id=1, source_target_pairs={{0,6},{2,4},{4,2},{6,0},{8,14},{10,12},{12,10},{14,8},{16,22},{18,... | collective-permute-start | bytes 2359304 | tf_op jit(solution)/shard_map/gather/ppermute | solution.py:506
  97.9 17.6 %collective-permute-start.14 = (bf16[24,128,128]{2,1,0:T(8,128)(2,1)}, bf16[24,128,128]{2,1,0:T(8,128)(2,1)}, u32[]{:S(2)}, u32[]{:S(2)}) collective-permute-start(bf16[24,128,128]{2,1,0:T(8,128)(2,1)} %get-tuple-element.108.refs_4_), channel_id=1, source_target_pairs={{0,8},{2,10},{4,12},{6,14},{8,0},{10,2},{12,4},{14,6},{16,24},{18,... | collective-permute-start | bytes 2359304 | tf_op jit(solution)/shard_map/gather/ppermute | solution.py:506
  97.9 18.7 %collective-permute-start.15 = (bf16[24,128,128]{2,1,0:T(8,128)(2,1)}, bf16[24,128,128]{2,1,0:T(8,128)(2,1)}, u32[]{:S(2)}, u32[]{:S(2)}) collective-permute-start(bf16[24,128,128]{2,1,0:T(8,128)(2,1)} %get-tuple-element.109.refs_6_), channel_id=1, source_target_pairs={{0,2},{2,0},{4,6},{6,4},{8,10},{10,8},{12,14},{14,12},{16,18},{18,... | collective-permute-start | bytes 2359304 | tf_op jit(solution)/shard_map/gather/ppermute | solution.py:506
  99.9 37.3 %all-to-all-start = ((bf16[8,256,256]{2,1,0:T(8,128)(2,1)}), bf16[8,256,256]{2,1,0:T(8,128)(2,1)S(1)}, u32[]{:S(2)}, u32[]{:S(2)}) async-start(bf16[8,256,256]{2,1,0:T(8,128)(2,1)} %fusion.1), calls=%async_computation | async-start | bytes 2097152 | tf_op jit(solution)/shard_map/weight_rows/all_to_all | solution.py:530
  107.6 94.7 %all-gather.3.cloned.1.call-start = ((), (), s32[]{:S(2)}) async-start(), calls=%async_computation.2 | async-start | bytes 4718592 | tf_op jit(solution)/shard_map/grad_queries/all_gather | solution.py:565
  137.3 21.1 %collective-permute-start.19 = (bf16[24,128,128]{2,1,0:T(8,128)(2,1)}, bf16[24,128,128]{2,1,0:T(8,128)(2,1)S(1)}, u32[]{:S(2)}, u32[]{:S(2)}) collective-permute-start(bf16[24,128,128]{2,1,0:T(8,128)(2,1)} %get-tuple-element.127), channel_id=1, source_target_pairs={{0,24},{2,26},{4,28},{6,30},{8,16},{10,18},{12,20},{14,22},{16,8},... | collective-permute-start | bytes 2359304 | tf_op jit(solution)/shard_map/return/ppermute | solution.py:66
  138.8 19.6 %collective-permute-start.20 = (bf16[24,128,128]{2,1,0:T(8,128)(2,1)}, bf16[24,128,128]{2,1,0:T(8,128)(2,1)S(1)}, u32[]{:S(2)}, u32[]{:S(2)}) collective-permute-start(bf16[24,128,128]{2,1,0:T(8,128)(2,1)} %get-tuple-element.128), channel_id=1, source_target_pairs={{0,6},{2,4},{4,2},{6,0},{8,14},{10,12},{12,10},{14,8},{16,22},{18,... | collective-permute-start | bytes 2359304 | tf_op jit(solution)/shard_map/return/ppermute | solution.py:66
  140.3 19.2 %collective-permute-start.21 = (bf16[24,128,128]{2,1,0:T(8,128)(2,1)}, bf16[24,128,128]{2,1,0:T(8,128)(2,1)S(1)}, u32[]{:S(2)}, u32[]{:S(2)}) collective-permute-start(bf16[24,128,128]{2,1,0:T(8,128)(2,1)} %get-tuple-element.129), channel_id=1, source_target_pairs={{0,8},{2,10},{4,12},{6,14},{8,0},{10,2},{12,4},{14,6},{16,24},{18,... | collective-permute-start | bytes 2359304 | tf_op jit(solution)/shard_map/return/ppermute | solution.py:66
  140.3 19.2 %collective-permute-start.22 = (bf16[24,128,128]{2,1,0:T(8,128)(2,1)S(1)}, bf16[24,128,128]{2,1,0:T(8,128)(2,1)S(1)}, u32[]{:S(2)}, u32[]{:S(2)}) collective-permute-start(bf16[24,128,128]{2,1,0:T(8,128)(2,1)S(1)} %copy-done.17), channel_id=1, source_target_pairs={{0,2},{2,0},{4,6},{6,4},{8,10},{10,8},{12,14},{14,12},{16,18},{18,... | collective-permute-start | bytes 2359304 | tf_op jit(solution)/shard_map/return/ppermute | solution.py:66
  161.1 11.5 %collective-permute-start.23 = (bf16[12,128,128]{2,1,0:T(8,128)(2,1)S(1)}, bf16[12,128,128]{2,1,0:T(8,128)(2,1)S(1)}, u32[]{:S(2)}, u32[]{:S(2)}) collective-permute-start(bf16[12,128,128]{2,1,0:T(8,128)(2,1)S(1)} %get-tuple-element.150), channel_id=1, source_target_pairs={{0,6},{2,4},{4,2},{6,0},{8,14},{10,12},{12,10},{14,8},{16,22},{18,... | collective-permute-start | bytes 1179656 | tf_op jit(solution)/shard_map/return/ppermute | solution.py:66
  161.8 12.4 %collective-permute-start.24 = (bf16[12,128,128]{2,1,0:T(8,128)(2,1)S(1)}, bf16[12,128,128]{2,1,0:T(8,128)(2,1)S(1)}, u32[]{:S(2)}, u32[]{:S(2)}) collective-permute-start(bf16[12,128,128]{2,1,0:T(8,128)(2,1)S(1)} %get-tuple-element.151), channel_id=1, source_target_pairs={{0,24},{2,26},{4,28},{6,30},{8,16},{10,18},{12,20},{14,22},{16,8},... | collective-permute-start | bytes 1179656 | tf_op jit(solution)/shard_map/return/ppermute | solution.py:66
  163.6 11.0 %collective-permute-start.25 = (bf16[12,128,128]{2,1,0:T(8,128)(2,1)S(1)}, bf16[12,128,128]{2,1,0:T(8,128)(2,1)S(1)}, u32[]{:S(2)}, u32[]{:S(2)}) collective-permute-start(bf16[12,128,128]{2,1,0:T(8,128)(2,1)S(1)} %get-tuple-element.152), channel_id=1, source_target_pairs={{0,2},{2,0},{4,6},{6,4},{8,10},{10,8},{12,14},{14,12},{16,18},{18,... | collective-permute-start | bytes 1179656 | tf_op jit(solution)/shard_map/return/ppermute | solution.py:66
  165.4 10.6 %collective-permute-start.26 = (bf16[12,128,128]{2,1,0:T(8,128)(2,1)S(1)}, bf16[12,128,128]{2,1,0:T(8,128)(2,1)S(1)}, u32[]{:S(2)}, u32[]{:S(2)}) collective-permute-start(bf16[12,128,128]{2,1,0:T(8,128)(2,1)S(1)} %get-tuple-element.153), channel_id=1, source_target_pairs={{0,8},{2,10},{4,12},{6,14},{8,0},{10,2},{12,4},{14,6},{16,24},{18,... | collective-permute-start | bytes 1179656 | tf_op jit(solution)/shard_map/return/ppermute | solution.py:66
  178.2 9.9 %collective-permute-start.29 = (bf16[2,3,128,128]{3,2,1,0:T(8,128)(2,1)S(1)}, bf16[2,3,128,128]{3,2,1,0:T(8,128)(2,1)}, u32[]{:S(2)}, u32[]{:S(2)}) collective-permute-start(bf16[2,3,128,128]{3,2,1,0:T(8,128)(2,1)S(1)} %get-tuple-element.173), channel_id=1, source_target_pairs={{0,2},{2,0},{4,6},{6,4},{8,10},{10,8},{12,14},{14,12},{16,18},{18,... | collective-permute-start | bytes 589832 | tf_op jit(solution)/shard_map/return/ppermute | solution.py:579
  188.1 14.1 %collective-permute-start.35 = (bf16[8,256,256]{2,1,0:T(8,128)(2,1)S(1)}, bf16[8,256,256]{2,1,0:T(8,128)(2,1)S(1)}, u32[]{:S(2)}, u32[]{:S(2)}) collective-permute-start(bf16[8,256,256]{2,1,0:T(8,128)(2,1)S(1)} %all-to-all-done.mine), channel_id=1, source_target_pairs={{0,1},{1,0},{2,3},{3,2},{4,5},{5,4},{6,7},{7,6},{8,9},{9,8},{10,11... | collective-permute-start | bytes 3145736 | tf_op jit(solution)/shard_map/grad_queries/ppermute | solution.py:62
  193.4 18.6 %all-to-all-start.1 = ((bf16[16,256,128]{2,1,0:T(8,128)(2,1)}), bf16[16,256,128]{2,1,0:T(8,128)(2,1)S(1)}, u32[]{:S(2)}, u32[]{:S(2)}) async-start(bf16[16,256,128]{2,1,0:T(8,128)(2,1)} %add_convert_fusion), calls=%async_computation.1 | async-start | bytes 2097152 | tf_op jit(solution)/shard_map/return/all_to_all | solution.py:584
  (34 other events, 326.3 us)
Sparse Core Ops, SparseCore 0:
  137.4 55.0 all-gather.2

commit v3 on v2

--- a/solution.py
+++ b/solution.py
@@ -181,7 +181,7 @@
         ],
         compiler_params=pltpu.CompilerParams(vmem_limit_bytes=6 * MIB),
         name="combine_last",
-    )(mine, *[in_hbm(a) for a in square])
+    )(*[in_hbm(a) for a in (mine, *square)])
 
 
 def square_join_body(*refs):
@@ -199,31 +199,20 @@
 
 
 def join_body(*refs):
-    held, came, out, sem = refs[:4], refs[4:8], refs[8:12], refs[12]
-    size = held[0].shape[0]
-    copies = []
-    for s in range(4):
-        for part, ref in enumerate((held[s], came[s])):
-            to = out[s].at[pl.ds(part * size, size)]
-            copies.append(pltpu.make_async_copy(ref, to, sem.at[2 * s + part]))
-    for copy in copies:
-        copy.start()
-    for copy in copies:
-        copy.wait()
+    size = refs[0].shape[0]
+
+    def step(i, carry):
+        for s in range(4):
+            refs[8 + s][i] = refs[s][i]
+            refs[8 + s][size + i] = refs[4 + s][i]
+        return carry
+
+    lax.fori_loop(0, size, step, 0, unroll=2)
 
 
 def join_halves(held, came):
     shape = jax.ShapeDtypeStruct((2 * held[0].shape[0], *held[0].shape[1:]), BF16)
-    left = pl.BlockSpec(memory_space=pl.ANY)
-    return pl.pallas_call(
-        join_body,
-        out_shape=[shape] * 4,
-        in_specs=[left] * 8,
-        out_specs=[left] * 4,
-        scratch_shapes=[pltpu.SemaphoreType.DMA((8,))],
-        compiler_params=pltpu.CompilerParams(vmem_limit_bytes=MIB),
-        name="join_halves",
-    )(*held, *came)
+    return in_vmem(join_body, "join_halves", [shape] * 4, *held, *came)
 
 
 def project_body(core, hid_ref, w_ref, own, other):
@@ -386,7 +375,7 @@
         ],
         compiler_params=pltpu.CompilerParams(vmem_limit_bytes=20 * MIB),
         name="attention",
-    )(slots, counts, q_own, q_sib, g_own, g_sib, *gathered)
+    )(slots, counts, q_own, q_sib, g_own, g_sib, *[in_hbm(a) for a in gathered])
 
 
 def weight_body(core, gq_ref, hid_ref, own, sib, gq_t):
@@ -580,7 +569,7 @@
             for pair in range(2)
             for m in range(3)
         ]
-        square, mine, terms = lax.optimization_barrier((square, mine, terms))
+        square[0], terms = lax.optimization_barrier((square[0], terms))
         terms = lax.all_to_all(terms, "chip", split_axis=0, concat_axis=0, tiled=True)
         d_hidden = hidden_grads(core_at, every_grad, weight_own, weight_other)
         sums, sums_sib = combine_last(mine, square)

time: 223 us -> 193 us (0.87)
  the two profiles are of different devices: /device:TPU:8 before, /device:TPU:1 now
where the time goes in v3:
time: 193 us; the launch traced here: 192 us
  starting transfers between devices  64.9 us (34%)
  waiting for transfers between devices  51.3 us (27%)
  Pallas kernels  46.9 us (24%)
  between operations  14.5 us (8%)
  other arithmetic  7.52 us (4%)
  local copies, waits for them, and re-layouts  6.71 us (3%)
    ppermute x8, starting transfers between devices, swap(): return lax.ppermute(value, 'core', [(0, 1), (1, 0)])  17.7 us
    ppermute x6, waiting for transfers between devices, per_device(): lax.ppermute(square[3 * pair + m], 'chip', square_pairs(pair, m + 1))  16.4 us
    pallas_call x1, Pallas kernels, attention(): pl.pallas_call(attention_body, out_shape=[small, small, pair] + large, in...  16.2 us
    ppermute x8, waiting for transfers between devices, send(): lax.ppermute(h, 'chip', LINKS[ORDERS[s][k]])  15.1 us
    ppermute x6, starting transfers between devices, per_device(): lax.ppermute(square[3 * pair + m], 'chip', square_pairs(pair, m + 1))  15 us
    ppermute x6, waiting for transfers between devices, per_device(): lax.ppermute(pairs[pair], 'chip', square_pairs(pair, m))  10.4 us
    pallas_call x1, Pallas kernels, weight_terms(): pl.pallas_call(weight_body, out_shape=[jax.ShapeDtypeStruct((CHIPS, head_...  7.83 us
    all_to_all x1, starting transfers between devices, per_device(): lax.all_to_all(asked, 'grp', split_axis=0, concat_axis=0, tiled=True)  7.46 us
  transfers between devices with their start and end apart: 39, of which 18 were waited for; matrix products, arithmetic and copies ran while one was open for 3% of the time, Pallas kernels for 24%

profile of v3, /device:TPU:1, one launch (start us, length us, event | category | flops | bytes accessed | tf_op | source)
XLA Modules:
  0.0 191.8 jit_solution(1039447848962841276)
XLA Ops:
  8.6 3.3 %collective-permute-start.1 = (bf16[2,3,128,128]{3,2,1,0:T(8,128)(2,1)S(1)}, bf16[2,3,128,128]{3,2,1,0:T(8,128)(2,1)S(1)}, u32[]{:S(2)}, u32[]{:S(2)}) collective-permute-start(bf16[2,3,128,128]{3,2,1,0:T(8,128)(2,1)S(1)} %get-tuple-element.193), channel_id=1, source_target_pairs={{0,1},{1,0},{2,3},{3,2},{4,5},{5,4},{6,7},{7,6},{8,9},{9,8},{10,11... | collective-permute-start | bytes 589832 | tf_op jit(solution)/shard_map/gather/ppermute | solution.py:62
  13.8 2.0 %collective-permute-start.2 = (bf16[2,3,128,128]{3,2,1,0:T(8,128)(2,1)S(1)}, bf16[2,3,128,128]{3,2,1,0:T(8,128)(2,1)S(1)}, u32[]{:S(2)}, u32[]{:S(2)}) collective-permute-start(bf16[2,3,128,128]{3,2,1,0:T(8,128)(2,1)S(1)} %pad_maximum_fusion.1.refs_0_), channel_id=1, source_target_pairs={{0,8},{2,10},{4,12},{6,14},{8,0},{10,2},{12,4},{14,6},{16,24},{18,... | collective-permute-start | bytes 589832 | tf_op jit(solution)/shard_map/gather/ppermute | solution.py:498
  15.8 3.2 %collective-permute-start.7 = (bf16[2,3,128,128]{3,2,1,0:T(8,128)(2,1)S(1)}, bf16[2,3,128,128]{3,2,1,0:T(8,128)(2,1)S(1)}, u32[]{:S(2)}, u32[]{:S(2)}) collective-permute-start(bf16[2,3,128,128]{3,2,1,0:T(8,128)(2,1)S(1)} %pad_maximum_fusion.2.refs_1_), channel_id=1, source_target_pairs={{0,30},{2,28},{4,26},{6,24},{8,22},{10,20},{12,18},{14,16},{16,14}... | collective-permute-start | bytes 589832 | tf_op jit(solution)/shard_map/gather/ppermute | solution.py:498
  21.0 3.3 %collective-permute-done.4.refs_4_ = bf16[2,3,128,128]{3,2,1,0:T(8,128)(2,1)S(1)} collective-permute-done((bf16[2,3,128,128]{3,2,1,0:T(8,128)(2,1)S(1)}, bf16[2,3,128,128]{3,2,1,0:T(8,128)(2,1)S(1)}, u32[]{:S(2)}, u32[]{:S(2)}) %collective-permute-start.4) | collective-permute-done | bytes 196640 | tf_op jit(solution)/shard_map/gather/ppermute | solution.py:498
  24.3 5.9 %collective-permute-done.5.refs_5_ = bf16[2,3,128,128]{3,2,1,0:T(8,128)(2,1)S(1)} collective-permute-done((bf16[2,3,128,128]{3,2,1,0:T(8,128)(2,1)S(1)}, bf16[2,3,128,128]{3,2,1,0:T(8,128)(2,1)S(1)}, u32[]{:S(2)}, u32[]{:S(2)}) %collective-permute-start.5) | collective-permute-done | bytes 196640 | tf_op jit(solution)/shard_map/gather/ppermute | solution.py:498
  35.8 7.5 %project.1 = (bf16[1024,128]{1,0:T(8,128)(2,1)S(1)}, bf16[1024,128]{1,0:T(8,128)(2,1)S(1)}) custom-call(s32[1]{0:T(128)} %bitcast.3.core, bf16[1024,4096]{1,0:T(8,128)(2,1)} %bitcast.39, bf16[4096,256]{1,0:T(8,128)(2,1)S(1)} %copy-done), custom_call_target="tpu_custom_call" | custom-call | tf_op jit(solution)/shard_map/queries/project/pallas_call | solution.py:238
  45.4 3.1 %join_halves.1 = (bf16[24,128,128]{2,1,0:T(8,128)(2,1)S(1)}, bf16[24,128,128]{2,1,0:T(8,128)(2,1)}, bf16[24,128,128]{2,1,0:T(8,128)(2,1)}, bf16[24,128,128]{2,1,0:T(8,128)(2,1)}) custom-call(bf16[12,128,128]{2,1,0:T(8,128)(2,1)S(1)} %get-tuple-element.96.refs_0_, bf16[12,128,128]{2,1,0:T(8,128)(2,1)S(1)} %copy-done.5, bf16[12,128,128]{2,1,0:T(8,128)(2,1)S(1)} %copy-done.7, ...), custom_call_target="tpu_custom_call" | custom-call | tf_op jit(solution)/shard_map/gather/join_halves/pallas_call | solution.py:98
  54.2 7.5 %all-to-all-start = ((bf16[8,256,256]{2,1,0:T(8,128)(2,1)}), bf16[8,256,256]{2,1,0:T(8,128)(2,1)S(1)}, u32[]{:S(2)}, u32[]{:S(2)}) async-start(bf16[8,256,256]{2,1,0:T(8,128)(2,1)} %fusion.1), calls=%async_computation | async-start | bytes 2097152 | tf_op jit(solution)/shard_map/weight_rows/all_to_all | solution.py:519
  63.8 3.2 %collective-permute-done.12.refs_1_ = bf16[24,128,128]{2,1,0:T(8,128)(2,1)} collective-permute-done((bf16[24,128,128]{2,1,0:T(8,128)(2,1)S(1)}, bf16[24,128,128]{2,1,0:T(8,128)(2,1)}, u32[]{:S(2)}, u32[]{:S(2)}) %collective-permute-start.12) | collective-permute-done | bytes 786464 | tf_op jit(solution)/shard_map/gather/ppermute | solution.py:495
  69.5 2.8 %collective-permute-start.16 = (bf16[16,64,128]{2,1,0:T(8,128)(2,1)S(1)}, bf16[16,64,128]{2,1,0:T(8,128)(2,1)S(1)}, u32[]{:S(2)}, u32[]{:S(2)}) collective-permute-start(bf16[16,64,128]{2,1,0:T(8,128)(2,1)S(1)} %bitcast.38), channel_id=1, source_target_pairs={{0,1},{1,0},{2,3},{3,2},{4,5},{5,4},{6,7},{7,6},{8,9},{9,8},{10,11... | collective-permute-start | bytes 786440 | tf_op jit(solution)/shard_map/queries/ppermute | solution.py:62
  73.5 16.2 %attention.1 = (bf16[16,64,128]{2,1,0:T(8,128)(2,1)S(1)}, bf16[16,64,128]{2,1,0:T(8,128)(2,1)S(1)}, bf16[2,16,64,128]{3,2,1,0:T(8,128)(2,1)S(1)}, bf16[12,128,12...) custom-call(s32[4,64]{1,0:T(4,128)S(1)} %pad_add_fusion.slots, ...), custom_call_target="tpu_custom_call" | custom-call | tf_op jit(solution)/shard_map/attend/attention/pallas_call | solution.py:364
  94.0 1.9 collective-permute-start.20
  97.4 7.8 %weight_terms.1 = (bf16[16,256,128]{2,1,0:T(8,128)(2,1)S(1)}, bf16[16,256,128]{2,1,0:T(8,128)(2,1)S(1)}) custom-call(s32[1]{0:T(128)} %bitcast.3.core, bf16[1024,256]{1,0:T(8,128)(2,1)S(1)} %copy-done.1, bf16[1024,4096]{1,0:T(8,128)(2,1)} %bitcast.40), custom_call_target="tpu_custom_call" | custom-call | tf_op jit(solution)/shard_map/return/weight_terms/pallas_call | solution.py:412
  106.2 6.9 %collective-permute-done.19.refs_4_ = bf16[24,128,128]{2,1,0:T(8,128)(2,1)S(1)} collective-permute-done((bf16[24,128,128]{2,1,0:T(8,128)(2,1)}, bf16[24,128,128]{2,1,0:T(8,128)(2,1)S(1)}, u32[]{:S(2)}, u32[]{:S(2)}) %collective-permute-start.19) | collective-permute-done | bytes 786464 | tf_op jit(solution)/shard_map/return/ppermute | solution.py:66
  115.8 1.8 collective-permute-start.27
  123.4 6.2 %collective-permute-done.23.refs_4_ = bf16[12,128,128]{2,1,0:T(8,128)(2,1)S(1)} collective-permute-done((bf16[12,128,128]{2,1,0:T(8,128)(2,1)S(1)}, bf16[12,128,128]{2,1,0:T(8,128)(2,1)S(1)}, u32[]{:S(2)}, u32[]{:S(2)}) %collective-permute-start.23) | collective-permute-done | bytes 393248 | tf_op jit(solution)/shard_map/return/ppermute | solution.py:66
  134.4 3.5 %collective-permute-done.28.refs_0_ = bf16[2,3,128,128]{3,2,1,0:T(8,128)(2,1)} collective-permute-done((bf16[2,3,128,128]{3,2,1,0:T(8,128)(2,1)S(1)}, bf16[2,3,128,128]{3,2,1,0:T(8,128)(2,1)}, u32[]{:S(2)}, u32[]{:S(2)}) %collective-permute-start.28) | collective-permute-done | bytes 196640 | tf_op jit(solution)/shard_map/return/ppermute | solution.py:568
  137.8 4.4 %all-to-all-start.1 = ((bf16[16,256,128]{2,1,0:T(8,128)(2,1)}), bf16[16,256,128]{2,1,0:T(8,128)(2,1)S(1)}, u32[]{:S(2)}, u32[]{:S(2)}) async-start(bf16[16,256,128]{2,1,0:T(8,128)(2,1)} %add_convert_fusion), calls=%async_computation.1 | async-start | bytes 2097152 | tf_op jit(solution)/shard_map/return/all_to_all | solution.py:573
  146.6 2.4 %collective-permute-start.32 = (bf16[2,3,128,128]{3,2,1,0:T(8,128)(2,1)S(1)}, bf16[2,3,128,128]{3,2,1,0:T(8,128)(2,1)S(1)}, u32[]{:S(2)}, u32[]{:S(2)}) collective-permute-start(bf16[2,3,128,128]{3,2,1,0:T(8,128)(2,1)S(1)} %get-tuple-element.173), channel_id=1, source_target_pairs={{0,6},{2,4},{4,2},{6,0},{8,14},{10,12},{12,10},{14,8},{16,22},{18,... | collective-permute-start | bytes 589832 | tf_op jit(solution)/shard_map/return/ppermute | solution.py:568
  149.0 10.0 %collective-permute-done.29.refs_1_ = bf16[2,3,128,128]{3,2,1,0:T(8,128)(2,1)S(1)} collective-permute-done((bf16[2,3,128,128]{3,2,1,0:T(8,128)(2,1)}, bf16[2,3,128,128]{3,2,1,0:T(8,128)(2,1)S(1)}, u32[]{:S(2)}, u32[]{:S(2)}) %collective-permute-start.29) | collective-permute-done | bytes 196640 | tf_op jit(solution)/shard_map/return/ppermute | solution.py:568
  159.0 7.9 %collective-permute-start.33 = (bf16[2,3,128,128]{3,2,1,0:T(8,128)(2,1)S(1)}, bf16[2,3,128,128]{3,2,1,0:T(8,128)(2,1)S(1)}, u32[]{:S(2)}, u32[]{:S(2)}) collective-permute-start(bf16[2,3,128,128]{3,2,1,0:T(8,128)(2,1)S(1)} %get-tuple-element.174), channel_id=1, source_target_pairs={{0,30},{2,28},{4,26},{6,24},{8,22},{10,20},{12,18},{14,16},{16,14}... | collective-permute-start | bytes 589832 | tf_op jit(solution)/shard_map/return/ppermute | solution.py:568
  166.9 3.0 %collective-permute-done.33.refs_5_ = bf16[2,3,128,128]{3,2,1,0:T(8,128)(2,1)S(1)} collective-permute-done((bf16[2,3,128,128]{3,2,1,0:T(8,128)(2,1)S(1)}, bf16[2,3,128,128]{3,2,1,0:T(8,128)(2,1)S(1)}, u32[]{:S(2)}, u32[]{:S(2)}) %collective-permute-start.33) | collective-permute-done | bytes 196640 | tf_op jit(solution)/shard_map/return/ppermute | solution.py:568
  172.3 4.3 %collective-permute-start.34 = (bf16[2,3,128,128]{3,2,1,0:T(8,128)(2,1)S(1)}, bf16[2,3,128,128]{3,2,1,0:T(8,128)(2,1)}, u32[]{:S(2)}, u32[]{:S(2)}) collective-permute-start(bf16[2,3,128,128]{3,2,1,0:T(8,128)(2,1)S(1)} %get-tuple-element.175), channel_id=1, source_target_pairs={{0,1},{1,0},{2,3},{3,2},{4,5},{5,4},{6,7},{7,6},{8,9},{9,8},{10,11... | collective-permute-start | bytes 589832 | tf_op jit(solution)/shard_map/return/ppermute | solution.py:62
  176.7 5.6 %hidden_grads.1 = bf16[1024,512]{1,0:T(8,128)(2,1)} custom-call(s32[1]{0:T(128)} %bitcast.3.core, bf16[8,1024,256]{2,1,0:T(8,128)(2,1)} %bitcast.41, bf16[8,256,256]{2,1,0:T(8,128)(2,1)S(1)} %all-to-all-done.mine, bf16[8,256,256]{2,1,0:T(8,128)(2,1)S(1)} %collective-permute-done.35.other), custom_call_target="tpu_custom_call" | custom-call | tf_op jit(solution)/shard_map/return/hidden_grads/pallas_call | solution.py:448
  (134 shorter events, 53.8 us)
Async XLA Ops:
  13.6 10.6 %collective-permute-start.4 = (bf16[2,3,128,128]{3,2,1,0:T(8,128)(2,1)S(1)}, bf16[2,3,128,128]{3,2,1,0:T(8,128)(2,1)S(1)}, u32[]{:S(2)}, u32[]{:S(2)}) collective-permute-start(bf16[2,3,128,128]{3,2,1,0:T(8,128)(2,1)S(1)} %pad_maximum_fusion.1.refs_0_), channel_id=1, source_target_pairs={{0,2},{2,0},{4,6},{6,4},{8,10},{10,8},{12,14},{14,12},{16,18},{18,... | collective-permute-start | bytes 589832 | tf_op jit(solution)/shard_map/gather/ppermute | solution.py:498
  19.0 11.2 %collective-permute-start.5 = (bf16[2,3,128,128]{3,2,1,0:T(8,128)(2,1)S(1)}, bf16[2,3,128,128]{3,2,1,0:T(8,128)(2,1)S(1)}, u32[]{:S(2)}, u32[]{:S(2)}) collective-permute-start(bf16[2,3,128,128]{3,2,1,0:T(8,128)(2,1)S(1)} %pad_maximum_fusion.2.refs_1_), channel_id=1, source_target_pairs={{0,6},{2,4},{4,2},{6,0},{8,14},{10,12},{12,10},{14,8},{16,22},{18,... | collective-permute-start | bytes 589832 | tf_op jit(solution)/shard_map/gather/ppermute | solution.py:498
  31.0 12.3 %collective-permute-start.8 = (bf16[12,128,128]{2,1,0:T(8,128)(2,1)S(1)}, bf16[12,128,128]{2,1,0:T(8,128)(2,1)}, u32[]{:S(2)}, u32[]{:S(2)}) collective-permute-start(bf16[12,128,128]{2,1,0:T(8,128)(2,1)S(1)} %get-tuple-element.96.refs_0_), channel_id=1, source_target_pairs={{0,6},{2,4},{4,2},{6,0},{8,14},{10,12},{12,10},{14,8},{16,22},{18,... | collective-permute-start | bytes 1179656 | tf_op jit(solution)/shard_map/gather/ppermute | solution.py:495
  32.0 11.3 %collective-permute-start.9 = (bf16[12,128,128]{2,1,0:T(8,128)(2,1)S(1)}, bf16[12,128,128]{2,1,0:T(8,128)(2,1)}, u32[]{:S(2)}, u32[]{:S(2)}) collective-permute-start(bf16[12,128,128]{2,1,0:T(8,128)(2,1)S(1)} %get-tuple-element.97.refs_1_), channel_id=1, source_target_pairs={{0,24},{2,26},{4,28},{6,30},{8,16},{10,18},{12,20},{14,22},{16,8},... | collective-permute-start | bytes 1179656 | tf_op jit(solution)/shard_map/gather/ppermute | solution.py:495
  34.2 27.8 %collective-permute-start = (s32[48]{0:T(128)}, s32[48]{0:T(128)S(1)}, u32[]{:S(2)}, u32[]{:S(2)}) collective-permute-start(s32[48]{0:T(128)} %pad_add_fusion.1), channel_id=1, source_target_pairs={{0,1},{1,0},{2,3},{3,2},{4,5},{5,4},{6,7},{7,6},{8,9},{9,8},{10,11... | collective-permute-start | bytes 584 | tf_op jit(solution)/shard_map/slots/ppermute | solution.py:62
  48.5 18.5 %collective-permute-start.12 = (bf16[24,128,128]{2,1,0:T(8,128)(2,1)S(1)}, bf16[24,128,128]{2,1,0:T(8,128)(2,1)}, u32[]{:S(2)}, u32[]{:S(2)}) collective-permute-start(bf16[24,128,128]{2,1,0:T(8,128)(2,1)S(1)} %get-tuple-element.100.refs_0_), channel_id=1, source_target_pairs={{0,24},{2,26},{4,28},{6,30},{8,16},{10,18},{12,20},{14,22},{16,8},... | collective-permute-start | bytes 2359304 | tf_op jit(solution)/shard_map/gather/ppermute | solution.py:495
  49.6 18.3 %collective-permute-start.13 = (bf16[24,128,128]{2,1,0:T(8,128)(2,1)}, bf16[24,128,128]{2,1,0:T(8,128)(2,1)}, u32[]{:S(2)}, u32[]{:S(2)}) collective-permute-start(bf16[24,128,128]{2,1,0:T(8,128)(2,1)} %get-tuple-element.101.refs_2_), channel_id=1, source_target_pairs={{0,6},{2,4},{4,2},{6,0},{8,14},{10,12},{12,10},{14,8},{16,22},{18,... | collective-permute-start | bytes 2359304 | tf_op jit(solution)/shard_map/gather/ppermute | solution.py:495
  51.3 16.8 %collective-permute-start.14 = (bf16[24,128,128]{2,1,0:T(8,128)(2,1)}, bf16[24,128,128]{2,1,0:T(8,128)(2,1)}, u32[]{:S(2)}, u32[]{:S(2)}) collective-permute-start(bf16[24,128,128]{2,1,0:T(8,128)(2,1)} %get-tuple-element.102.refs_4_), channel_id=1, source_target_pairs={{0,8},{2,10},{4,12},{6,14},{8,0},{10,2},{12,4},{14,6},{16,24},{18,... | collective-permute-start | bytes 2359304 | tf_op jit(solution)/shard_map/gather/ppermute | solution.py:495
  52.0 17.5 %collective-permute-start.15 = (bf16[24,128,128]{2,1,0:T(8,128)(2,1)}, bf16[24,128,128]{2,1,0:T(8,128)(2,1)}, u32[]{:S(2)}, u32[]{:S(2)}) collective-permute-start(bf16[24,128,128]{2,1,0:T(8,128)(2,1)} %get-tuple-element.103.refs_6_), channel_id=1, source_target_pairs={{0,2},{2,0},{4,6},{6,4},{8,10},{10,8},{12,14},{14,12},{16,18},{18,... | collective-permute-start | bytes 2359304 | tf_op jit(solution)/shard_map/gather/ppermute | solution.py:495
  54.2 38.5 %all-to-all-start = ((bf16[8,256,256]{2,1,0:T(8,128)(2,1)}), bf16[8,256,256]{2,1,0:T(8,128)(2,1)S(1)}, u32[]{:S(2)}, u32[]{:S(2)}) async-start(bf16[8,256,256]{2,1,0:T(8,128)(2,1)} %fusion.1), calls=%async_computation | async-start | bytes 2097152 | tf_op jit(solution)/shard_map/weight_rows/all_to_all | solution.py:519
  61.7 114.9 %all-gather.3.cloned.1.call-start = ((), (), s32[]{:S(2)}) async-start(), calls=%async_computation.2 | async-start | bytes 4718592 | tf_op jit(solution)/shard_map/grad_queries/all_gather | solution.py:554
  92.7 20.4 %collective-permute-start.19 = (bf16[24,128,128]{2,1,0:T(8,128)(2,1)}, bf16[24,128,128]{2,1,0:T(8,128)(2,1)S(1)}, u32[]{:S(2)}, u32[]{:S(2)}) collective-permute-start(bf16[24,128,128]{2,1,0:T(8,128)(2,1)} %get-tuple-element.121), channel_id=1, source_target_pairs={{0,24},{2,26},{4,28},{6,30},{8,16},{10,18},{12,20},{14,22},{16,8},... | collective-permute-start | bytes 2359304 | tf_op jit(solution)/shard_map/return/ppermute | solution.py:66
  94.0 20.0 %collective-permute-start.20 = (bf16[24,128,128]{2,1,0:T(8,128)(2,1)}, bf16[24,128,128]{2,1,0:T(8,128)(2,1)S(1)}, u32[]{:S(2)}, u32[]{:S(2)}) collective-permute-start(bf16[24,128,128]{2,1,0:T(8,128)(2,1)} %get-tuple-element.122), channel_id=1, source_target_pairs={{0,6},{2,4},{4,2},{6,0},{8,14},{10,12},{12,10},{14,8},{16,22},{18,... | collective-permute-start | bytes 2359304 | tf_op jit(solution)/shard_map/return/ppermute | solution.py:66
  95.8 18.4 %collective-permute-start.21 = (bf16[24,128,128]{2,1,0:T(8,128)(2,1)}, bf16[24,128,128]{2,1,0:T(8,128)(2,1)S(1)}, u32[]{:S(2)}, u32[]{:S(2)}) collective-permute-start(bf16[24,128,128]{2,1,0:T(8,128)(2,1)} %get-tuple-element.123), channel_id=1, source_target_pairs={{0,8},{2,10},{4,12},{6,14},{8,0},{10,2},{12,4},{14,6},{16,24},{18,... | collective-permute-start | bytes 2359304 | tf_op jit(solution)/shard_map/return/ppermute | solution.py:66
  95.8 18.4 %collective-permute-start.22 = (bf16[24,128,128]{2,1,0:T(8,128)(2,1)S(1)}, bf16[24,128,128]{2,1,0:T(8,128)(2,1)S(1)}, u32[]{:S(2)}, u32[]{:S(2)}) collective-permute-start(bf16[24,128,128]{2,1,0:T(8,128)(2,1)S(1)} %copy-done.20), channel_id=1, source_target_pairs={{0,2},{2,0},{4,6},{6,4},{8,10},{10,8},{12,14},{14,12},{16,18},{18,... | collective-permute-start | bytes 2359304 | tf_op jit(solution)/shard_map/return/ppermute | solution.py:66
  117.6 12.0 %collective-permute-start.23 = (bf16[12,128,128]{2,1,0:T(8,128)(2,1)S(1)}, bf16[12,128,128]{2,1,0:T(8,128)(2,1)S(1)}, u32[]{:S(2)}, u32[]{:S(2)}) collective-permute-start(bf16[12,128,128]{2,1,0:T(8,128)(2,1)S(1)} %get-tuple-element.144), channel_id=1, source_target_pairs={{0,6},{2,4},{4,2},{6,0},{8,14},{10,12},{12,10},{14,8},{16,22},{18,... | collective-permute-start | bytes 1179656 | tf_op jit(solution)/shard_map/return/ppermute | solution.py:66
  118.8 11.7 %collective-permute-start.24 = (bf16[12,128,128]{2,1,0:T(8,128)(2,1)S(1)}, bf16[12,128,128]{2,1,0:T(8,128)(2,1)S(1)}, u32[]{:S(2)}, u32[]{:S(2)}) collective-permute-start(bf16[12,128,128]{2,1,0:T(8,128)(2,1)S(1)} %get-tuple-element.145), channel_id=1, source_target_pairs={{0,24},{2,26},{4,28},{6,30},{8,16},{10,18},{12,20},{14,22},{16,8},... | collective-permute-start | bytes 1179656 | tf_op jit(solution)/shard_map/return/ppermute | solution.py:66
  132.8 43.8 %collective-permute-start.35 = (bf16[8,256,256]{2,1,0:T(8,128)(2,1)S(1)}, bf16[8,256,256]{2,1,0:T(8,128)(2,1)S(1)}, u32[]{:S(2)}, u32[]{:S(2)}) collective-permute-start(bf16[8,256,256]{2,1,0:T(8,128)(2,1)S(1)} %all-to-all-done.mine), channel_id=1, source_target_pairs={{0,1},{1,0},{2,3},{3,2},{4,5},{5,4},{6,7},{7,6},{8,9},{9,8},{10,11... | collective-permute-start | bytes 3145736 | tf_op jit(solution)/shard_map/grad_queries/ppermute | solution.py:62
  137.8 44.5 %all-to-all-start.1 = ((bf16[16,256,128]{2,1,0:T(8,128)(2,1)}), bf16[16,256,128]{2,1,0:T(8,128)(2,1)S(1)}, u32[]{:S(2)}, u32[]{:S(2)}) async-start(bf16[16,256,128]{2,1,0:T(8,128)(2,1)} %add_convert_fusion), calls=%async_computation.1 | async-start | bytes 2097152 | tf_op jit(solution)/shard_map/return/all_to_all | solution.py:573
  142.3 16.7 %collective-permute-start.29 = (bf16[2,3,128,128]{3,2,1,0:T(8,128)(2,1)}, bf16[2,3,128,128]{3,2,1,0:T(8,128)(2,1)S(1)}, u32[]{:S(2)}, u32[]{:S(2)}) collective-permute-start(bf16[2,3,128,128]{3,2,1,0:T(8,128)(2,1)} %copy-done.12), channel_id=1, source_target_pairs={{0,2},{2,0},{4,6},{6,4},{8,10},{10,8},{12,14},{14,12},{16,18},{18,... | collective-permute-start | bytes 589832 | tf_op jit(solution)/shard_map/return/ppermute | solution.py:568
  143.6 23.2 %collective-permute-start.30 = (bf16[2,3,128,128]{3,2,1,0:T(8,128)(2,1)}, bf16[2,3,128,128]{3,2,1,0:T(8,128)(2,1)S(1)}, u32[]{:S(2)}, u32[]{:S(2)}) collective-permute-start(bf16[2,3,128,128]{3,2,1,0:T(8,128)(2,1)} %copy-done.11), channel_id=1, source_target_pairs={{0,10},{2,8},{4,14},{6,12},{8,2},{10,0},{12,6},{14,4},{16,26},{18,... | collective-permute-start | bytes 589832 | tf_op jit(solution)/shard_map/return/ppermute | solution.py:568
  144.8 22.0 %collective-permute-start.31 = (bf16[2,3,128,128]{3,2,1,0:T(8,128)(2,1)}, bf16[2,3,128,128]{3,2,1,0:T(8,128)(2,1)S(1)}, u32[]{:S(2)}, u32[]{:S(2)}) collective-permute-start(bf16[2,3,128,128]{3,2,1,0:T(8,128)(2,1)} %copy-done.10), channel_id=1, source_target_pairs={{0,24},{2,26},{4,28},{6,30},{8,16},{10,18},{12,20},{14,22},{16,8},... | collective-permute-start | bytes 589832 | tf_op jit(solution)/shard_map/return/ppermute | solution.py:568
  146.6 20.2 %collective-permute-start.32 = (bf16[2,3,128,128]{3,2,1,0:T(8,128)(2,1)S(1)}, bf16[2,3,128,128]{3,2,1,0:T(8,128)(2,1)S(1)}, u32[]{:S(2)}, u32[]{:S(2)}) collective-permute-start(bf16[2,3,128,128]{3,2,1,0:T(8,128)(2,1)S(1)} %get-tuple-element.173), channel_id=1, source_target_pairs={{0,6},{2,4},{4,2},{6,0},{8,14},{10,12},{12,10},{14,8},{16,22},{18,... | collective-permute-start | bytes 589832 | tf_op jit(solution)/shard_map/return/ppermute | solution.py:568
  159.0 10.9 %collective-permute-start.33 = (bf16[2,3,128,128]{3,2,1,0:T(8,128)(2,1)S(1)}, bf16[2,3,128,128]{3,2,1,0:T(8,128)(2,1)S(1)}, u32[]{:S(2)}, u32[]{:S(2)}) collective-permute-start(bf16[2,3,128,128]{3,2,1,0:T(8,128)(2,1)S(1)} %get-tuple-element.174), channel_id=1, source_target_pairs={{0,30},{2,28},{4,26},{6,24},{8,22},{10,20},{12,18},{14,16},{16,14}... | collective-permute-start | bytes 589832 | tf_op jit(solution)/shard_map/return/ppermute | solution.py:568
  (37 other events, 294.6 us)
Sparse Core Ops, SparseCore 0:
  92.9 54.6 all-gather.2

commit v4 on v3

--- a/solution.py
+++ b/solution.py
@@ -569,7 +569,7 @@
             for pair in range(2)
             for m in range(3)
         ]
-        square[0], terms = lax.optimization_barrier((square[0], terms))
+        square, mine, terms = lax.optimization_barrier((square, mine, terms))
         terms = lax.all_to_all(terms, "chip", split_axis=0, concat_axis=0, tiled=True)
         d_hidden = hidden_grads(core_at, every_grad, weight_own, weight_other)
         sums, sums_sib = combine_last(mine, square)

time: 193 us -> 177 us (0.917)
  the two profiles are of different devices: /device:TPU:1 before, /device:TPU:8 now
where the time goes in v4:
time: 177 us; the launch traced here: 176 us
  starting transfers between devices  53.3 us (30%)
  waiting for transfers between devices  47.5 us (27%)
  Pallas kernels  47 us (27%)
  between operations  14.4 us (8%)
  other arithmetic  7.49 us (4%)
  local copies, waits for them, and re-layouts  5.99 us (3%)
    pallas_call x1, Pallas kernels, attention(): pl.pallas_call(attention_body, out_shape=[small, small, pair] + large, in...  16.2 us
    ppermute x8, waiting for transfers between devices, send(): lax.ppermute(h, 'chip', LINKS[ORDERS[s][k]])  15 us
    ppermute x6, starting transfers between devices, per_device(): lax.ppermute(pairs[pair], 'chip', square_pairs(pair, m))  10.6 us
    ppermute x8, starting transfers between devices, across(): lax.ppermute(p, 'chip', LINKS[ORDERS[s][k]])  10.3 us
    ppermute x8, waiting for transfers between devices, across(): lax.ppermute(p, 'chip', LINKS[ORDERS[s][k]])  10.2 us
    ppermute x8, starting transfers between devices, send(): lax.ppermute(h, 'chip', LINKS[ORDERS[s][k]])  9.42 us
    ppermute x6, starting transfers between devices, per_device(): lax.ppermute(square[3 * pair + m], 'chip', square_pairs(pair, m + 1))  8.79 us
    pallas_call x1, Pallas kernels, weight_terms(): pl.pallas_call(weight_body, out_shape=[jax.ShapeDtypeStruct((CHIPS, head_...  7.86 us
  transfers between devices with their start and end apart: 39, of which 23 were waited for; matrix products, arithmetic and copies ran while one was open for 3% of the time, Pallas kernels for 26%

profile of v4, /device:TPU:8, one launch (start us, length us, event | category | flops | bytes accessed | tf_op | source)
XLA Modules:
  0.0 175.7 jit_solution(11771526690846064257)
XLA Ops:
  13.9 3.6 %collective-permute-start.7 = (bf16[2,3,128,128]{3,2,1,0:T(8,128)(2,1)S(1)}, bf16[2,3,128,128]{3,2,1,0:T(8,128)(2,1)S(1)}, u32[]{:S(2)}, u32[]{:S(2)}) collective-permute-start(bf16[2,3,128,128]{3,2,1,0:T(8,128)(2,1)S(1)} %pad_maximum_fusion.2.refs_1_), channel_id=1, source_target_pairs={{0,30},{2,28},{4,26},{6,24},{8,22},{10,20},{12,18},{14,16},{16,14}... | collective-permute-start | bytes 589832 | tf_op jit(solution)/shard_map/gather/ppermute | solution.py:498
  19.0 2.8 %collective-permute-start.3 = (bf16[2,3,128,128]{3,2,1,0:T(8,128)(2,1)S(1)}, bf16[2,3,128,128]{3,2,1,0:T(8,128)(2,1)S(1)}, u32[]{:S(2)}, u32[]{:S(2)}) collective-permute-start(bf16[2,3,128,128]{3,2,1,0:T(8,128)(2,1)S(1)} %pad_maximum_fusion.2.refs_1_), channel_id=1, source_target_pairs={{0,24},{2,26},{4,28},{6,30},{8,16},{10,18},{12,20},{14,22},{16,8},... | collective-permute-start | bytes 589832 | tf_op jit(solution)/shard_map/gather/ppermute | solution.py:498
  23.1 3.5 %collective-permute-done.5.refs_5_ = bf16[2,3,128,128]{3,2,1,0:T(8,128)(2,1)S(1)} collective-permute-done((bf16[2,3,128,128]{3,2,1,0:T(8,128)(2,1)S(1)}, bf16[2,3,128,128]{3,2,1,0:T(8,128)(2,1)S(1)}, u32[]{:S(2)}, u32[]{:S(2)}) %collective-permute-start.5) | collective-permute-done | bytes 196640 | tf_op jit(solution)/shard_map/gather/ppermute | solution.py:498
  28.6 2.4 %collective-permute-start.9 = (bf16[12,128,128]{2,1,0:T(8,128)(2,1)S(1)}, bf16[12,128,128]{2,1,0:T(8,128)(2,1)}, u32[]{:S(2)}, u32[]{:S(2)}) collective-permute-start(bf16[12,128,128]{2,1,0:T(8,128)(2,1)S(1)} %get-tuple-element.103.refs_1_), channel_id=1, source_target_pairs={{0,24},{2,26},{4,28},{6,30},{8,16},{10,18},{12,20},{14,22},{16,8},... | collective-permute-start | bytes 1179656 | tf_op jit(solution)/shard_map/gather/ppermute | solution.py:495
  31.1 2.9 %collective-permute-start.10 = (bf16[12,128,128]{2,1,0:T(8,128)(2,1)S(1)}, bf16[12,128,128]{2,1,0:T(8,128)(2,1)}, u32[]{:S(2)}, u32[]{:S(2)}) collective-permute-start(bf16[12,128,128]{2,1,0:T(8,128)(2,1)S(1)} %get-tuple-element.104.refs_2_), channel_id=1, source_target_pairs={{0,2},{2,0},{4,6},{6,4},{8,10},{10,8},{12,14},{14,12},{16,18},{18,... | collective-permute-start | bytes 1179656 | tf_op jit(solution)/shard_map/gather/ppermute | solution.py:495
  34.8 7.5 %project.1 = (bf16[1024,128]{1,0:T(8,128)(2,1)S(1)}, bf16[1024,128]{1,0:T(8,128)(2,1)S(1)}) custom-call(s32[1]{0:T(128)} %bitcast.3.core, bf16[1024,4096]{1,0:T(8,128)(2,1)} %bitcast.39, bf16[4096,256]{1,0:T(8,128)(2,1)S(1)} %copy-done), custom_call_target="tpu_custom_call" | custom-call | tf_op jit(solution)/shard_map/queries/project/pallas_call | solution.py:238
  45.9 3.1 %join_halves.1 = (bf16[24,128,128]{2,1,0:T(8,128)(2,1)S(1)}, bf16[24,128,128]{2,1,0:T(8,128)(2,1)}, bf16[24,128,128]{2,1,0:T(8,128)(2,1)}, bf16[24,128,128]{2,1,0:T(8,128)(2,1)}) custom-call(bf16[12,128,128]{2,1,0:T(8,128)(2,1)S(1)} %get-tuple-element.102.refs_0_, bf16[12,128,128]{2,1,0:T(8,128)(2,1)S(1)} %copy-done.5, bf16[12,128,128]{2,1,0:T(8,128)(2,1)S(1)} %copy-done.7, ...), custom_call_target="tpu_custom_call" | custom-call | tf_op jit(solution)/shard_map/gather/join_halves/pallas_call | solution.py:98
  53.9 7.7 %all-to-all-start = ((bf16[8,256,256]{2,1,0:T(8,128)(2,1)}), bf16[8,256,256]{2,1,0:T(8,128)(2,1)S(1)}, u32[]{:S(2)}, u32[]{:S(2)}) async-start(bf16[8,256,256]{2,1,0:T(8,128)(2,1)} %fusion.1), calls=%async_computation | async-start | bytes 2097152 | tf_op jit(solution)/shard_map/weight_rows/all_to_all | solution.py:519
  62.1 6.7 %collective-permute-done.12.refs_1_ = bf16[24,128,128]{2,1,0:T(8,128)(2,1)} collective-permute-done((bf16[24,128,128]{2,1,0:T(8,128)(2,1)S(1)}, bf16[24,128,128]{2,1,0:T(8,128)(2,1)}, u32[]{:S(2)}, u32[]{:S(2)}) %collective-permute-start.12) | collective-permute-done | bytes 786464 | tf_op jit(solution)/shard_map/gather/ppermute | solution.py:495
  72.2 16.2 %attention.1 = (bf16[16,64,128]{2,1,0:T(8,128)(2,1)S(1)}, bf16[16,64,128]{2,1,0:T(8,128)(2,1)S(1)}, bf16[2,16,64,128]{3,2,1,0:T(8,128)(2,1)S(1)}, bf16[12,128,12...) custom-call(s32[4,64]{1,0:T(4,128)S(1)} %pad_add_fusion.slots, ...), custom_call_target="tpu_custom_call" | custom-call | tf_op jit(solution)/shard_map/attend/attention/pallas_call | solution.py:364
  88.6 1.8 %collective-permute-done.18 = bf16[2,16,64,128]{3,2,1,0:T(8,128)(2,1)S(1)} collective-permute-done((bf16[2,16,64,128]{3,2,1,0:T(8,128)(2,1)S(1)}, bf16[2,16,64,128]{3,2,1,0:T(8,128)(2,1)S(1)}, u32[]{:S(2)}, u32[]{:S(2)}) %collective-permute-start.18) | collective-permute-done | bytes 524320 | tf_op jit(solution)/shard_map/grad_queries/ppermute | solution.py:62
  96.8 7.9 %weight_terms.1 = (bf16[16,256,128]{2,1,0:T(8,128)(2,1)S(1)}, bf16[16,256,128]{2,1,0:T(8,128)(2,1)S(1)}) custom-call(s32[1]{0:T(128)} %bitcast.3.core, bf16[1024,256]{1,0:T(8,128)(2,1)S(1)} %copy-done.1, bf16[1024,4096]{1,0:T(8,128)(2,1)} %bitcast.40), custom_call_target="tpu_custom_call" | custom-call | tf_op jit(solution)/shard_map/return/weight_terms/pallas_call | solution.py:412
  105.6 6.9 %collective-permute-done.19.refs_4_ = bf16[24,128,128]{2,1,0:T(8,128)(2,1)S(1)} collective-permute-done((bf16[24,128,128]{2,1,0:T(8,128)(2,1)}, bf16[24,128,128]{2,1,0:T(8,128)(2,1)S(1)}, u32[]{:S(2)}, u32[]{:S(2)}) %collective-permute-start.19) | collective-permute-done | bytes 786464 | tf_op jit(solution)/shard_map/return/ppermute | solution.py:66
  115.9 1.8 %collective-permute-start.24 = (bf16[12,128,128]{2,1,0:T(8,128)(2,1)S(1)}, bf16[12,128,128]{2,1,0:T(8,128)(2,1)S(1)}, u32[]{:S(2)}, u32[]{:S(2)}) collective-permute-start(bf16[12,128,128]{2,1,0:T(8,128)(2,1)S(1)} %get-tuple-element.151), channel_id=1, source_target_pairs={{0,24},{2,26},{4,28},{6,30},{8,16},{10,18},{12,20},{14,22},{16,8},... | collective-permute-start | bytes 1179656 | tf_op jit(solution)/shard_map/return/ppermute | solution.py:66
  117.8 1.8 %collective-permute-start.25 = (bf16[12,128,128]{2,1,0:T(8,128)(2,1)S(1)}, bf16[12,128,128]{2,1,0:T(8,128)(2,1)S(1)}, u32[]{:S(2)}, u32[]{:S(2)}) collective-permute-start(bf16[12,128,128]{2,1,0:T(8,128)(2,1)S(1)} %get-tuple-element.152), channel_id=1, source_target_pairs={{0,2},{2,0},{4,6},{6,4},{8,10},{10,8},{12,14},{14,12},{16,18},{18,... | collective-permute-start | bytes 1179656 | tf_op jit(solution)/shard_map/return/ppermute | solution.py:66
  123.3 3.6 %collective-permute-done.23.refs_4_ = bf16[12,128,128]{2,1,0:T(8,128)(2,1)S(1)} collective-permute-done((bf16[12,128,128]{2,1,0:T(8,128)(2,1)S(1)}, bf16[12,128,128]{2,1,0:T(8,128)(2,1)S(1)}, u32[]{:S(2)}, u32[]{:S(2)}) %collective-permute-start.23) | collective-permute-done | bytes 393248 | tf_op jit(solution)/shard_map/return/ppermute | solution.py:66
  132.6 2.3 %collective-permute-start.30 = (bf16[2,3,128,128]{3,2,1,0:T(8,128)(2,1)S(1)}, bf16[2,3,128,128]{3,2,1,0:T(8,128)(2,1)S(1)}, u32[]{:S(2)}, u32[]{:S(2)}) collective-permute-start(bf16[2,3,128,128]{3,2,1,0:T(8,128)(2,1)S(1)} %get-tuple-element.174), channel_id=1, source_target_pairs={{0,10},{2,8},{4,14},{6,12},{8,2},{10,0},{12,6},{14,4},{16,26},{18,... | collective-permute-start | bytes 589832 | tf_op jit(solution)/shard_map/return/ppermute | solution.py:568
  134.9 1.8 %collective-permute-start.31 = (bf16[2,3,128,128]{3,2,1,0:T(8,128)(2,1)S(1)}, bf16[2,3,128,128]{3,2,1,0:T(8,128)(2,1)S(1)}, u32[]{:S(2)}, u32[]{:S(2)}) collective-permute-start(bf16[2,3,128,128]{3,2,1,0:T(8,128)(2,1)S(1)} %get-tuple-element.175), channel_id=1, source_target_pairs={{0,24},{2,26},{4,28},{6,30},{8,16},{10,18},{12,20},{14,22},{16,8},... | collective-permute-start | bytes 589832 | tf_op jit(solution)/shard_map/return/ppermute | solution.py:568
  139.1 2.4 %collective-permute-start.33 = (bf16[2,3,128,128]{3,2,1,0:T(8,128)(2,1)S(1)}, bf16[2,3,128,128]{3,2,1,0:T(8,128)(2,1)S(1)}, u32[]{:S(2)}, u32[]{:S(2)}) collective-permute-start(bf16[2,3,128,128]{3,2,1,0:T(8,128)(2,1)S(1)} %get-tuple-element.177), channel_id=1, source_target_pairs={{0,30},{2,28},{4,26},{6,24},{8,22},{10,20},{12,18},{14,16},{16,14}... | collective-permute-start | bytes 589832 | tf_op jit(solution)/shard_map/return/ppermute | solution.py:568
  144.3 2.6 %collective-permute-done.33.refs_5_ = bf16[2,3,128,128]{3,2,1,0:T(8,128)(2,1)S(1)} collective-permute-done((bf16[2,3,128,128]{3,2,1,0:T(8,128)(2,1)S(1)}, bf16[2,3,128,128]{3,2,1,0:T(8,128)(2,1)S(1)}, u32[]{:S(2)}, u32[]{:S(2)}) %collective-permute-start.33) | collective-permute-done | bytes 196640 | tf_op jit(solution)/shard_map/return/ppermute | solution.py:568
  147.6 5.9 %all-to-all-start.1 = ((bf16[16,256,128]{2,1,0:T(8,128)(2,1)}), bf16[16,256,128]{2,1,0:T(8,128)(2,1)S(1)}, u32[]{:S(2)}, u32[]{:S(2)}) async-start(bf16[16,256,128]{2,1,0:T(8,128)(2,1)} %add_convert_fusion), calls=%async_computation.1 | async-start | bytes 2097152 | tf_op jit(solution)/shard_map/return/all_to_all | solution.py:573
  153.5 1.7 combine_last.1
  155.4 5.6 %hidden_grads.1 = bf16[1024,512]{1,0:T(8,128)(2,1)} custom-call(s32[1]{0:T(128)} %bitcast.3.core, bf16[8,1024,256]{2,1,0:T(8,128)(2,1)} %bitcast.41, bf16[8,256,256]{2,1,0:T(8,128)(2,1)S(1)} %all-to-all-done.mine, bf16[8,256,256]{2,1,0:T(8,128)(2,1)S(1)} %collective-permute-done.35.other), custom_call_target="tpu_custom_call" | custom-call | tf_op jit(solution)/shard_map/return/hidden_grads/pallas_call | solution.py:448
  161.0 5.1 %all-to-all-done.1.terms = bf16[16,256,128]{2,1,0:T(8,128)(2,1)S(1)} async-done(((bf16[16,256,128]{2,1,0:T(8,128)(2,1)}), bf16[16,256,128]{2,1,0:T(8,128)(2,1)S(1)}, u32[]{:S(2)}, u32[]{:S(2)}) %all-to-all-start.1) | async-done | bytes 1048608 | tf_op jit(solution)/shard_map/return/all_to_all | solution.py:573
  (128 shorter events, 53.6 us)
Async XLA Ops:
  11.7 10.7 %collective-permute-start.4 = (bf16[2,3,128,128]{3,2,1,0:T(8,128)(2,1)S(1)}, bf16[2,3,128,128]{3,2,1,0:T(8,128)(2,1)S(1)}, u32[]{:S(2)}, u32[]{:S(2)}) collective-permute-start(bf16[2,3,128,128]{3,2,1,0:T(8,128)(2,1)S(1)} %pad_maximum_fusion.1.refs_0_), channel_id=1, source_target_pairs={{0,2},{2,0},{4,6},{6,4},{8,10},{10,8},{12,14},{14,12},{16,18},{18,... | collective-permute-start | bytes 589832 | tf_op jit(solution)/shard_map/gather/ppermute | solution.py:498
  13.2 9.9 %collective-permute-start.2 = (bf16[2,3,128,128]{3,2,1,0:T(8,128)(2,1)S(1)}, bf16[2,3,128,128]{3,2,1,0:T(8,128)(2,1)S(1)}, u32[]{:S(2)}, u32[]{:S(2)}) collective-permute-start(bf16[2,3,128,128]{3,2,1,0:T(8,128)(2,1)S(1)} %pad_maximum_fusion.1.refs_0_), channel_id=1, source_target_pairs={{0,8},{2,10},{4,12},{6,14},{8,0},{10,2},{12,4},{14,6},{16,24},{18,... | collective-permute-start | bytes 589832 | tf_op jit(solution)/shard_map/gather/ppermute | solution.py:498
  27.5 14.8 %collective-permute-start.8 = (bf16[12,128,128]{2,1,0:T(8,128)(2,1)S(1)}, bf16[12,128,128]{2,1,0:T(8,128)(2,1)}, u32[]{:S(2)}, u32[]{:S(2)}) collective-permute-start(bf16[12,128,128]{2,1,0:T(8,128)(2,1)S(1)} %get-tuple-element.102.refs_0_), channel_id=1, source_target_pairs={{0,6},{2,4},{4,2},{6,0},{8,14},{10,12},{12,10},{14,8},{16,22},{18,... | collective-permute-start | bytes 1179656 | tf_op jit(solution)/shard_map/gather/ppermute | solution.py:495
  28.6 13.6 %collective-permute-start.9 = (bf16[12,128,128]{2,1,0:T(8,128)(2,1)S(1)}, bf16[12,128,128]{2,1,0:T(8,128)(2,1)}, u32[]{:S(2)}, u32[]{:S(2)}) collective-permute-start(bf16[12,128,128]{2,1,0:T(8,128)(2,1)S(1)} %get-tuple-element.103.refs_1_), channel_id=1, source_target_pairs={{0,24},{2,26},{4,28},{6,30},{8,16},{10,18},{12,20},{14,22},{16,8},... | collective-permute-start | bytes 1179656 | tf_op jit(solution)/shard_map/gather/ppermute | solution.py:495
  31.1 11.2 %collective-permute-start.10 = (bf16[12,128,128]{2,1,0:T(8,128)(2,1)S(1)}, bf16[12,128,128]{2,1,0:T(8,128)(2,1)}, u32[]{:S(2)}, u32[]{:S(2)}) collective-permute-start(bf16[12,128,128]{2,1,0:T(8,128)(2,1)S(1)} %get-tuple-element.104.refs_2_), channel_id=1, source_target_pairs={{0,2},{2,0},{4,6},{6,4},{8,10},{10,8},{12,14},{14,12},{16,18},{18,... | collective-permute-start | bytes 1179656 | tf_op jit(solution)/shard_map/gather/ppermute | solution.py:495
  34.0 9.9 %collective-permute-start.11 = (bf16[12,128,128]{2,1,0:T(8,128)(2,1)}, bf16[12,128,128]{2,1,0:T(8,128)(2,1)}, u32[]{:S(2)}, u32[]{:S(2)}) collective-permute-start(bf16[12,128,128]{2,1,0:T(8,128)(2,1)} %get-tuple-element.105.refs_3_), channel_id=1, source_target_pairs={{0,8},{2,10},{4,12},{6,14},{8,0},{10,2},{12,4},{14,6},{16,24},{18,... | collective-permute-start | bytes 1179656 | tf_op jit(solution)/shard_map/gather/ppermute | solution.py:495
  34.8 27.1 %collective-permute-start = (s32[48]{0:T(128)}, s32[48]{0:T(128)S(1)}, u32[]{:S(2)}, u32[]{:S(2)}) collective-permute-start(s32[48]{0:T(128)} %pad_add_fusion.1), channel_id=1, source_target_pairs={{0,1},{1,0},{2,3},{3,2},{4,5},{5,4},{6,7},{7,6},{8,9},{9,8},{10,11... | collective-permute-start | bytes 584 | tf_op jit(solution)/shard_map/slots/ppermute | solution.py:62
  49.0 19.7 %collective-permute-start.12 = (bf16[24,128,128]{2,1,0:T(8,128)(2,1)S(1)}, bf16[24,128,128]{2,1,0:T(8,128)(2,1)}, u32[]{:S(2)}, u32[]{:S(2)}) collective-permute-start(bf16[24,128,128]{2,1,0:T(8,128)(2,1)S(1)} %get-tuple-element.106.refs_0_), channel_id=1, source_target_pairs={{0,24},{2,26},{4,28},{6,30},{8,16},{10,18},{12,20},{14,22},{16,8},... | collective-permute-start | bytes 2359304 | tf_op jit(solution)/shard_map/gather/ppermute | solution.py:495
  50.6 18.1 %collective-permute-start.13 = (bf16[24,128,128]{2,1,0:T(8,128)(2,1)}, bf16[24,128,128]{2,1,0:T(8,128)(2,1)}, u32[]{:S(2)}, u32[]{:S(2)}) collective-permute-start(bf16[24,128,128]{2,1,0:T(8,128)(2,1)} %get-tuple-element.107.refs_2_), channel_id=1, source_target_pairs={{0,6},{2,4},{4,2},{6,0},{8,14},{10,12},{12,10},{14,8},{16,22},{18,... | collective-permute-start | bytes 2359304 | tf_op jit(solution)/shard_map/gather/ppermute | solution.py:495
  51.9 17.6 %collective-permute-start.14 = (bf16[24,128,128]{2,1,0:T(8,128)(2,1)}, bf16[24,128,128]{2,1,0:T(8,128)(2,1)}, u32[]{:S(2)}, u32[]{:S(2)}) collective-permute-start(bf16[24,128,128]{2,1,0:T(8,128)(2,1)} %get-tuple-element.108.refs_4_), channel_id=1, source_target_pairs={{0,8},{2,10},{4,12},{6,14},{8,0},{10,2},{12,4},{14,6},{16,24},{18,... | collective-permute-start | bytes 2359304 | tf_op jit(solution)/shard_map/gather/ppermute | solution.py:495
  52.0 18.7 %collective-permute-start.15 = (bf16[24,128,128]{2,1,0:T(8,128)(2,1)}, bf16[24,128,128]{2,1,0:T(8,128)(2,1)}, u32[]{:S(2)}, u32[]{:S(2)}) collective-permute-start(bf16[24,128,128]{2,1,0:T(8,128)(2,1)} %get-tuple-element.109.refs_6_), channel_id=1, source_target_pairs={{0,2},{2,0},{4,6},{6,4},{8,10},{10,8},{12,14},{14,12},{16,18},{18,... | collective-permute-start | bytes 2359304 | tf_op jit(solution)/shard_map/gather/ppermute | solution.py:495
  53.9 37.5 %all-to-all-start = ((bf16[8,256,256]{2,1,0:T(8,128)(2,1)}), bf16[8,256,256]{2,1,0:T(8,128)(2,1)S(1)}, u32[]{:S(2)}, u32[]{:S(2)}) async-start(bf16[8,256,256]{2,1,0:T(8,128)(2,1)} %fusion.1), calls=%async_computation | async-start | bytes 2097152 | tf_op jit(solution)/shard_map/weight_rows/all_to_all | solution.py:519
  61.6 93.8 %all-gather.3.cloned.1.call-start = ((), (), s32[]{:S(2)}) async-start(), calls=%async_computation.2 | async-start | bytes 4718592 | tf_op jit(solution)/shard_map/grad_queries/all_gather | solution.py:554
  91.5 21.1 %collective-permute-start.19 = (bf16[24,128,128]{2,1,0:T(8,128)(2,1)}, bf16[24,128,128]{2,1,0:T(8,128)(2,1)S(1)}, u32[]{:S(2)}, u32[]{:S(2)}) collective-permute-start(bf16[24,128,128]{2,1,0:T(8,128)(2,1)} %get-tuple-element.127), channel_id=1, source_target_pairs={{0,24},{2,26},{4,28},{6,30},{8,16},{10,18},{12,20},{14,22},{16,8},... | collective-permute-start | bytes 2359304 | tf_op jit(solution)/shard_map/return/ppermute | solution.py:66
  93.0 19.6 %collective-permute-start.20 = (bf16[24,128,128]{2,1,0:T(8,128)(2,1)}, bf16[24,128,128]{2,1,0:T(8,128)(2,1)S(1)}, u32[]{:S(2)}, u32[]{:S(2)}) collective-permute-start(bf16[24,128,128]{2,1,0:T(8,128)(2,1)} %get-tuple-element.128), channel_id=1, source_target_pairs={{0,6},{2,4},{4,2},{6,0},{8,14},{10,12},{12,10},{14,8},{16,22},{18,... | collective-permute-start | bytes 2359304 | tf_op jit(solution)/shard_map/return/ppermute | solution.py:66
  94.5 19.2 %collective-permute-start.21 = (bf16[24,128,128]{2,1,0:T(8,128)(2,1)}, bf16[24,128,128]{2,1,0:T(8,128)(2,1)S(1)}, u32[]{:S(2)}, u32[]{:S(2)}) collective-permute-start(bf16[24,128,128]{2,1,0:T(8,128)(2,1)} %get-tuple-element.129), channel_id=1, source_target_pairs={{0,8},{2,10},{4,12},{6,14},{8,0},{10,2},{12,4},{14,6},{16,24},{18,... | collective-permute-start | bytes 2359304 | tf_op jit(solution)/shard_map/return/ppermute | solution.py:66
  94.5 19.2 %collective-permute-start.22 = (bf16[24,128,128]{2,1,0:T(8,128)(2,1)S(1)}, bf16[24,128,128]{2,1,0:T(8,128)(2,1)S(1)}, u32[]{:S(2)}, u32[]{:S(2)}) collective-permute-start(bf16[24,128,128]{2,1,0:T(8,128)(2,1)S(1)} %copy-done.17), channel_id=1, source_target_pairs={{0,2},{2,0},{4,6},{6,4},{8,10},{10,8},{12,14},{14,12},{16,18},{18,... | collective-permute-start | bytes 2359304 | tf_op jit(solution)/shard_map/return/ppermute | solution.py:66
  115.3 11.5 %collective-permute-start.23 = (bf16[12,128,128]{2,1,0:T(8,128)(2,1)S(1)}, bf16[12,128,128]{2,1,0:T(8,128)(2,1)S(1)}, u32[]{:S(2)}, u32[]{:S(2)}) collective-permute-start(bf16[12,128,128]{2,1,0:T(8,128)(2,1)S(1)} %get-tuple-element.150), channel_id=1, source_target_pairs={{0,6},{2,4},{4,2},{6,0},{8,14},{10,12},{12,10},{14,8},{16,22},{18,... | collective-permute-start | bytes 1179656 | tf_op jit(solution)/shard_map/return/ppermute | solution.py:66
  115.9 12.4 %collective-permute-start.24 = (bf16[12,128,128]{2,1,0:T(8,128)(2,1)S(1)}, bf16[12,128,128]{2,1,0:T(8,128)(2,1)S(1)}, u32[]{:S(2)}, u32[]{:S(2)}) collective-permute-start(bf16[12,128,128]{2,1,0:T(8,128)(2,1)S(1)} %get-tuple-element.151), channel_id=1, source_target_pairs={{0,24},{2,26},{4,28},{6,30},{8,16},{10,18},{12,20},{14,22},{16,8},... | collective-permute-start | bytes 1179656 | tf_op jit(solution)/shard_map/return/ppermute | solution.py:66
  117.8 11.0 %collective-permute-start.25 = (bf16[12,128,128]{2,1,0:T(8,128)(2,1)S(1)}, bf16[12,128,128]{2,1,0:T(8,128)(2,1)S(1)}, u32[]{:S(2)}, u32[]{:S(2)}) collective-permute-start(bf16[12,128,128]{2,1,0:T(8,128)(2,1)S(1)} %get-tuple-element.152), channel_id=1, source_target_pairs={{0,2},{2,0},{4,6},{6,4},{8,10},{10,8},{12,14},{14,12},{16,18},{18,... | collective-permute-start | bytes 1179656 | tf_op jit(solution)/shard_map/return/ppermute | solution.py:66
  119.6 10.6 %collective-permute-start.26 = (bf16[12,128,128]{2,1,0:T(8,128)(2,1)S(1)}, bf16[12,128,128]{2,1,0:T(8,128)(2,1)S(1)}, u32[]{:S(2)}, u32[]{:S(2)}) collective-permute-start(bf16[12,128,128]{2,1,0:T(8,128)(2,1)S(1)} %get-tuple-element.153), channel_id=1, source_target_pairs={{0,8},{2,10},{4,12},{6,14},{8,0},{10,2},{12,4},{14,6},{16,24},{18,... | collective-permute-start | bytes 1179656 | tf_op jit(solution)/shard_map/return/ppermute | solution.py:66
  132.4 9.9 %collective-permute-start.29 = (bf16[2,3,128,128]{3,2,1,0:T(8,128)(2,1)S(1)}, bf16[2,3,128,128]{3,2,1,0:T(8,128)(2,1)}, u32[]{:S(2)}, u32[]{:S(2)}) collective-permute-start(bf16[2,3,128,128]{3,2,1,0:T(8,128)(2,1)S(1)} %get-tuple-element.173), channel_id=1, source_target_pairs={{0,2},{2,0},{4,6},{6,4},{8,10},{10,8},{12,14},{14,12},{16,18},{18,... | collective-permute-start | bytes 589832 | tf_op jit(solution)/shard_map/return/ppermute | solution.py:568
  142.3 13.0 %collective-permute-start.35 = (bf16[8,256,256]{2,1,0:T(8,128)(2,1)S(1)}, bf16[8,256,256]{2,1,0:T(8,128)(2,1)S(1)}, u32[]{:S(2)}, u32[]{:S(2)}) collective-permute-start(bf16[8,256,256]{2,1,0:T(8,128)(2,1)S(1)} %all-to-all-done.mine), channel_id=1, source_target_pairs={{0,1},{1,0},{2,3},{3,2},{4,5},{5,4},{6,7},{7,6},{8,9},{9,8},{10,11... | collective-permute-start | bytes 3145736 | tf_op jit(solution)/shard_map/grad_queries/ppermute | solution.py:62
  147.6 18.6 %all-to-all-start.1 = ((bf16[16,256,128]{2,1,0:T(8,128)(2,1)}), bf16[16,256,128]{2,1,0:T(8,128)(2,1)S(1)}, u32[]{:S(2)}, u32[]{:S(2)}) async-start(bf16[16,256,128]{2,1,0:T(8,128)(2,1)} %add_convert_fusion), calls=%async_computation.1 | async-start | bytes 2097152 | tf_op jit(solution)/shard_map/return/all_to_all | solution.py:573
  (34 other events, 286.2 us)
Sparse Core Ops, SparseCore 0:
  91.6 55.0 all-gather.2

commit v5 on v4

--- a/solution.py
+++ b/solution.py
@@ -14,6 +14,7 @@
 F32 = jnp.float32
 BF16 = jnp.bfloat16
 MIB = 2**20
+PARTS = 4
 
 
 def chip_pairs(move):
@@ -294,7 +295,10 @@
     cols = (((0,), (0,)), ((), ()))
 
     def step(i, carry):
-        batch = [(q_own, g_own, i, i), (q_sib, g_sib, i, i + spans)]
+        batch = []
+        for part in range(PARTS):
+            at = i + part * (spans // PARTS)
+            batch += [(q_own, g_own, at, at), (q_sib, g_sib, at, at + spans)]
         q = [qr[n] for qr, _, n, _ in batch]
         g = [gr[n] for _, gr, n, _ in batch]
         refs = [(2 * span, 2 * span + 1) for _, _, _, span in batch]
@@ -318,10 +322,12 @@
         gq = [(jnp.dot(a, b, preferred_element_type=F32) * scale).astype(BF16) for a, b in zip(gs, k)]
         dk = [lax.dot_general(a, b, cols, preferred_element_type=F32).astype(BF16) for a, b in zip(gs, q)]
         dv = [lax.dot_general(a, b, cols, preferred_element_type=F32).astype(BF16) for a, b in zip(low, g)]
-        ctx_own[i] = ctx[0]
-        gq_own[i] = gq[0]
-        pair_sib[0, i] = ctx[1]
-        pair_sib[1, i] = gq[1]
+        for n in range(0, len(batch), 2):
+            at = batch[n][2]
+            ctx_own[at] = ctx[n]
+            gq_own[at] = gq[n]
+            pair_sib[0, at] = ctx[n + 1]
+            pair_sib[1, at] = gq[n + 1]
         for n, pair in enumerate(refs):
             for j, r in enumerate(pair):
                 at = slots[2, r]
@@ -332,7 +338,7 @@
                 dv_all[at] = (dv_all[at].astype(F32) + part).astype(BF16)
         return carry
 
-    lax.fori_loop(0, spans, step, 0, unroll=2)
+    lax.fori_loop(0, spans // PARTS, step, 0)
     stores = []
     for s in range(4):
         whole = dk_all if s < 2 else dv_all

time: 177 us -> 175 us (0.989)
  Pallas kernels: 47 us -> 41.5 us
  waiting for transfers between devices: 47.5 us -> 50.5 us
    pallas_call x1, Pallas kernels: 16.2 us -> 10.7 us  [attention(): pl.pallas_call(attention_body, out_shape=[small, small, pair] + large, in...]
    all_to_all x1, waiting for transfers between devices: 0.01 us -> 3.01 us  [per_device(): lax.all_to_all(asked, 'grp', split_axis=0, concat_axis=0, tiled=True)]
  transfers between devices with their start and end apart: 39 -> 39, of which waited for: 23 -> 25; matrix products, arithmetic and copies ran while one was open for 3% -> 3% of each run, Pallas kernels for 26% -> 23%
where the time goes in v5:
time: 175 us; the launch traced here: 174 us
  starting transfers between devices  54.2 us (31%)
  waiting for transfers between devices  50.5 us (29%)
  Pallas kernels  41.5 us (24%)
  between operations  14.4 us (8%)
  other arithmetic  7.49 us (4%)
  local copies, waits for them, and re-layouts  5.99 us (3%)
    ppermute x8, waiting for transfers between devices, send(): lax.ppermute(h, 'chip', LINKS[ORDERS[s][k]])  14.6 us
    ppermute x8, starting transfers between devices, send(): lax.ppermute(h, 'chip', LINKS[ORDERS[s][k]])  11 us
    pallas_call x1, Pallas kernels, attention(): pl.pallas_call(attention_body, out_shape=[small, small, pair] + large, in...  10.7 us
    ppermute x6, starting transfers between devices, per_device(): lax.ppermute(pairs[pair], 'chip', square_pairs(pair, m))  10.6 us
    ppermute x8, starting transfers between devices, across(): lax.ppermute(p, 'chip', LINKS[ORDERS[s][k]])  10.3 us
    ppermute x8, waiting for transfers between devices, across(): lax.ppermute(p, 'chip', LINKS[ORDERS[s][k]])  10.2 us
    ppermute x6, starting transfers between devices, per_device(): lax.ppermute(square[3 * pair + m], 'chip', square_pairs(pair, m + 1))  8.4 us
    pallas_call x1, Pallas kernels, weight_terms(): pl.pallas_call(weight_body, out_shape=[jax.ShapeDtypeStruct((CHIPS, head_...  7.85 us
  transfers between devices with their start and end apart: 39, of which 25 were waited for; matrix products, arithmetic and copies ran while one was open for 3% of the time, Pallas kernels for 23%

profile of v5, /device:TPU:8, one launch (start us, length us, event | category | flops | bytes accessed | tf_op | source)
XLA Modules:
  0.0 174.1 jit_solution(7956702958866574372)
XLA Ops:
  13.9 3.6 %collective-permute-start.7 = (bf16[2,3,128,128]{3,2,1,0:T(8,128)(2,1)S(1)}, bf16[2,3,128,128]{3,2,1,0:T(8,128)(2,1)S(1)}, u32[]{:S(2)}, u32[]{:S(2)}) collective-permute-start(bf16[2,3,128,128]{3,2,1,0:T(8,128)(2,1)S(1)} %pad_maximum_fusion.2.refs_1_), channel_id=1, source_target_pairs={{0,30},{2,28},{4,26},{6,24},{8,22},{10,20},{12,18},{14,16},{16,14}... | collective-permute-start | bytes 589832 | tf_op jit(solution)/shard_map/gather/ppermute | solution.py:504
  19.0 2.8 %collective-permute-start.3 = (bf16[2,3,128,128]{3,2,1,0:T(8,128)(2,1)S(1)}, bf16[2,3,128,128]{3,2,1,0:T(8,128)(2,1)S(1)}, u32[]{:S(2)}, u32[]{:S(2)}) collective-permute-start(bf16[2,3,128,128]{3,2,1,0:T(8,128)(2,1)S(1)} %pad_maximum_fusion.2.refs_1_), channel_id=1, source_target_pairs={{0,24},{2,26},{4,28},{6,30},{8,16},{10,18},{12,20},{14,22},{16,8},... | collective-permute-start | bytes 589832 | tf_op jit(solution)/shard_map/gather/ppermute | solution.py:504
  23.1 3.5 %collective-permute-done.5.refs_5_ = bf16[2,3,128,128]{3,2,1,0:T(8,128)(2,1)S(1)} collective-permute-done((bf16[2,3,128,128]{3,2,1,0:T(8,128)(2,1)S(1)}, bf16[2,3,128,128]{3,2,1,0:T(8,128)(2,1)S(1)}, u32[]{:S(2)}, u32[]{:S(2)}) %collective-permute-start.5) | collective-permute-done | bytes 196640 | tf_op jit(solution)/shard_map/gather/ppermute | solution.py:504
  28.6 2.4 %collective-permute-start.9 = (bf16[12,128,128]{2,1,0:T(8,128)(2,1)S(1)}, bf16[12,128,128]{2,1,0:T(8,128)(2,1)}, u32[]{:S(2)}, u32[]{:S(2)}) collective-permute-start(bf16[12,128,128]{2,1,0:T(8,128)(2,1)S(1)} %get-tuple-element.103.refs_1_), channel_id=1, source_target_pairs={{0,24},{2,26},{4,28},{6,30},{8,16},{10,18},{12,20},{14,22},{16,8},... | collective-permute-start | bytes 1179656 | tf_op jit(solution)/shard_map/gather/ppermute | solution.py:501
  31.1 2.9 %collective-permute-start.10 = (bf16[12,128,128]{2,1,0:T(8,128)(2,1)S(1)}, bf16[12,128,128]{2,1,0:T(8,128)(2,1)}, u32[]{:S(2)}, u32[]{:S(2)}) collective-permute-start(bf16[12,128,128]{2,1,0:T(8,128)(2,1)S(1)} %get-tuple-element.104.refs_2_), channel_id=1, source_target_pairs={{0,2},{2,0},{4,6},{6,4},{8,10},{10,8},{12,14},{14,12},{16,18},{18,... | collective-permute-start | bytes 1179656 | tf_op jit(solution)/shard_map/gather/ppermute | solution.py:501
  34.8 7.5 %project.1 = (bf16[1024,128]{1,0:T(8,128)(2,1)S(1)}, bf16[1024,128]{1,0:T(8,128)(2,1)S(1)}) custom-call(s32[1]{0:T(128)} %bitcast.3.core, bf16[1024,4096]{1,0:T(8,128)(2,1)} %bitcast.39, bf16[4096,256]{1,0:T(8,128)(2,1)S(1)} %copy-done), custom_call_target="tpu_custom_call" | custom-call | tf_op jit(solution)/shard_map/queries/project/pallas_call | solution.py:239
  45.9 3.1 %join_halves.1 = (bf16[24,128,128]{2,1,0:T(8,128)(2,1)S(1)}, bf16[24,128,128]{2,1,0:T(8,128)(2,1)}, bf16[24,128,128]{2,1,0:T(8,128)(2,1)}, bf16[24,128,128]{2,1,0:T(8,128)(2,1)}) custom-call(bf16[12,128,128]{2,1,0:T(8,128)(2,1)S(1)} %get-tuple-element.102.refs_0_, bf16[12,128,128]{2,1,0:T(8,128)(2,1)S(1)} %copy-done.5, bf16[12,128,128]{2,1,0:T(8,128)(2,1)S(1)} %copy-done.7, ...), custom_call_target="tpu_custom_call" | custom-call | tf_op jit(solution)/shard_map/gather/join_halves/pallas_call | solution.py:99
  53.9 7.7 %all-to-all-start = ((bf16[8,256,256]{2,1,0:T(8,128)(2,1)}), bf16[8,256,256]{2,1,0:T(8,128)(2,1)S(1)}, u32[]{:S(2)}, u32[]{:S(2)}) async-start(bf16[8,256,256]{2,1,0:T(8,128)(2,1)} %fusion.1), calls=%async_computation | async-start | bytes 2097152 | tf_op jit(solution)/shard_map/weight_rows/all_to_all | solution.py:525
  62.1 6.7 %collective-permute-done.12.refs_1_ = bf16[24,128,128]{2,1,0:T(8,128)(2,1)} collective-permute-done((bf16[24,128,128]{2,1,0:T(8,128)(2,1)S(1)}, bf16[24,128,128]{2,1,0:T(8,128)(2,1)}, u32[]{:S(2)}, u32[]{:S(2)}) %collective-permute-start.12) | collective-permute-done | bytes 786464 | tf_op jit(solution)/shard_map/gather/ppermute | solution.py:501
  72.2 10.7 %attention.1 = (bf16[16,64,128]{2,1,0:T(8,128)(2,1)S(1)}, bf16[16,64,128]{2,1,0:T(8,128)(2,1)S(1)}, bf16[2,16,64,128]{3,2,1,0:T(8,128)(2,1)S(1)}, bf16[12,128,12...) custom-call(s32[4,64]{1,0:T(4,128)S(1)} %pad_add_fusion.slots, ...), custom_call_target="tpu_custom_call" | custom-call | tf_op jit(solution)/shard_map/attend/attention/pallas_call | solution.py:370
  85.9 3.0 %all-to-all-done.mine = bf16[8,256,256]{2,1,0:T(8,128)(2,1)S(1)} async-done(((bf16[8,256,256]{2,1,0:T(8,128)(2,1)}), bf16[8,256,256]{2,1,0:T(8,128)(2,1)S(1)}, u32[]{:S(2)}, u32[]{:S(2)}) %all-to-all-start) | async-done | bytes 1048608 | tf_op jit(solution)/shard_map/weight_rows/all_to_all | solution.py:525
  89.0 2.3 %collective-permute-start.19 = (bf16[24,128,128]{2,1,0:T(8,128)(2,1)}, bf16[24,128,128]{2,1,0:T(8,128)(2,1)S(1)}, u32[]{:S(2)}, u32[]{:S(2)}) collective-permute-start(bf16[24,128,128]{2,1,0:T(8,128)(2,1)} %get-tuple-element.127), channel_id=1, source_target_pairs={{0,24},{2,26},{4,28},{6,30},{8,16},{10,18},{12,20},{14,22},{16,8},... | collective-permute-start | bytes 2359304 | tf_op jit(solution)/shard_map/return/ppermute | solution.py:67
  94.9 7.9 %weight_terms.1 = (bf16[16,256,128]{2,1,0:T(8,128)(2,1)S(1)}, bf16[16,256,128]{2,1,0:T(8,128)(2,1)S(1)}) custom-call(s32[1]{0:T(128)} %bitcast.3.core, bf16[1024,256]{1,0:T(8,128)(2,1)S(1)} %copy-done.1, bf16[1024,4096]{1,0:T(8,128)(2,1)} %bitcast.40), custom_call_target="tpu_custom_call" | custom-call | tf_op jit(solution)/shard_map/return/weight_terms/pallas_call | solution.py:418
  103.7 5.5 %collective-permute-done.19.refs_4_ = bf16[24,128,128]{2,1,0:T(8,128)(2,1)S(1)} collective-permute-done((bf16[24,128,128]{2,1,0:T(8,128)(2,1)}, bf16[24,128,128]{2,1,0:T(8,128)(2,1)S(1)}, u32[]{:S(2)}, u32[]{:S(2)}) %collective-permute-start.19) | collective-permute-done | bytes 786464 | tf_op jit(solution)/shard_map/return/ppermute | solution.py:67
  115.2 3.0 %collective-permute-start.25 = (bf16[12,128,128]{2,1,0:T(8,128)(2,1)S(1)}, bf16[12,128,128]{2,1,0:T(8,128)(2,1)S(1)}, u32[]{:S(2)}, u32[]{:S(2)}) collective-permute-start(bf16[12,128,128]{2,1,0:T(8,128)(2,1)S(1)} %get-tuple-element.152), channel_id=1, source_target_pairs={{0,2},{2,0},{4,6},{6,4},{8,10},{10,8},{12,14},{14,12},{16,18},{18,... | collective-permute-start | bytes 1179656 | tf_op jit(solution)/shard_map/return/ppermute | solution.py:67
  121.5 2.6 %collective-permute-done.23.refs_4_ = bf16[12,128,128]{2,1,0:T(8,128)(2,1)S(1)} collective-permute-done((bf16[12,128,128]{2,1,0:T(8,128)(2,1)S(1)}, bf16[12,128,128]{2,1,0:T(8,128)(2,1)S(1)}, u32[]{:S(2)}, u32[]{:S(2)}) %collective-permute-start.23) | collective-permute-done | bytes 393248 | tf_op jit(solution)/shard_map/return/ppermute | solution.py:67
  124.1 2.5 %collective-permute-done.24.refs_5_ = bf16[12,128,128]{2,1,0:T(8,128)(2,1)S(1)} collective-permute-done((bf16[12,128,128]{2,1,0:T(8,128)(2,1)S(1)}, bf16[12,128,128]{2,1,0:T(8,128)(2,1)S(1)}, u32[]{:S(2)}, u32[]{:S(2)}) %collective-permute-start.24) | collective-permute-done | bytes 393248 | tf_op jit(solution)/shard_map/return/ppermute | solution.py:67
  130.8 2.7 %collective-permute-start.30 = (bf16[2,3,128,128]{3,2,1,0:T(8,128)(2,1)S(1)}, bf16[2,3,128,128]{3,2,1,0:T(8,128)(2,1)S(1)}, u32[]{:S(2)}, u32[]{:S(2)}) collective-permute-start(bf16[2,3,128,128]{3,2,1,0:T(8,128)(2,1)S(1)} %get-tuple-element.174), channel_id=1, source_target_pairs={{0,10},{2,8},{4,14},{6,12},{8,2},{10,0},{12,6},{14,4},{16,26},{18,... | collective-permute-start | bytes 589832 | tf_op jit(solution)/shard_map/return/ppermute | solution.py:574
  133.5 1.9 %collective-permute-start.31 = (bf16[2,3,128,128]{3,2,1,0:T(8,128)(2,1)S(1)}, bf16[2,3,128,128]{3,2,1,0:T(8,128)(2,1)S(1)}, u32[]{:S(2)}, u32[]{:S(2)}) collective-permute-start(bf16[2,3,128,128]{3,2,1,0:T(8,128)(2,1)S(1)} %get-tuple-element.175), channel_id=1, source_target_pairs={{0,24},{2,26},{4,28},{6,30},{8,16},{10,18},{12,20},{14,22},{16,8},... | collective-permute-start | bytes 589832 | tf_op jit(solution)/shard_map/return/ppermute | solution.py:574
  137.7 2.2 %collective-permute-start.33 = (bf16[2,3,128,128]{3,2,1,0:T(8,128)(2,1)S(1)}, bf16[2,3,128,128]{3,2,1,0:T(8,128)(2,1)S(1)}, u32[]{:S(2)}, u32[]{:S(2)}) collective-permute-start(bf16[2,3,128,128]{3,2,1,0:T(8,128)(2,1)S(1)} %get-tuple-element.177), channel_id=1, source_target_pairs={{0,30},{2,28},{4,26},{6,24},{8,22},{10,20},{12,18},{14,16},{16,14}... | collective-permute-start | bytes 589832 | tf_op jit(solution)/shard_map/return/ppermute | solution.py:574
  142.7 2.8 %collective-permute-done.33.refs_5_ = bf16[2,3,128,128]{3,2,1,0:T(8,128)(2,1)S(1)} collective-permute-done((bf16[2,3,128,128]{3,2,1,0:T(8,128)(2,1)S(1)}, bf16[2,3,128,128]{3,2,1,0:T(8,128)(2,1)S(1)}, u32[]{:S(2)}, u32[]{:S(2)}) %collective-permute-start.33) | collective-permute-done | bytes 196640 | tf_op jit(solution)/shard_map/return/ppermute | solution.py:574
  146.2 5.7 %all-to-all-start.1 = ((bf16[16,256,128]{2,1,0:T(8,128)(2,1)}), bf16[16,256,128]{2,1,0:T(8,128)(2,1)S(1)}, u32[]{:S(2)}, u32[]{:S(2)}) async-start(bf16[16,256,128]{2,1,0:T(8,128)(2,1)} %add_convert_fusion), calls=%async_computation.1 | async-start | bytes 2097152 | tf_op jit(solution)/shard_map/return/all_to_all | solution.py:579
  153.8 5.6 %hidden_grads.1 = bf16[1024,512]{1,0:T(8,128)(2,1)} custom-call(s32[1]{0:T(128)} %bitcast.3.core, bf16[8,1024,256]{2,1,0:T(8,128)(2,1)} %bitcast.41, bf16[8,256,256]{2,1,0:T(8,128)(2,1)S(1)} %all-to-all-done.mine, bf16[8,256,256]{2,1,0:T(8,128)(2,1)S(1)} %collective-permute-done.35.other), custom_call_target="tpu_custom_call" | custom-call | tf_op jit(solution)/shard_map/return/hidden_grads/pallas_call | solution.py:454
  159.4 5.2 %all-to-all-done.1.terms = bf16[16,256,128]{2,1,0:T(8,128)(2,1)S(1)} async-done(((bf16[16,256,128]{2,1,0:T(8,128)(2,1)}), bf16[16,256,128]{2,1,0:T(8,128)(2,1)S(1)}, u32[]{:S(2)}, u32[]{:S(2)}) %all-to-all-start.1) | async-done | bytes 1048608 | tf_op jit(solution)/shard_map/return/all_to_all | solution.py:579
  (128 shorter events, 56.0 us)
Async XLA Ops:
  11.7 10.7 %collective-permute-start.4 = (bf16[2,3,128,128]{3,2,1,0:T(8,128)(2,1)S(1)}, bf16[2,3,128,128]{3,2,1,0:T(8,128)(2,1)S(1)}, u32[]{:S(2)}, u32[]{:S(2)}) collective-permute-start(bf16[2,3,128,128]{3,2,1,0:T(8,128)(2,1)S(1)} %pad_maximum_fusion.1.refs_0_), channel_id=1, source_target_pairs={{0,2},{2,0},{4,6},{6,4},{8,10},{10,8},{12,14},{14,12},{16,18},{18,... | collective-permute-start | bytes 589832 | tf_op jit(solution)/shard_map/gather/ppermute | solution.py:504
  13.2 9.9 %collective-permute-start.2 = (bf16[2,3,128,128]{3,2,1,0:T(8,128)(2,1)S(1)}, bf16[2,3,128,128]{3,2,1,0:T(8,128)(2,1)S(1)}, u32[]{:S(2)}, u32[]{:S(2)}) collective-permute-start(bf16[2,3,128,128]{3,2,1,0:T(8,128)(2,1)S(1)} %pad_maximum_fusion.1.refs_0_), channel_id=1, source_target_pairs={{0,8},{2,10},{4,12},{6,14},{8,0},{10,2},{12,4},{14,6},{16,24},{18,... | collective-permute-start | bytes 589832 | tf_op jit(solution)/shard_map/gather/ppermute | solution.py:504
  27.5 14.8 %collective-permute-start.8 = (bf16[12,128,128]{2,1,0:T(8,128)(2,1)S(1)}, bf16[12,128,128]{2,1,0:T(8,128)(2,1)}, u32[]{:S(2)}, u32[]{:S(2)}) collective-permute-start(bf16[12,128,128]{2,1,0:T(8,128)(2,1)S(1)} %get-tuple-element.102.refs_0_), channel_id=1, source_target_pairs={{0,6},{2,4},{4,2},{6,0},{8,14},{10,12},{12,10},{14,8},{16,22},{18,... | collective-permute-start | bytes 1179656 | tf_op jit(solution)/shard_map/gather/ppermute | solution.py:501
  28.6 13.6 %collective-permute-start.9 = (bf16[12,128,128]{2,1,0:T(8,128)(2,1)S(1)}, bf16[12,128,128]{2,1,0:T(8,128)(2,1)}, u32[]{:S(2)}, u32[]{:S(2)}) collective-permute-start(bf16[12,128,128]{2,1,0:T(8,128)(2,1)S(1)} %get-tuple-element.103.refs_1_), channel_id=1, source_target_pairs={{0,24},{2,26},{4,28},{6,30},{8,16},{10,18},{12,20},{14,22},{16,8},... | collective-permute-start | bytes 1179656 | tf_op jit(solution)/shard_map/gather/ppermute | solution.py:501
  31.1 11.2 %collective-permute-start.10 = (bf16[12,128,128]{2,1,0:T(8,128)(2,1)S(1)}, bf16[12,128,128]{2,1,0:T(8,128)(2,1)}, u32[]{:S(2)}, u32[]{:S(2)}) collective-permute-start(bf16[12,128,128]{2,1,0:T(8,128)(2,1)S(1)} %get-tuple-element.104.refs_2_), channel_id=1, source_target_pairs={{0,2},{2,0},{4,6},{6,4},{8,10},{10,8},{12,14},{14,12},{16,18},{18,... | collective-permute-start | bytes 1179656 | tf_op jit(solution)/shard_map/gather/ppermute | solution.py:501
  34.0 9.9 %collective-permute-start.11 = (bf16[12,128,128]{2,1,0:T(8,128)(2,1)}, bf16[12,128,128]{2,1,0:T(8,128)(2,1)}, u32[]{:S(2)}, u32[]{:S(2)}) collective-permute-start(bf16[12,128,128]{2,1,0:T(8,128)(2,1)} %get-tuple-element.105.refs_3_), channel_id=1, source_target_pairs={{0,8},{2,10},{4,12},{6,14},{8,0},{10,2},{12,4},{14,6},{16,24},{18,... | collective-permute-start | bytes 1179656 | tf_op jit(solution)/shard_map/gather/ppermute | solution.py:501
  34.8 27.1 %collective-permute-start = (s32[48]{0:T(128)}, s32[48]{0:T(128)S(1)}, u32[]{:S(2)}, u32[]{:S(2)}) collective-permute-start(s32[48]{0:T(128)} %pad_add_fusion.1), channel_id=1, source_target_pairs={{0,1},{1,0},{2,3},{3,2},{4,5},{5,4},{6,7},{7,6},{8,9},{9,8},{10,11... | collective-permute-start | bytes 584 | tf_op jit(solution)/shard_map/slots/ppermute | solution.py:63
  49.0 19.7 %collective-permute-start.12 = (bf16[24,128,128]{2,1,0:T(8,128)(2,1)S(1)}, bf16[24,128,128]{2,1,0:T(8,128)(2,1)}, u32[]{:S(2)}, u32[]{:S(2)}) collective-permute-start(bf16[24,128,128]{2,1,0:T(8,128)(2,1)S(1)} %get-tuple-element.106.refs_0_), channel_id=1, source_target_pairs={{0,24},{2,26},{4,28},{6,30},{8,16},{10,18},{12,20},{14,22},{16,8},... | collective-permute-start | bytes 2359304 | tf_op jit(solution)/shard_map/gather/ppermute | solution.py:501
  50.6 18.1 %collective-permute-start.13 = (bf16[24,128,128]{2,1,0:T(8,128)(2,1)}, bf16[24,128,128]{2,1,0:T(8,128)(2,1)}, u32[]{:S(2)}, u32[]{:S(2)}) collective-permute-start(bf16[24,128,128]{2,1,0:T(8,128)(2,1)} %get-tuple-element.107.refs_2_), channel_id=1, source_target_pairs={{0,6},{2,4},{4,2},{6,0},{8,14},{10,12},{12,10},{14,8},{16,22},{18,... | collective-permute-start | bytes 2359304 | tf_op jit(solution)/shard_map/gather/ppermute | solution.py:501
  51.9 17.6 %collective-permute-start.14 = (bf16[24,128,128]{2,1,0:T(8,128)(2,1)}, bf16[24,128,128]{2,1,0:T(8,128)(2,1)}, u32[]{:S(2)}, u32[]{:S(2)}) collective-permute-start(bf16[24,128,128]{2,1,0:T(8,128)(2,1)} %get-tuple-element.108.refs_4_), channel_id=1, source_target_pairs={{0,8},{2,10},{4,12},{6,14},{8,0},{10,2},{12,4},{14,6},{16,24},{18,... | collective-permute-start | bytes 2359304 | tf_op jit(solution)/shard_map/gather/ppermute | solution.py:501
  52.0 18.7 %collective-permute-start.15 = (bf16[24,128,128]{2,1,0:T(8,128)(2,1)}, bf16[24,128,128]{2,1,0:T(8,128)(2,1)}, u32[]{:S(2)}, u32[]{:S(2)}) collective-permute-start(bf16[24,128,128]{2,1,0:T(8,128)(2,1)} %get-tuple-element.109.refs_6_), channel_id=1, source_target_pairs={{0,2},{2,0},{4,6},{6,4},{8,10},{10,8},{12,14},{14,12},{16,18},{18,... | collective-permute-start | bytes 2359304 | tf_op jit(solution)/shard_map/gather/ppermute | solution.py:501
  53.9 35.0 %all-to-all-start = ((bf16[8,256,256]{2,1,0:T(8,128)(2,1)}), bf16[8,256,256]{2,1,0:T(8,128)(2,1)S(1)}, u32[]{:S(2)}, u32[]{:S(2)}) async-start(bf16[8,256,256]{2,1,0:T(8,128)(2,1)} %fusion.1), calls=%async_computation | async-start | bytes 2097152 | tf_op jit(solution)/shard_map/weight_rows/all_to_all | solution.py:525
  61.6 92.2 %all-gather.3.cloned.1.call-start = ((), (), s32[]{:S(2)}) async-start(), calls=%async_computation.2 | async-start | bytes 4718592 | tf_op jit(solution)/shard_map/grad_queries/all_gather | solution.py:560
  89.0 20.3 %collective-permute-start.19 = (bf16[24,128,128]{2,1,0:T(8,128)(2,1)}, bf16[24,128,128]{2,1,0:T(8,128)(2,1)S(1)}, u32[]{:S(2)}, u32[]{:S(2)}) collective-permute-start(bf16[24,128,128]{2,1,0:T(8,128)(2,1)} %get-tuple-element.127), channel_id=1, source_target_pairs={{0,24},{2,26},{4,28},{6,30},{8,16},{10,18},{12,20},{14,22},{16,8},... | collective-permute-start | bytes 2359304 | tf_op jit(solution)/shard_map/return/ppermute | solution.py:67
  91.3 19.4 %collective-permute-start.20 = (bf16[24,128,128]{2,1,0:T(8,128)(2,1)}, bf16[24,128,128]{2,1,0:T(8,128)(2,1)S(1)}, u32[]{:S(2)}, u32[]{:S(2)}) collective-permute-start(bf16[24,128,128]{2,1,0:T(8,128)(2,1)} %get-tuple-element.128), channel_id=1, source_target_pairs={{0,6},{2,4},{4,2},{6,0},{8,14},{10,12},{12,10},{14,8},{16,22},{18,... | collective-permute-start | bytes 2359304 | tf_op jit(solution)/shard_map/return/ppermute | solution.py:67
  91.9 18.8 %collective-permute-start.21 = (bf16[24,128,128]{2,1,0:T(8,128)(2,1)}, bf16[24,128,128]{2,1,0:T(8,128)(2,1)S(1)}, u32[]{:S(2)}, u32[]{:S(2)}) collective-permute-start(bf16[24,128,128]{2,1,0:T(8,128)(2,1)} %get-tuple-element.129), channel_id=1, source_target_pairs={{0,8},{2,10},{4,12},{6,14},{8,0},{10,2},{12,4},{14,6},{16,24},{18,... | collective-permute-start | bytes 2359304 | tf_op jit(solution)/shard_map/return/ppermute | solution.py:67
  92.7 18.3 %collective-permute-start.22 = (bf16[24,128,128]{2,1,0:T(8,128)(2,1)S(1)}, bf16[24,128,128]{2,1,0:T(8,128)(2,1)S(1)}, u32[]{:S(2)}, u32[]{:S(2)}) collective-permute-start(bf16[24,128,128]{2,1,0:T(8,128)(2,1)S(1)} %copy-done.17), channel_id=1, source_target_pairs={{0,2},{2,0},{4,6},{6,4},{8,10},{10,8},{12,14},{14,12},{16,18},{18,... | collective-permute-start | bytes 2359304 | tf_op jit(solution)/shard_map/return/ppermute | solution.py:67
  112.6 11.5 %collective-permute-start.23 = (bf16[12,128,128]{2,1,0:T(8,128)(2,1)S(1)}, bf16[12,128,128]{2,1,0:T(8,128)(2,1)S(1)}, u32[]{:S(2)}, u32[]{:S(2)}) collective-permute-start(bf16[12,128,128]{2,1,0:T(8,128)(2,1)S(1)} %get-tuple-element.150), channel_id=1, source_target_pairs={{0,6},{2,4},{4,2},{6,0},{8,14},{10,12},{12,10},{14,8},{16,22},{18,... | collective-permute-start | bytes 1179656 | tf_op jit(solution)/shard_map/return/ppermute | solution.py:67
  114.2 12.4 %collective-permute-start.24 = (bf16[12,128,128]{2,1,0:T(8,128)(2,1)S(1)}, bf16[12,128,128]{2,1,0:T(8,128)(2,1)S(1)}, u32[]{:S(2)}, u32[]{:S(2)}) collective-permute-start(bf16[12,128,128]{2,1,0:T(8,128)(2,1)S(1)} %get-tuple-element.151), channel_id=1, source_target_pairs={{0,24},{2,26},{4,28},{6,30},{8,16},{10,18},{12,20},{14,22},{16,8},... | collective-permute-start | bytes 1179656 | tf_op jit(solution)/shard_map/return/ppermute | solution.py:67
  115.2 12.1 %collective-permute-start.25 = (bf16[12,128,128]{2,1,0:T(8,128)(2,1)S(1)}, bf16[12,128,128]{2,1,0:T(8,128)(2,1)S(1)}, u32[]{:S(2)}, u32[]{:S(2)}) collective-permute-start(bf16[12,128,128]{2,1,0:T(8,128)(2,1)S(1)} %get-tuple-element.152), channel_id=1, source_target_pairs={{0,2},{2,0},{4,6},{6,4},{8,10},{10,8},{12,14},{14,12},{16,18},{18,... | collective-permute-start | bytes 1179656 | tf_op jit(solution)/shard_map/return/ppermute | solution.py:67
  118.2 10.6 %collective-permute-start.26 = (bf16[12,128,128]{2,1,0:T(8,128)(2,1)S(1)}, bf16[12,128,128]{2,1,0:T(8,128)(2,1)S(1)}, u32[]{:S(2)}, u32[]{:S(2)}) collective-permute-start(bf16[12,128,128]{2,1,0:T(8,128)(2,1)S(1)} %get-tuple-element.153), channel_id=1, source_target_pairs={{0,8},{2,10},{4,12},{6,14},{8,0},{10,2},{12,4},{14,6},{16,24},{18,... | collective-permute-start | bytes 1179656 | tf_op jit(solution)/shard_map/return/ppermute | solution.py:67
  130.6 10.0 %collective-permute-start.29 = (bf16[2,3,128,128]{3,2,1,0:T(8,128)(2,1)S(1)}, bf16[2,3,128,128]{3,2,1,0:T(8,128)(2,1)}, u32[]{:S(2)}, u32[]{:S(2)}) collective-permute-start(bf16[2,3,128,128]{3,2,1,0:T(8,128)(2,1)S(1)} %get-tuple-element.173), channel_id=1, source_target_pairs={{0,2},{2,0},{4,6},{6,4},{8,10},{10,8},{12,14},{14,12},{16,18},{18,... | collective-permute-start | bytes 589832 | tf_op jit(solution)/shard_map/return/ppermute | solution.py:574
  140.5 13.2 %collective-permute-start.35 = (bf16[8,256,256]{2,1,0:T(8,128)(2,1)S(1)}, bf16[8,256,256]{2,1,0:T(8,128)(2,1)S(1)}, u32[]{:S(2)}, u32[]{:S(2)}) collective-permute-start(bf16[8,256,256]{2,1,0:T(8,128)(2,1)S(1)} %all-to-all-done.mine), channel_id=1, source_target_pairs={{0,1},{1,0},{2,3},{3,2},{4,5},{5,4},{6,7},{7,6},{8,9},{9,8},{10,11... | collective-permute-start | bytes 3145736 | tf_op jit(solution)/shard_map/grad_queries/ppermute | solution.py:63
  146.2 18.4 %all-to-all-start.1 = ((bf16[16,256,128]{2,1,0:T(8,128)(2,1)}), bf16[16,256,128]{2,1,0:T(8,128)(2,1)S(1)}, u32[]{:S(2)}, u32[]{:S(2)}) async-start(bf16[16,256,128]{2,1,0:T(8,128)(2,1)} %add_convert_fusion), calls=%async_computation.1 | async-start | bytes 2097152 | tf_op jit(solution)/shard_map/return/all_to_all | solution.py:579
  (34 other events, 291.0 us)
Sparse Core Ops, SparseCore 0:
  89.1 52.0 all-gather.2

commit v6 on v5

--- a/solution.py
+++ b/solution.py
@@ -14,7 +14,7 @@
 F32 = jnp.float32
 BF16 = jnp.bfloat16
 MIB = 2**20
-PARTS = 4
+PARTS = 8
 
 
 def chip_pairs(move):

time: 175 us -> 175 us (level)
  transfers between devices with their start and end apart: 39 -> 39, of which waited for: 25 -> 25; matrix products, arithmetic and copies ran while one was open for 3% -> 3% of each run, Pallas kernels for 23% -> 22%
where the time goes in v6:
time: 175 us; the launch traced here: 174 us
  starting transfers between devices  54.3 us (31%)
  waiting for transfers between devices  51 us (29%)
  Pallas kernels  40.8 us (23%)
  between operations  14.4 us (8%)
  other arithmetic  7.49 us (4%)
  local copies, waits for them, and re-layouts  5.99 us (3%)
    ppermute x8, waiting for transfers between devices, send(): lax.ppermute(h, 'chip', LINKS[ORDERS[s][k]])  14.6 us
    ppermute x8, starting transfers between devices, send(): lax.ppermute(h, 'chip', LINKS[ORDERS[s][k]])  10.9 us
    ppermute x6, starting transfers between devices, per_device(): lax.ppermute(pairs[pair], 'chip', square_pairs(pair, m))  10.6 us
    ppermute x8, starting transfers between devices, across(): lax.ppermute(p, 'chip', LINKS[ORDERS[s][k]])  10.3 us
    ppermute x8, waiting for transfers between devices, across(): lax.ppermute(p, 'chip', LINKS[ORDERS[s][k]])  10.2 us
    pallas_call x1, Pallas kernels, attention(): pl.pallas_call(attention_body, out_shape=[small, small, pair] + large, in...  10.1 us
    ppermute x6, starting transfers between devices, per_device(): lax.ppermute(square[3 * pair + m], 'chip', square_pairs(pair, m + 1))  8.48 us
    pallas_call x1, Pallas kernels, weight_terms(): pl.pallas_call(weight_body, out_shape=[jax.ShapeDtypeStruct((CHIPS, head_...  7.77 us
  transfers between devices with their start and end apart: 39, of which 25 were waited for; matrix products, arithmetic and copies ran while one was open for 3% of the time, Pallas kernels for 22%

profile of v6, /device:TPU:8, one launch (start us, length us, event | category | flops | bytes accessed | tf_op | source)
XLA Modules:
  0.0 174.1 jit_solution(10120954669631860629)
XLA Ops:
  13.9 3.6 %collective-permute-start.7 = (bf16[2,3,128,128]{3,2,1,0:T(8,128)(2,1)S(1)}, bf16[2,3,128,128]{3,2,1,0:T(8,128)(2,1)S(1)}, u32[]{:S(2)}, u32[]{:S(2)}) collective-permute-start(bf16[2,3,128,128]{3,2,1,0:T(8,128)(2,1)S(1)} %pad_maximum_fusion.2.refs_1_), channel_id=1, source_target_pairs={{0,30},{2,28},{4,26},{6,24},{8,22},{10,20},{12,18},{14,16},{16,14}... | collective-permute-start | bytes 589832 | tf_op jit(solution)/shard_map/gather/ppermute | solution.py:504
  19.0 2.8 %collective-permute-start.3 = (bf16[2,3,128,128]{3,2,1,0:T(8,128)(2,1)S(1)}, bf16[2,3,128,128]{3,2,1,0:T(8,128)(2,1)S(1)}, u32[]{:S(2)}, u32[]{:S(2)}) collective-permute-start(bf16[2,3,128,128]{3,2,1,0:T(8,128)(2,1)S(1)} %pad_maximum_fusion.2.refs_1_), channel_id=1, source_target_pairs={{0,24},{2,26},{4,28},{6,30},{8,16},{10,18},{12,20},{14,22},{16,8},... | collective-permute-start | bytes 589832 | tf_op jit(solution)/shard_map/gather/ppermute | solution.py:504
  23.1 3.5 %collective-permute-done.5.refs_5_ = bf16[2,3,128,128]{3,2,1,0:T(8,128)(2,1)S(1)} collective-permute-done((bf16[2,3,128,128]{3,2,1,0:T(8,128)(2,1)S(1)}, bf16[2,3,128,128]{3,2,1,0:T(8,128)(2,1)S(1)}, u32[]{:S(2)}, u32[]{:S(2)}) %collective-permute-start.5) | collective-permute-done | bytes 196640 | tf_op jit(solution)/shard_map/gather/ppermute | solution.py:504
  28.6 2.4 %collective-permute-start.9 = (bf16[12,128,128]{2,1,0:T(8,128)(2,1)S(1)}, bf16[12,128,128]{2,1,0:T(8,128)(2,1)}, u32[]{:S(2)}, u32[]{:S(2)}) collective-permute-start(bf16[12,128,128]{2,1,0:T(8,128)(2,1)S(1)} %get-tuple-element.103.refs_1_), channel_id=1, source_target_pairs={{0,24},{2,26},{4,28},{6,30},{8,16},{10,18},{12,20},{14,22},{16,8},... | collective-permute-start | bytes 1179656 | tf_op jit(solution)/shard_map/gather/ppermute | solution.py:501
  31.1 2.9 %collective-permute-start.10 = (bf16[12,128,128]{2,1,0:T(8,128)(2,1)S(1)}, bf16[12,128,128]{2,1,0:T(8,128)(2,1)}, u32[]{:S(2)}, u32[]{:S(2)}) collective-permute-start(bf16[12,128,128]{2,1,0:T(8,128)(2,1)S(1)} %get-tuple-element.104.refs_2_), channel_id=1, source_target_pairs={{0,2},{2,0},{4,6},{6,4},{8,10},{10,8},{12,14},{14,12},{16,18},{18,... | collective-permute-start | bytes 1179656 | tf_op jit(solution)/shard_map/gather/ppermute | solution.py:501
  34.8 7.5 %project.1 = (bf16[1024,128]{1,0:T(8,128)(2,1)S(1)}, bf16[1024,128]{1,0:T(8,128)(2,1)S(1)}) custom-call(s32[1]{0:T(128)} %bitcast.3.core, bf16[1024,4096]{1,0:T(8,128)(2,1)} %bitcast.39, bf16[4096,256]{1,0:T(8,128)(2,1)S(1)} %copy-done), custom_call_target="tpu_custom_call" | custom-call | tf_op jit(solution)/shard_map/queries/project/pallas_call | solution.py:239
  45.9 3.1 %join_halves.1 = (bf16[24,128,128]{2,1,0:T(8,128)(2,1)S(1)}, bf16[24,128,128]{2,1,0:T(8,128)(2,1)}, bf16[24,128,128]{2,1,0:T(8,128)(2,1)}, bf16[24,128,128]{2,1,0:T(8,128)(2,1)}) custom-call(bf16[12,128,128]{2,1,0:T(8,128)(2,1)S(1)} %get-tuple-element.102.refs_0_, bf16[12,128,128]{2,1,0:T(8,128)(2,1)S(1)} %copy-done.5, bf16[12,128,128]{2,1,0:T(8,128)(2,1)S(1)} %copy-done.7, ...), custom_call_target="tpu_custom_call" | custom-call | tf_op jit(solution)/shard_map/gather/join_halves/pallas_call | solution.py:99
  53.9 7.7 %all-to-all-start = ((bf16[8,256,256]{2,1,0:T(8,128)(2,1)}), bf16[8,256,256]{2,1,0:T(8,128)(2,1)S(1)}, u32[]{:S(2)}, u32[]{:S(2)}) async-start(bf16[8,256,256]{2,1,0:T(8,128)(2,1)} %fusion.1), calls=%async_computation | async-start | bytes 2097152 | tf_op jit(solution)/shard_map/weight_rows/all_to_all | solution.py:525
  62.1 6.7 %collective-permute-done.12.refs_1_ = bf16[24,128,128]{2,1,0:T(8,128)(2,1)} collective-permute-done((bf16[24,128,128]{2,1,0:T(8,128)(2,1)S(1)}, bf16[24,128,128]{2,1,0:T(8,128)(2,1)}, u32[]{:S(2)}, u32[]{:S(2)}) %collective-permute-start.12) | collective-permute-done | bytes 786464 | tf_op jit(solution)/shard_map/gather/ppermute | solution.py:501
  72.2 10.1 %attention.1 = (bf16[16,64,128]{2,1,0:T(8,128)(2,1)S(1)}, bf16[16,64,128]{2,1,0:T(8,128)(2,1)S(1)}, bf16[2,16,64,128]{3,2,1,0:T(8,128)(2,1)S(1)}, bf16[12,128,12...) custom-call(s32[4,64]{1,0:T(4,128)S(1)} %pad_add_fusion.slots, ...), custom_call_target="tpu_custom_call" | custom-call | tf_op jit(solution)/shard_map/attend/attention/pallas_call | solution.py:370
  85.4 3.6 %all-to-all-done.mine = bf16[8,256,256]{2,1,0:T(8,128)(2,1)S(1)} async-done(((bf16[8,256,256]{2,1,0:T(8,128)(2,1)}), bf16[8,256,256]{2,1,0:T(8,128)(2,1)S(1)}, u32[]{:S(2)}, u32[]{:S(2)}) %all-to-all-start) | async-done | bytes 1048608 | tf_op jit(solution)/shard_map/weight_rows/all_to_all | solution.py:525
  89.0 2.3 %collective-permute-start.19 = (bf16[24,128,128]{2,1,0:T(8,128)(2,1)}, bf16[24,128,128]{2,1,0:T(8,128)(2,1)S(1)}, u32[]{:S(2)}, u32[]{:S(2)}) collective-permute-start(bf16[24,128,128]{2,1,0:T(8,128)(2,1)} %get-tuple-element.127), channel_id=1, source_target_pairs={{0,24},{2,26},{4,28},{6,30},{8,16},{10,18},{12,20},{14,22},{16,8},... | collective-permute-start | bytes 2359304 | tf_op jit(solution)/shard_map/return/ppermute | solution.py:67
  94.9 7.8 %weight_terms.1 = (bf16[16,256,128]{2,1,0:T(8,128)(2,1)S(1)}, bf16[16,256,128]{2,1,0:T(8,128)(2,1)S(1)}) custom-call(s32[1]{0:T(128)} %bitcast.3.core, bf16[1024,256]{1,0:T(8,128)(2,1)S(1)} %copy-done.1, bf16[1024,4096]{1,0:T(8,128)(2,1)} %bitcast.40), custom_call_target="tpu_custom_call" | custom-call | tf_op jit(solution)/shard_map/return/weight_terms/pallas_call | solution.py:418
  103.6 5.6 %collective-permute-done.19.refs_4_ = bf16[24,128,128]{2,1,0:T(8,128)(2,1)S(1)} collective-permute-done((bf16[24,128,128]{2,1,0:T(8,128)(2,1)}, bf16[24,128,128]{2,1,0:T(8,128)(2,1)S(1)}, u32[]{:S(2)}, u32[]{:S(2)}) %collective-permute-start.19) | collective-permute-done | bytes 786464 | tf_op jit(solution)/shard_map/return/ppermute | solution.py:67
  115.2 2.9 %collective-permute-start.25 = (bf16[12,128,128]{2,1,0:T(8,128)(2,1)S(1)}, bf16[12,128,128]{2,1,0:T(8,128)(2,1)S(1)}, u32[]{:S(2)}, u32[]{:S(2)}) collective-permute-start(bf16[12,128,128]{2,1,0:T(8,128)(2,1)S(1)} %get-tuple-element.152), channel_id=1, source_target_pairs={{0,2},{2,0},{4,6},{6,4},{8,10},{10,8},{12,14},{14,12},{16,18},{18,... | collective-permute-start | bytes 1179656 | tf_op jit(solution)/shard_map/return/ppermute | solution.py:67
  121.5 2.7 %collective-permute-done.23.refs_4_ = bf16[12,128,128]{2,1,0:T(8,128)(2,1)S(1)} collective-permute-done((bf16[12,128,128]{2,1,0:T(8,128)(2,1)S(1)}, bf16[12,128,128]{2,1,0:T(8,128)(2,1)S(1)}, u32[]{:S(2)}, u32[]{:S(2)}) %collective-permute-start.23) | collective-permute-done | bytes 393248 | tf_op jit(solution)/shard_map/return/ppermute | solution.py:67
  124.1 2.5 %collective-permute-done.24.refs_5_ = bf16[12,128,128]{2,1,0:T(8,128)(2,1)S(1)} collective-permute-done((bf16[12,128,128]{2,1,0:T(8,128)(2,1)S(1)}, bf16[12,128,128]{2,1,0:T(8,128)(2,1)S(1)}, u32[]{:S(2)}, u32[]{:S(2)}) %collective-permute-start.24) | collective-permute-done | bytes 393248 | tf_op jit(solution)/shard_map/return/ppermute | solution.py:67
  130.8 2.7 %collective-permute-start.30 = (bf16[2,3,128,128]{3,2,1,0:T(8,128)(2,1)S(1)}, bf16[2,3,128,128]{3,2,1,0:T(8,128)(2,1)S(1)}, u32[]{:S(2)}, u32[]{:S(2)}) collective-permute-start(bf16[2,3,128,128]{3,2,1,0:T(8,128)(2,1)S(1)} %get-tuple-element.174), channel_id=1, source_target_pairs={{0,10},{2,8},{4,14},{6,12},{8,2},{10,0},{12,6},{14,4},{16,26},{18,... | collective-permute-start | bytes 589832 | tf_op jit(solution)/shard_map/return/ppermute | solution.py:574
  133.5 1.9 %collective-permute-start.31 = (bf16[2,3,128,128]{3,2,1,0:T(8,128)(2,1)S(1)}, bf16[2,3,128,128]{3,2,1,0:T(8,128)(2,1)S(1)}, u32[]{:S(2)}, u32[]{:S(2)}) collective-permute-start(bf16[2,3,128,128]{3,2,1,0:T(8,128)(2,1)S(1)} %get-tuple-element.175), channel_id=1, source_target_pairs={{0,24},{2,26},{4,28},{6,30},{8,16},{10,18},{12,20},{14,22},{16,8},... | collective-permute-start | bytes 589832 | tf_op jit(solution)/shard_map/return/ppermute | solution.py:574
  137.7 2.2 %collective-permute-start.33 = (bf16[2,3,128,128]{3,2,1,0:T(8,128)(2,1)S(1)}, bf16[2,3,128,128]{3,2,1,0:T(8,128)(2,1)S(1)}, u32[]{:S(2)}, u32[]{:S(2)}) collective-permute-start(bf16[2,3,128,128]{3,2,1,0:T(8,128)(2,1)S(1)} %get-tuple-element.177), channel_id=1, source_target_pairs={{0,30},{2,28},{4,26},{6,24},{8,22},{10,20},{12,18},{14,16},{16,14}... | collective-permute-start | bytes 589832 | tf_op jit(solution)/shard_map/return/ppermute | solution.py:574
  142.7 2.8 %collective-permute-done.33.refs_5_ = bf16[2,3,128,128]{3,2,1,0:T(8,128)(2,1)S(1)} collective-permute-done((bf16[2,3,128,128]{3,2,1,0:T(8,128)(2,1)S(1)}, bf16[2,3,128,128]{3,2,1,0:T(8,128)(2,1)S(1)}, u32[]{:S(2)}, u32[]{:S(2)}) %collective-permute-start.33) | collective-permute-done | bytes 196640 | tf_op jit(solution)/shard_map/return/ppermute | solution.py:574
  146.2 5.7 %all-to-all-start.1 = ((bf16[16,256,128]{2,1,0:T(8,128)(2,1)}), bf16[16,256,128]{2,1,0:T(8,128)(2,1)S(1)}, u32[]{:S(2)}, u32[]{:S(2)}) async-start(bf16[16,256,128]{2,1,0:T(8,128)(2,1)} %add_convert_fusion), calls=%async_computation.1 | async-start | bytes 2097152 | tf_op jit(solution)/shard_map/return/all_to_all | solution.py:579
  153.8 5.6 %hidden_grads.1 = bf16[1024,512]{1,0:T(8,128)(2,1)} custom-call(s32[1]{0:T(128)} %bitcast.3.core, bf16[8,1024,256]{2,1,0:T(8,128)(2,1)} %bitcast.41, bf16[8,256,256]{2,1,0:T(8,128)(2,1)S(1)} %all-to-all-done.mine, bf16[8,256,256]{2,1,0:T(8,128)(2,1)S(1)} %collective-permute-done.35.other), custom_call_target="tpu_custom_call" | custom-call | tf_op jit(solution)/shard_map/return/hidden_grads/pallas_call | solution.py:454
  159.4 5.2 %all-to-all-done.1.terms = bf16[16,256,128]{2,1,0:T(8,128)(2,1)S(1)} async-done(((bf16[16,256,128]{2,1,0:T(8,128)(2,1)}), bf16[16,256,128]{2,1,0:T(8,128)(2,1)S(1)}, u32[]{:S(2)}, u32[]{:S(2)}) %all-to-all-start.1) | async-done | bytes 1048608 | tf_op jit(solution)/shard_map/return/all_to_all | solution.py:579
  (128 shorter events, 56.0 us)
Async XLA Ops:
  11.7 10.7 %collective-permute-start.4 = (bf16[2,3,128,128]{3,2,1,0:T(8,128)(2,1)S(1)}, bf16[2,3,128,128]{3,2,1,0:T(8,128)(2,1)S(1)}, u32[]{:S(2)}, u32[]{:S(2)}) collective-permute-start(bf16[2,3,128,128]{3,2,1,0:T(8,128)(2,1)S(1)} %pad_maximum_fusion.1.refs_0_), channel_id=1, source_target_pairs={{0,2},{2,0},{4,6},{6,4},{8,10},{10,8},{12,14},{14,12},{16,18},{18,... | collective-permute-start | bytes 589832 | tf_op jit(solution)/shard_map/gather/ppermute | solution.py:504
  13.2 9.9 %collective-permute-start.2 = (bf16[2,3,128,128]{3,2,1,0:T(8,128)(2,1)S(1)}, bf16[2,3,128,128]{3,2,1,0:T(8,128)(2,1)S(1)}, u32[]{:S(2)}, u32[]{:S(2)}) collective-permute-start(bf16[2,3,128,128]{3,2,1,0:T(8,128)(2,1)S(1)} %pad_maximum_fusion.1.refs_0_), channel_id=1, source_target_pairs={{0,8},{2,10},{4,12},{6,14},{8,0},{10,2},{12,4},{14,6},{16,24},{18,... | collective-permute-start | bytes 589832 | tf_op jit(solution)/shard_map/gather/ppermute | solution.py:504
  27.5 14.8 %collective-permute-start.8 = (bf16[12,128,128]{2,1,0:T(8,128)(2,1)S(1)}, bf16[12,128,128]{2,1,0:T(8,128)(2,1)}, u32[]{:S(2)}, u32[]{:S(2)}) collective-permute-start(bf16[12,128,128]{2,1,0:T(8,128)(2,1)S(1)} %get-tuple-element.102.refs_0_), channel_id=1, source_target_pairs={{0,6},{2,4},{4,2},{6,0},{8,14},{10,12},{12,10},{14,8},{16,22},{18,... | collective-permute-start | bytes 1179656 | tf_op jit(solution)/shard_map/gather/ppermute | solution.py:501
  28.6 13.6 %collective-permute-start.9 = (bf16[12,128,128]{2,1,0:T(8,128)(2,1)S(1)}, bf16[12,128,128]{2,1,0:T(8,128)(2,1)}, u32[]{:S(2)}, u32[]{:S(2)}) collective-permute-start(bf16[12,128,128]{2,1,0:T(8,128)(2,1)S(1)} %get-tuple-element.103.refs_1_), channel_id=1, source_target_pairs={{0,24},{2,26},{4,28},{6,30},{8,16},{10,18},{12,20},{14,22},{16,8},... | collective-permute-start | bytes 1179656 | tf_op jit(solution)/shard_map/gather/ppermute | solution.py:501
  31.1 11.2 %collective-permute-start.10 = (bf16[12,128,128]{2,1,0:T(8,128)(2,1)S(1)}, bf16[12,128,128]{2,1,0:T(8,128)(2,1)}, u32[]{:S(2)}, u32[]{:S(2)}) collective-permute-start(bf16[12,128,128]{2,1,0:T(8,128)(2,1)S(1)} %get-tuple-element.104.refs_2_), channel_id=1, source_target_pairs={{0,2},{2,0},{4,6},{6,4},{8,10},{10,8},{12,14},{14,12},{16,18},{18,... | collective-permute-start | bytes 1179656 | tf_op jit(solution)/shard_map/gather/ppermute | solution.py:501
  34.0 9.9 %collective-permute-start.11 = (bf16[12,128,128]{2,1,0:T(8,128)(2,1)}, bf16[12,128,128]{2,1,0:T(8,128)(2,1)}, u32[]{:S(2)}, u32[]{:S(2)}) collective-permute-start(bf16[12,128,128]{2,1,0:T(8,128)(2,1)} %get-tuple-element.105.refs_3_), channel_id=1, source_target_pairs={{0,8},{2,10},{4,12},{6,14},{8,0},{10,2},{12,4},{14,6},{16,24},{18,... | collective-permute-start | bytes 1179656 | tf_op jit(solution)/shard_map/gather/ppermute | solution.py:501
  34.8 27.1 %collective-permute-start = (s32[48]{0:T(128)}, s32[48]{0:T(128)S(1)}, u32[]{:S(2)}, u32[]{:S(2)}) collective-permute-start(s32[48]{0:T(128)} %pad_add_fusion.1), channel_id=1, source_target_pairs={{0,1},{1,0},{2,3},{3,2},{4,5},{5,4},{6,7},{7,6},{8,9},{9,8},{10,11... | collective-permute-start | bytes 584 | tf_op jit(solution)/shard_map/slots/ppermute | solution.py:63
  49.0 19.7 %collective-permute-start.12 = (bf16[24,128,128]{2,1,0:T(8,128)(2,1)S(1)}, bf16[24,128,128]{2,1,0:T(8,128)(2,1)}, u32[]{:S(2)}, u32[]{:S(2)}) collective-permute-start(bf16[24,128,128]{2,1,0:T(8,128)(2,1)S(1)} %get-tuple-element.106.refs_0_), channel_id=1, source_target_pairs={{0,24},{2,26},{4,28},{6,30},{8,16},{10,18},{12,20},{14,22},{16,8},... | collective-permute-start | bytes 2359304 | tf_op jit(solution)/shard_map/gather/ppermute | solution.py:501
  50.6 18.1 %collective-permute-start.13 = (bf16[24,128,128]{2,1,0:T(8,128)(2,1)}, bf16[24,128,128]{2,1,0:T(8,128)(2,1)}, u32[]{:S(2)}, u32[]{:S(2)}) collective-permute-start(bf16[24,128,128]{2,1,0:T(8,128)(2,1)} %get-tuple-element.107.refs_2_), channel_id=1, source_target_pairs={{0,6},{2,4},{4,2},{6,0},{8,14},{10,12},{12,10},{14,8},{16,22},{18,... | collective-permute-start | bytes 2359304 | tf_op jit(solution)/shard_map/gather/ppermute | solution.py:501
  51.9 17.6 %collective-permute-start.14 = (bf16[24,128,128]{2,1,0:T(8,128)(2,1)}, bf16[24,128,128]{2,1,0:T(8,128)(2,1)}, u32[]{:S(2)}, u32[]{:S(2)}) collective-permute-start(bf16[24,128,128]{2,1,0:T(8,128)(2,1)} %get-tuple-element.108.refs_4_), channel_id=1, source_target_pairs={{0,8},{2,10},{4,12},{6,14},{8,0},{10,2},{12,4},{14,6},{16,24},{18,... | collective-permute-start | bytes 2359304 | tf_op jit(solution)/shard_map/gather/ppermute | solution.py:501
  52.0 18.7 %collective-permute-start.15 = (bf16[24,128,128]{2,1,0:T(8,128)(2,1)}, bf16[24,128,128]{2,1,0:T(8,128)(2,1)}, u32[]{:S(2)}, u32[]{:S(2)}) collective-permute-start(bf16[24,128,128]{2,1,0:T(8,128)(2,1)} %get-tuple-element.109.refs_6_), channel_id=1, source_target_pairs={{0,2},{2,0},{4,6},{6,4},{8,10},{10,8},{12,14},{14,12},{16,18},{18,... | collective-permute-start | bytes 2359304 | tf_op jit(solution)/shard_map/gather/ppermute | solution.py:501
  53.9 35.0 %all-to-all-start = ((bf16[8,256,256]{2,1,0:T(8,128)(2,1)}), bf16[8,256,256]{2,1,0:T(8,128)(2,1)S(1)}, u32[]{:S(2)}, u32[]{:S(2)}) async-start(bf16[8,256,256]{2,1,0:T(8,128)(2,1)} %fusion.1), calls=%async_computation | async-start | bytes 2097152 | tf_op jit(solution)/shard_map/weight_rows/all_to_all | solution.py:525
  61.6 92.2 %all-gather.3.cloned.1.call-start = ((), (), s32[]{:S(2)}) async-start(), calls=%async_computation.2 | async-start | bytes 4718592 | tf_op jit(solution)/shard_map/grad_queries/all_gather | solution.py:560
  89.0 20.3 %collective-permute-start.19 = (bf16[24,128,128]{2,1,0:T(8,128)(2,1)}, bf16[24,128,128]{2,1,0:T(8,128)(2,1)S(1)}, u32[]{:S(2)}, u32[]{:S(2)}) collective-permute-start(bf16[24,128,128]{2,1,0:T(8,128)(2,1)} %get-tuple-element.127), channel_id=1, source_target_pairs={{0,24},{2,26},{4,28},{6,30},{8,16},{10,18},{12,20},{14,22},{16,8},... | collective-permute-start | bytes 2359304 | tf_op jit(solution)/shard_map/return/ppermute | solution.py:67
  91.3 19.4 %collective-permute-start.20 = (bf16[24,128,128]{2,1,0:T(8,128)(2,1)}, bf16[24,128,128]{2,1,0:T(8,128)(2,1)S(1)}, u32[]{:S(2)}, u32[]{:S(2)}) collective-permute-start(bf16[24,128,128]{2,1,0:T(8,128)(2,1)} %get-tuple-element.128), channel_id=1, source_target_pairs={{0,6},{2,4},{4,2},{6,0},{8,14},{10,12},{12,10},{14,8},{16,22},{18,... | collective-permute-start | bytes 2359304 | tf_op jit(solution)/shard_map/return/ppermute | solution.py:67
  91.9 18.8 %collective-permute-start.21 = (bf16[24,128,128]{2,1,0:T(8,128)(2,1)}, bf16[24,128,128]{2,1,0:T(8,128)(2,1)S(1)}, u32[]{:S(2)}, u32[]{:S(2)}) collective-permute-start(bf16[24,128,128]{2,1,0:T(8,128)(2,1)} %get-tuple-element.129), channel_id=1, source_target_pairs={{0,8},{2,10},{4,12},{6,14},{8,0},{10,2},{12,4},{14,6},{16,24},{18,... | collective-permute-start | bytes 2359304 | tf_op jit(solution)/shard_map/return/ppermute | solution.py:67
  92.7 18.3 %collective-permute-start.22 = (bf16[24,128,128]{2,1,0:T(8,128)(2,1)S(1)}, bf16[24,128,128]{2,1,0:T(8,128)(2,1)S(1)}, u32[]{:S(2)}, u32[]{:S(2)}) collective-permute-start(bf16[24,128,128]{2,1,0:T(8,128)(2,1)S(1)} %copy-done.17), channel_id=1, source_target_pairs={{0,2},{2,0},{4,6},{6,4},{8,10},{10,8},{12,14},{14,12},{16,18},{18,... | collective-permute-start | bytes 2359304 | tf_op jit(solution)/shard_map/return/ppermute | solution.py:67
  112.6 11.5 %collective-permute-start.23 = (bf16[12,128,128]{2,1,0:T(8,128)(2,1)S(1)}, bf16[12,128,128]{2,1,0:T(8,128)(2,1)S(1)}, u32[]{:S(2)}, u32[]{:S(2)}) collective-permute-start(bf16[12,128,128]{2,1,0:T(8,128)(2,1)S(1)} %get-tuple-element.150), channel_id=1, source_target_pairs={{0,6},{2,4},{4,2},{6,0},{8,14},{10,12},{12,10},{14,8},{16,22},{18,... | collective-permute-start | bytes 1179656 | tf_op jit(solution)/shard_map/return/ppermute | solution.py:67
  114.2 12.4 %collective-permute-start.24 = (bf16[12,128,128]{2,1,0:T(8,128)(2,1)S(1)}, bf16[12,128,128]{2,1,0:T(8,128)(2,1)S(1)}, u32[]{:S(2)}, u32[]{:S(2)}) collective-permute-start(bf16[12,128,128]{2,1,0:T(8,128)(2,1)S(1)} %get-tuple-element.151), channel_id=1, source_target_pairs={{0,24},{2,26},{4,28},{6,30},{8,16},{10,18},{12,20},{14,22},{16,8},... | collective-permute-start | bytes 1179656 | tf_op jit(solution)/shard_map/return/ppermute | solution.py:67
  115.2 12.1 %collective-permute-start.25 = (bf16[12,128,128]{2,1,0:T(8,128)(2,1)S(1)}, bf16[12,128,128]{2,1,0:T(8,128)(2,1)S(1)}, u32[]{:S(2)}, u32[]{:S(2)}) collective-permute-start(bf16[12,128,128]{2,1,0:T(8,128)(2,1)S(1)} %get-tuple-element.152), channel_id=1, source_target_pairs={{0,2},{2,0},{4,6},{6,4},{8,10},{10,8},{12,14},{14,12},{16,18},{18,... | collective-permute-start | bytes 1179656 | tf_op jit(solution)/shard_map/return/ppermute | solution.py:67
  118.2 10.6 %collective-permute-start.26 = (bf16[12,128,128]{2,1,0:T(8,128)(2,1)S(1)}, bf16[12,128,128]{2,1,0:T(8,128)(2,1)S(1)}, u32[]{:S(2)}, u32[]{:S(2)}) collective-permute-start(bf16[12,128,128]{2,1,0:T(8,128)(2,1)S(1)} %get-tuple-element.153), channel_id=1, source_target_pairs={{0,8},{2,10},{4,12},{6,14},{8,0},{10,2},{12,4},{14,6},{16,24},{18,... | collective-permute-start | bytes 1179656 | tf_op jit(solution)/shard_map/return/ppermute | solution.py:67
  130.5 10.0 %collective-permute-start.29 = (bf16[2,3,128,128]{3,2,1,0:T(8,128)(2,1)S(1)}, bf16[2,3,128,128]{3,2,1,0:T(8,128)(2,1)}, u32[]{:S(2)}, u32[]{:S(2)}) collective-permute-start(bf16[2,3,128,128]{3,2,1,0:T(8,128)(2,1)S(1)} %get-tuple-element.173), channel_id=1, source_target_pairs={{0,2},{2,0},{4,6},{6,4},{8,10},{10,8},{12,14},{14,12},{16,18},{18,... | collective-permute-start | bytes 589832 | tf_op jit(solution)/shard_map/return/ppermute | solution.py:574
  140.5 13.2 %collective-permute-start.35 = (bf16[8,256,256]{2,1,0:T(8,128)(2,1)S(1)}, bf16[8,256,256]{2,1,0:T(8,128)(2,1)S(1)}, u32[]{:S(2)}, u32[]{:S(2)}) collective-permute-start(bf16[8,256,256]{2,1,0:T(8,128)(2,1)S(1)} %all-to-all-done.mine), channel_id=1, source_target_pairs={{0,1},{1,0},{2,3},{3,2},{4,5},{5,4},{6,7},{7,6},{8,9},{9,8},{10,11... | collective-permute-start | bytes 3145736 | tf_op jit(solution)/shard_map/grad_queries/ppermute | solution.py:63
  146.2 18.4 %all-to-all-start.1 = ((bf16[16,256,128]{2,1,0:T(8,128)(2,1)}), bf16[16,256,128]{2,1,0:T(8,128)(2,1)S(1)}, u32[]{:S(2)}, u32[]{:S(2)}) async-start(bf16[16,256,128]{2,1,0:T(8,128)(2,1)} %add_convert_fusion), calls=%async_computation.1 | async-start | bytes 2097152 | tf_op jit(solution)/shard_map/return/all_to_all | solution.py:579
  (34 other events, 291.5 us)
Sparse Core Ops, SparseCore 0:
  89.1 51.4 all-gather.2
